TPU v7x, 256 devices: a whole 4x4x8 slice. The times are simulated.
256 devices in a mesh: rep: 16 (over z, core), row: 4 (over y), col: 4 (over x).
Axes of the slice: x: 4, y: 4, z: 8, core: 2. Of those that a mesh axis runs over, the one named last changes fastest.
Arguments:
- hidden_in: bfloat16 [16384, 2048], P(('rep', 'row', 'col')), may hold values from -6 to 6
- w_qkv: bfloat16 [2048, 16, 384], P(None, ('row', 'col')), may hold values from -0.125 to 0.125
- w_out: bfloat16 [16, 128, 2048], P(('row', 'col')), may hold values from -0.5 to 0.5
- w_gate_up: bfloat16 [2048, 2, 8192], P(None, None, ('row', 'col')), may hold values from -0.125 to 0.125
- w_down: bfloat16 [8192, 2048], P(('row', 'col')), may hold values from -0.0625 to 0.0625
- cache: bfloat16 [128, 2, 256, 16, 128], P('rep', None, None, ('row', 'col'))
- span_len: int32 [128], replicated, may hold values from 1 to 128, 8192 in all
- cache_len: int32 [128], replicated, may hold values from 1 to 256, 16384 in all
- new_slot: int32 [128], replicated, may hold values from 0 to 127, as said below
Outputs:
- hidden_out: bfloat16 [16384, 2048], P(('rep', 'row', 'col'))
- cache_out: bfloat16 [128, 2, 384, 16, 128], P('rep', None, None, ('row', 'col'))
Inputs may be any that keep to these rules, and one draw needn't show every extreme that they name: A permutation of the 128 slots; slot s lies on replica s // 8, and new_slot[r] mod 8 equals r mod 8; the 8 requests of one replica go to at most 1 slots of any one replica, and some pair of replicas has exactly 1.
All inputs are finite; a program needn't handle non-finite values.
Results may differ from a plain program's by a relative error of at most 0.014.
The roundings to bfloat16 on the way count: a program that leaves them out, or rounds other values in their place, can miss the bound.
Values may be sent and summed in bfloat16 or wider, within the bound.
No kernel may reach another device: no remote copies, remote signals or barrier semaphores. Data moves between devices by JAX's collectives and lax.ppermute only.
A program may use at most 128 MiB of HBM per device.

v0:
```python
import math

import jax
import jax.numpy as jnp
from jax import lax
from jax.experimental import pallas as pl
from jax.experimental.pallas import tpu as pltpu
from jax.sharding import PartitionSpec as P

EPSILON = 1e-05


def layer_norm(values):
    centred = values - jnp.mean(values, axis=-1, keepdims=True)
    spread = jnp.mean(centred * centred, axis=-1, keepdims=True)
    return centred * lax.rsqrt(spread + EPSILON)


def swap(axis, k, array):
    size = lax.axis_size(axis)
    return lax.ppermute(array, axis, [(i, i ^ k) for i in range(size)])


def together(sent):
    got = [swap(axis, k, array) for axis, k, array in sent]
    return lax.optimization_barrier(got)


def gather_plane(rows, extra):
    half = rows.shape[0] // 2
    one, two = rows[:half], rows[half:]
    with_extra = jnp.concatenate([two, extra], axis=0)
    got = together([x for k in (1, 3, 2) for x in (("col", k, one), ("row", k, with_extra))])
    extra = jnp.stack([extra, got[1][half:], got[5][half:], got[3][half:]], axis=0)
    one = jnp.concatenate([one, got[0], got[4], got[2]], axis=0)
    two = jnp.concatenate([two, got[1][:half], got[5][:half], got[3][:half]], axis=0)
    got = together([x for k in (1, 3, 2) for x in (("row", k, one), ("col", k, two))])
    one = jnp.concatenate([one, got[0], got[4], got[2]], axis=0)
    two = jnp.concatenate([two, got[1], got[5], got[3]], axis=0)
    return one, two, extra


def gather_block(rows):
    half = rows.shape[0] // 2
    one, two = rows[:half], rows[half:]
    got = together([("col", 1, one), ("row", 1, two), ("col", 3, one), ("col", 2, one)])
    one = jnp.concatenate([one, got[0], got[3], got[2]], axis=0)
    two = jnp.concatenate([two, got[1]], axis=0)
    got = together([("row", 1, one), ("col", 1, two), ("col", 3, two), ("col", 2, two)])
    return jnp.concatenate([one, got[0], two, got[1], got[3], got[2]], axis=0)


def wide_sum(arrays):
    total = arrays[0].astype(jnp.float32)
    for array in arrays[1:]:
        total = total + array.astype(jnp.float32)
    return total


def scatter_block(sums, half):
    one = [sums[4 * half * n : 4 * half * (n + 1)] for n in range(2)]
    two = [sums[8 * half + 2 * half * n : 8 * half + 2 * half * (n + 1)] for n in range(4)]
    got = together([("row", 1, one[1]), ("col", 1, two[1]), ("col", 3, two[3]), ("col", 2, two[2])])
    one = wide_sum([one[0], got[0]]).astype(jnp.bfloat16)
    two = wide_sum([two[0], got[1], got[3], got[2]]).astype(jnp.bfloat16)
    one = [one[half * n : half * (n + 1)] for n in range(4)]
    two = [two[half * n : half * (n + 1)] for n in range(2)]
    got = together([("col", 1, one[1]), ("row", 1, two[1]), ("col", 3, one[3]), ("col", 2, one[2])])
    return jnp.concatenate(
        [wide_sum([one[0], got[0], got[3], got[2]]), wide_sum([two[0], got[1]])], axis=0
    )


def attend_kernel(
    meta_ref, one_ref, two_ref, cache_ref, cos_ref, sin_ref, context_ref, new_ref
):
    g = pl.program_id(0)

    def entry(n):
        return meta_ref[16 * g + n]

    length_old = entry(2)

    def block(ref, n):
        return ref[pl.ds(pl.multiple_of(32 * entry(n), 32), 32), :]

    joined = jnp.concatenate(
        [block(one_ref, 3), block(two_ref, 5), block(one_ref, 4), block(two_ref, 6)], axis=0
    )
    cosine, sine = cos_ref[0], sin_ref[0]

    def turned(part):
        return (part * cosine + pltpu.roll(part, 64, axis=1) * sine).astype(jnp.bfloat16)

    queries = turned(joined[:, :128])
    keys_new = turned(joined[:, 128:256])
    values_new = joined[:, 256:].astype(jnp.bfloat16)
    stored = cache_ref.shape[2]
    whole = new_ref.shape[2]
    live = lax.broadcasted_iota(jnp.int32, keys_new.shape, 0) < entry(9)
    rows = lax.broadcasted_iota(jnp.int32, (whole, keys_new.shape[1]), 0)
    for kind, fresh in enumerate((keys_new, values_new)):
        fresh = jnp.where(live, fresh.astype(jnp.float32), 0.0)
        fresh = jnp.concatenate(
            [fresh, jnp.zeros((whole - fresh.shape[0], fresh.shape[1]), jnp.float32)], axis=0
        )
        old = cache_ref[0, kind].astype(jnp.float32)
        old = jnp.concatenate(
            [old, jnp.zeros((whole - stored, old.shape[1]), jnp.float32)], axis=0
        )
        fresh = pltpu.roll(fresh, length_old, axis=0)
        new_ref[0, kind] = jnp.where(rows < length_old, old, fresh).astype(jnp.bfloat16)
    scale = 1.0 / math.sqrt(128)
    contract = (((1,), (1,)), ((), ()))
    old = (
        lax.dot_general(queries, cache_ref[0, 0], contract, preferred_element_type=jnp.float32)
        * scale
    )
    new = (
        lax.dot_general(queries, keys_new, contract, preferred_element_type=jnp.float32) * scale
    )
    old_ok = lax.broadcasted_iota(jnp.int32, old.shape, 1) < length_old
    new_ok = lax.broadcasted_iota(jnp.int32, new.shape, 1) <= lax.broadcasted_iota(
        jnp.int32, new.shape, 0
    )
    old = jnp.where(old_ok, old, -1e30)
    new = jnp.where(new_ok, new, -1e30)
    highest = jnp.maximum(
        jnp.max(old, axis=1, keepdims=True), jnp.max(new, axis=1, keepdims=True)
    )
    old = jnp.where(old_ok, jnp.exp(old - highest), 0.0)
    new = jnp.where(new_ok, jnp.exp(new - highest), 0.0)
    total = jnp.sum(old, axis=1, keepdims=True) + jnp.sum(new, axis=1, keepdims=True)
    old_weights = (old / total).astype(jnp.bfloat16)
    new_weights = (new / total).astype(jnp.bfloat16)
    stored_values = cache_ref[0, 1]
    context = jnp.dot(
        old_weights, stored_values, preferred_element_type=jnp.float32
    ) + jnp.dot(new_weights, values_new, preferred_element_type=jnp.float32)
    context = context.astype(jnp.bfloat16)
    for n in range(2):
        place = pl.multiple_of(64 * entry(7 + n), 64)
        context_ref[pl.ds(place, 64), :] = context[64 * n : 64 * n + 64]


def attend(meta, one, two, cache, cosine, sine, replicas):
    slots, kinds, stored, size = cache.shape
    span = cosine.shape[1]
    whole = lambda g, m: (0, 0)
    mine = lambda g, m: (m[16 * g], 0, 0)
    return pl.pallas_call(
        attend_kernel,
        out_shape=(
            jax.ShapeDtypeStruct((slots * span, size), jnp.bfloat16),
            jax.ShapeDtypeStruct((replicas, kinds, stored + span, size), jnp.bfloat16),
        ),
        grid_spec=pltpu.PrefetchScalarGridSpec(
            num_scalar_prefetch=1,
            grid=(slots,),
            in_specs=[
                pl.BlockSpec(one.shape, whole),
                pl.BlockSpec(two.shape, whole),
                pl.BlockSpec((1, kinds, stored, size), lambda g, m: (m[16 * g], 0, 0, 0)),
                pl.BlockSpec((1, span, size), mine),
                pl.BlockSpec((1, span, size), mine),
            ],
            out_specs=[
                pl.BlockSpec((slots * span, size), whole),
                pl.BlockSpec(
                    (1, kinds, stored + span, size), lambda g, m: (m[16 * g + 1], 0, 0, 0)
                ),
            ],
        ),
        cost_estimate=pl.CostEstimate(
            flops=4 * slots * span * (stored + span) * size,
            transcendentals=slots * span * (stored + span),
            bytes_accessed=6 << 20,
        ),
        name="attend",
    )(meta, one, two, cache, cosine, sine)


def pick_kernel(source_ref, moved_ref, out_ref, sems):
    copies = [
        pltpu.make_async_copy(moved_ref.at[source_ref[t]], out_ref.at[t], sems.at[t])
        for t in range(out_ref.shape[0])
    ]
    for copy in copies:
        copy.start()
    for copy in copies:
        copy.wait()


def pick(moved, source):
    shape = (source.shape[0],) + moved.shape[1:]
    return pl.pallas_call(
        pick_kernel,
        out_shape=jax.ShapeDtypeStruct(shape, moved.dtype),
        in_specs=[pl.BlockSpec(memory_space=pltpu.SMEM), pl.BlockSpec(memory_space=pl.ANY)],
        out_specs=pl.BlockSpec(memory_space=pl.ANY),
        scratch_shapes=[pltpu.SemaphoreType.DMA((shape[0],))],
        cost_estimate=pl.CostEstimate(
            flops=0, transcendentals=0, bytes_accessed=4 * math.prod(shape)
        ),
        name="pick",
    )(source, moved)


def attend_table(targets, lengths, spans, row, column):
    step = jnp.arange(8, dtype=jnp.int32)
    request = 2 * (row ^ (step // 2)) + step % 2
    away = row ^ (request // 2)
    fields = [request, targets[request], lengths[request]]
    columns = [column ^ (2 * (request % 2)), column ^ (2 * (request % 2) + 1)]
    fields += [4 * away + c for c in columns]
    fields += [4 * c + away for c in columns]
    fields += [4 * (step // 2) + c for c in columns]
    fields += [spans[request]]
    fields += [jnp.zeros_like(step)] * (16 - len(fields))
    return jnp.stack(fields, axis=1).reshape(-1)


def body(hidden_in, w_qkv, w_out, w_gate_up, w_down, cache, span_len, cache_len, new_slot):
    slots, kinds, stored, _, size = cache.shape
    local_rows, width = hidden_in.shape
    units = w_down.shape[0]
    span = 16 * local_rows // slots
    replica = lax.axis_index("rep")
    replicas = lax.axis_size("rep")
    row, column = lax.axis_index("row"), lax.axis_index("col")
    cache = cache.reshape(slots, kinds, stored, size)
    lengths = lax.dynamic_slice_in_dim(cache_len, replica * slots, slots)
    spans = lax.dynamic_slice_in_dim(span_len, replica * slots, slots)
    targets = lax.dynamic_slice_in_dim(new_slot, replica * slots, slots) // slots
    my_slots = replica * slots + jnp.arange(slots, dtype=jnp.int32)
    arrivals = (new_slot[None, :] == my_slots[:, None]).astype(jnp.int32)
    requests = jnp.arange(new_slot.shape[0], dtype=jnp.int32)
    source = jnp.sum(arrivals * (requests // slots)[None, :], axis=1)

    share = size // replicas
    out_slice = lax.dynamic_slice_in_dim(w_out.reshape(size, width), replica * share, share)
    rows_in, rows_down = width // replicas, units // replicas
    in_slice = lax.dynamic_slice_in_dim(w_gate_up, replica * rows_in, rows_in)
    down_slice = lax.dynamic_slice_in_dim(w_down, replica * rows_down, rows_down)
    feed_slice = jnp.concatenate(
        [in_slice.reshape(rows_in, 2 * units), down_slice[:, : 2 * units], down_slice[:, 2 * units :]],
        axis=0,
    )

    inputs = hidden_in.astype(jnp.float32)
    normed = layer_norm(inputs).astype(jnp.bfloat16)
    one, two, out_slices = gather_plane(normed, out_slice)
    w_rows = lax.all_gather(out_slices, "rep", axis=1, tiled=True).reshape(4 * size, width)
    w_in = w_gate_up.reshape(width, 2 * units)
    one, two, w_in, feed_slice = lax.optimization_barrier((one, two, w_in, feed_slice))
    feed_far = swap("row", 2, feed_slice)
    heads = w_qkv.reshape(width, 3 * size)
    joined_one = jnp.dot(one, heads, preferred_element_type=jnp.float32)
    joined_two = jnp.dot(two, heads, preferred_element_type=jnp.float32)

    offsets = jnp.arange(span, dtype=jnp.int32)
    positions = (lengths[:, None] + offsets[None, :]).astype(jnp.float32)
    frequency = 10000.0 ** (-(jnp.arange(size // 2, dtype=jnp.float32) * 2.0 / size))
    angles = positions[:, :, None] * frequency
    cosine, sine = jnp.cos(angles), jnp.sin(angles)
    cosine = jnp.concatenate([cosine, cosine], axis=-1)
    sine = jnp.concatenate([-sine, sine], axis=-1)
    meta = attend_table(targets, lengths, spans, row, column)
    context, sent = attend(meta, joined_one, joined_two, cache, cosine, sine, replicas)
    context, feed_far = lax.optimization_barrier((context, feed_far))
    fed = lax.all_gather(feed_far, "rep", axis=0, tiled=False)
    w_in_far = fed[:, :rows_in].reshape(width, 2 * units)
    w_down_far = jnp.concatenate(
        [fed[:, rows_in : rows_in + rows_down], fed[:, rows_in + rows_down :]], axis=2
    ).reshape(units, width)

    context = context.reshape(4, 4 * local_rows, size)
    got = together([("row", k, context[k]) for k in (1, 3, 2)])
    parts = jnp.concatenate([context[0], got[0], got[2], got[1]], axis=1)
    partial = jnp.dot(parts, w_rows, preferred_element_type=jnp.float32).astype(jnp.bfloat16)
    partial = partial.reshape(4, local_rows, width)
    got = together([("col", k, partial[k]) for k in (1, 3, 2)])
    middle = (inputs + wide_sum([partial[0], got[0], got[2], got[1]])).astype(jnp.bfloat16)
    normed_mid = layer_norm(middle.astype(jnp.float32)).astype(jnp.bfloat16)

    moved = lax.all_to_all(sent, "rep", split_axis=0, concat_axis=0, tiled=True)

    tokens = gather_block(normed_mid)
    down_sum = jnp.zeros((tokens.shape[0], width), jnp.float32)
    for w_in, w_back in ((w_in, w_down), (w_in_far, w_down_far)):
        gate_up = jnp.dot(tokens, w_in, preferred_element_type=jnp.float32)
        hidden = (jax.nn.silu(gate_up[:, :units]) * gate_up[:, units:]).astype(jnp.bfloat16)
        down_sum = down_sum + jnp.dot(hidden, w_back, preferred_element_type=jnp.float32)
    down_sum = scatter_block(down_sum.astype(jnp.bfloat16), local_rows // 2)

    cache_out = pick(moved, source)
    first_row = (row * 4 + column) * local_rows
    within = first_row % span + jnp.arange(local_rows, dtype=jnp.int32)
    live = within < lax.dynamic_index_in_dim(spans, first_row // span, keepdims=False)
    hidden_out = jnp.where(live[:, None], middle.astype(jnp.float32) + down_sum, 0.0)
    return (
        hidden_out.astype(jnp.bfloat16),
        cache_out.reshape(slots, kinds, stored + span, 1, size),
    )


def solution(mesh):
    in_specs = (
        P(("rep", "row", "col"), None),
        P(None, ("row", "col"), None),
        P(("row", "col"), None, None),
        P(None, None, ("row", "col")),
        P(("row", "col"), None),
        P("rep", None, None, ("row", "col"), None),
        P(),
        P(),
        P(),
    )
    out_specs = (P(("rep", "row", "col"), None), P("rep", None, None, ("row", "col"), None))
    return jax.shard_map(body, mesh=mesh, in_specs=in_specs, out_specs=out_specs, check_vma=False)
```

profile of v0, /device:TPU:1, one launch (start us, length us, event | category | flops | bytes accessed | tf_op | source)
XLA Modules:
  0.0 274.7 jit_solution(15389726489820242190)
XLA Ops:
  11.5 3.6 %collective-permute-start.4 = (bf16[32,2048]{1,0:T(8,128)(2,1)}, bf16[32,2048]{1,0:T(8,128)(2,1)S(1)}, u32[]{:S(2)}, u32[]{:S(2)}) collective-permute-start(bf16[32,2048]{1,0:T(8,128)(2,1)} %get-tuple-element.117), channel_id=1, source_target_pairs={{0,2},{1,3},{2,0},{3,1},{4,6},{5,7},{6,4},{7,5},{8,10},{9,11},{10,... | collective-permute-start | bytes 393224 | tf_op jit(solution)/shard_map/ppermute | solution.py:21
  17.4 2.9 %collective-permute-start.5 = (bf16[40,2048]{1,0:T(8,128)(2,1)}, bf16[40,2048]{1,0:T(8,128)(2,1)}, u32[]{:S(2)}, u32[]{:S(2)}) collective-permute-start(bf16[40,2048]{1,0:T(8,128)(2,1)} %pad_maximum_fusion.8), channel_id=1, source_target_pairs={{0,8},{4,12},{8,0},{12,4},{1,9},{5,13},{9,1},{13,5},{2,10},{6,14},... | collective-permute-start | bytes 491528 | tf_op jit(solution)/shard_map/ppermute | solution.py:21
  29.6 2.4 collective-permute-done.1
  41.6 3.0 %collective-permute-start.11 = (bf16[128,2048]{1,0:T(8,128)(2,1)}, bf16[128,2048]{1,0:T(8,128)(2,1)}, u32[]{:S(2)}, u32[]{:S(2)}) collective-permute-start(bf16[128,2048]{1,0:T(8,128)(2,1)} %pad_maximum_fusion.2), channel_id=1, source_target_pairs={{0,2},{1,3},{2,0},{3,1},{4,6},{5,7},{6,4},{7,5},{8,10},{9,11},{10,... | collective-permute-start | bytes 1572872 | tf_op jit(solution)/shard_map/ppermute | solution.py:21
  50.1 5.5 %copy.23 = bf16[256,8,2,512]{3,1,2,0:T(8,128)(2,1)} copy(bf16[256,8,2,512]{3,2,1,0:T(2,128)(2,1)} %bitcast.40) | data formatting | bytes 8388608
  63.5 4.9 %collective-permute-done.9 = bf16[128,2048]{1,0:T(8,128)(2,1)S(1)} collective-permute-done((bf16[128,2048]{1,0:T(8,128)(2,1)}, bf16[128,2048]{1,0:T(8,128)(2,1)S(1)}, u32[]{:S(2)}, u32[]{:S(2)}) %collective-permute-start.9) | collective-permute-done | bytes 524320 | tf_op jit(solution)/shard_map/ppermute | solution.py:21
  70.1 15.4 %collective-permute-done.8 = bf16[128,2048]{1,0:T(8,128)(2,1)S(1)} collective-permute-done((bf16[128,2048]{1,0:T(8,128)(2,1)S(1)}, bf16[128,2048]{1,0:T(8,128)(2,1)S(1)}, u32[]{:S(2)}, u32[]{:S(2)}) %collective-permute-start.8) | collective-permute-done | bytes 524320 | tf_op jit(solution)/shard_map/ppermute | solution.py:21
  92.8 9.4 %attend.1 = (bf16[1024,128]{1,0:T(8,128)(2,1)}, bf16[16,2,384,128]{3,2,1,0:T(8,128)(2,1)}) custom-call(s32[128]{0:T(128)} %reshape.307.meta_ref, f32[512,384]{1,0:T(8,128)} %fusion.2.one_ref, f32[512,384]{1,0:T(8,128)} %fusion.two_ref, bf16[8,2,256,128]{3,2,1,0:T(8,128)(2,1)} %bitcast.47, f32[8,128,128]{2,1,0:T(8,128)} %get-tuple-element.139.cos_ref, ...), custom_call_target="tpu_custom_call" | custom-call | flops 201326592 | bytes 6291456 | tf_op jit(solution)/shard_map/attend/pallas_call | solution.py:151
  110.7 2.3 convolution_convert_fusion
  113.2 3.1 %collective-permute-start.18 = (bf16[64,2048]{1,0:T(8,128)(2,1)S(1)}, bf16[64,2048]{1,0:T(8,128)(2,1)S(1)}, u32[]{:S(2)}, u32[]{:S(2)}) collective-permute-start(bf16[64,2048]{1,0:T(8,128)(2,1)S(1)} %get-tuple-element.101), channel_id=1, source_target_pairs={{0,2},{1,3},{2,0},{3,1},{4,6},{5,7},{6,4},{7,5},{8,10},{9,11},{10,... | collective-permute-start | bytes 786440 | tf_op jit(solution)/shard_map/ppermute | solution.py:21
  117.1 2.9 %collective-permute-done.18 = bf16[64,2048]{1,0:T(8,128)(2,1)S(1)} collective-permute-done((bf16[64,2048]{1,0:T(8,128)(2,1)S(1)}, bf16[64,2048]{1,0:T(8,128)(2,1)S(1)}, u32[]{:S(2)}, u32[]{:S(2)}) %collective-permute-start.18) | collective-permute-done | bytes 262176 | tf_op jit(solution)/shard_map/ppermute | solution.py:21
  120.0 7.7 %collective-permute-done.17 = bf16[64,2048]{1,0:T(8,128)(2,1)S(1)} collective-permute-done((bf16[64,2048]{1,0:T(8,128)(2,1)S(1)}, bf16[64,2048]{1,0:T(8,128)(2,1)S(1)}, u32[]{:S(2)}, u32[]{:S(2)}) %collective-permute-start.17) | collective-permute-done | bytes 262176 | tf_op jit(solution)/shard_map/ppermute | solution.py:21
  130.6 2.5 collective-permute-start.21
  133.1 11.1 %all-to-all-start = ((bf16[16,2,384,128]{3,2,1,0:T(8,128)(2,1)}), bf16[16,2,384,128]{3,2,1,0:T(8,128)(2,1)}, u32[]{:S(2)}, u32[]{:S(2)}) async-start(bf16[16,2,384,128]{3,2,1,0:T(8,128)(2,1)} %get-tuple-element.85), calls=%async_computation | async-start | bytes 6291456 | tf_op jit(solution)/shard_map/all_to_all | solution.py:286
  144.2 2.3 collective-permute-start.26
  153.7 6.1 %collective-permute-done.25 = bf16[64,2048]{1,0:T(8,128)(2,1)S(1)} collective-permute-done((bf16[64,2048]{1,0:T(8,128)(2,1)S(1)}, bf16[64,2048]{1,0:T(8,128)(2,1)S(1)}, u32[]{:S(2)}, u32[]{:S(2)}) %collective-permute-start.25) | collective-permute-done | bytes 262176 | tf_op jit(solution)/shard_map/ppermute | solution.py:21
  166.0 4.1 %fusion.58 = f32[512,1024]{1,0:T(8,128)S(1)} fusion(bf16[512,2048]{1,0:T(8,128)(2,1)} %constant_dynamic-update-slice_fusion.14, bf16[2048,1024]{1,0:T(8,128)(2,1)S(1)} %bitcast.41), kind=kOutput, calls=%fused_computation.148 | convolution fusion | flops 2147483648 | bytes 8388608 | tf_op jit(solution)/shard_map/dot_general | solution.py:291
  170.2 3.4 %fusion.17 = f32[512,2048]{1,0:T(8,128)} fusion(bf16[512,2048]{1,0:T(8,128)(2,1)S(1)} %copy-done.11, f32[512,1024]{1,0:T(8,128)S(1)} %fusion.58), kind=kOutput, calls=%fused_computation.34 | convolution fusion | flops 1075314688 | bytes 8388608 | tf_op jit(solution)/shard_map/dot_general | solution.py:293
  173.6 2.6 slice.180
  179.6 2.4 fusion.59
  188.9 3.5 %collective-permute-done.30 = bf16[64,2048]{1,0:T(8,128)(2,1)S(1)} collective-permute-done((bf16[64,2048]{1,0:T(8,128)(2,1)S(1)}, bf16[64,2048]{1,0:T(8,128)(2,1)S(1)}, u32[]{:S(2)}, u32[]{:S(2)}) %collective-permute-start.30) | collective-permute-done | bytes 262176 | tf_op jit(solution)/shard_map/ppermute | solution.py:21
  192.4 7.5 %collective-permute-done.29 = bf16[64,2048]{1,0:T(8,128)(2,1)S(1)} collective-permute-done((bf16[64,2048]{1,0:T(8,128)(2,1)S(1)}, bf16[64,2048]{1,0:T(8,128)(2,1)S(1)}, u32[]{:S(2)}, u32[]{:S(2)}) %collective-permute-start.29) | collective-permute-done | bytes 262176 | tf_op jit(solution)/shard_map/ppermute | solution.py:21
  208.4 8.9 %all-to-all-done.moved_ref = bf16[16,2,384,128]{3,2,1,0:T(8,128)(2,1)} async-done(((bf16[16,2,384,128]{3,2,1,0:T(8,128)(2,1)}), bf16[16,2,384,128]{3,2,1,0:T(8,128)(2,1)}, u32[]{:S(2)}, u32[]{:S(2)}) %all-to-all-start) | async-done | bytes 3145760 | tf_op jit(solution)/shard_map/all_to_all | solution.py:286
  217.3 49.6 %pick.1 = bf16[8,2,384,128]{3,2,1,0:T(8,128)(2,1)} custom-call(s32[8]{0:T(128)} %select_reduce_fusion.source_ref, bf16[16,2,384,128]{3,2,1,0:T(8,128)(2,1)} %all-to-all-done.moved_ref), custom_call_target="tpu_custom_call" | custom-call | bytes 3145728 | tf_op jit(solution)/shard_map/pick/pallas_call | solution.py:196
  (187 shorter events, 93.1 us)
Async XLA Ops:
  7.2 103.6 %all-gather.4.cloned.1.call-start = ((), (), s32[]{:S(2)}) async-start(), calls=%async_computation.1 | async-start | bytes 2228224 | tf_op jit(solution)/shard_map/all_gather | solution.py:253
  11.5 15.9 %collective-permute-start.4 = (bf16[32,2048]{1,0:T(8,128)(2,1)}, bf16[32,2048]{1,0:T(8,128)(2,1)S(1)}, u32[]{:S(2)}, u32[]{:S(2)}) collective-permute-start(bf16[32,2048]{1,0:T(8,128)(2,1)} %get-tuple-element.117), channel_id=1, source_target_pairs={{0,2},{1,3},{2,0},{3,1},{4,6},{5,7},{6,4},{7,5},{8,10},{9,11},{10,... | collective-permute-start | bytes 393224 | tf_op jit(solution)/shard_map/ppermute | solution.py:21
  15.1 14.2 %collective-permute-start.2 = (bf16[32,2048]{1,0:T(8,128)(2,1)}, bf16[32,2048]{1,0:T(8,128)(2,1)}, u32[]{:S(2)}, u32[]{:S(2)}) collective-permute-start(bf16[32,2048]{1,0:T(8,128)(2,1)} %get-tuple-element.117), channel_id=1, source_target_pairs={{0,3},{1,2},{2,1},{3,0},{4,7},{5,6},{6,5},{7,4},{8,11},{9,10},{10,... | collective-permute-start | bytes 393224 | tf_op jit(solution)/shard_map/ppermute | solution.py:21
  16.0 13.3 %collective-permute-start = (bf16[32,2048]{1,0:T(8,128)(2,1)}, bf16[32,2048]{1,0:T(8,128)(2,1)}, u32[]{:S(2)}, u32[]{:S(2)}) collective-permute-start(bf16[32,2048]{1,0:T(8,128)(2,1)} %get-tuple-element.117), channel_id=1, source_target_pairs={{0,1},{1,0},{2,3},{3,2},{4,5},{5,4},{6,7},{7,6},{8,9},{9,8},{10,11... | collective-permute-start | bytes 393224 | tf_op jit(solution)/shard_map/ppermute | solution.py:21
  17.4 11.9 %collective-permute-start.5 = (bf16[40,2048]{1,0:T(8,128)(2,1)}, bf16[40,2048]{1,0:T(8,128)(2,1)}, u32[]{:S(2)}, u32[]{:S(2)}) collective-permute-start(bf16[40,2048]{1,0:T(8,128)(2,1)} %pad_maximum_fusion.8), channel_id=1, source_target_pairs={{0,8},{4,12},{8,0},{12,4},{1,9},{5,13},{9,1},{13,5},{2,10},{6,14},... | collective-permute-start | bytes 491528 | tf_op jit(solution)/shard_map/ppermute | solution.py:21
  36.6 136.9 %all-gather.6.cloned.1.call-start = ((), (), s32[]{:S(2)}) async-start(), calls=%async_computation.2 | async-start | bytes 6684672 | tf_op jit(solution)/shard_map/all_gather | solution.py:271
  41.6 19.8 %collective-permute-start.11 = (bf16[128,2048]{1,0:T(8,128)(2,1)}, bf16[128,2048]{1,0:T(8,128)(2,1)}, u32[]{:S(2)}, u32[]{:S(2)}) collective-permute-start(bf16[128,2048]{1,0:T(8,128)(2,1)} %pad_maximum_fusion.2), channel_id=1, source_target_pairs={{0,2},{1,3},{2,0},{3,1},{4,6},{5,7},{6,4},{7,5},{8,10},{9,11},{10,... | collective-permute-start | bytes 1572872 | tf_op jit(solution)/shard_map/ppermute | solution.py:21
  60.6 25.0 %collective-permute-start.8 = (bf16[128,2048]{1,0:T(8,128)(2,1)S(1)}, bf16[128,2048]{1,0:T(8,128)(2,1)S(1)}, u32[]{:S(2)}, u32[]{:S(2)}) collective-permute-start(bf16[128,2048]{1,0:T(8,128)(2,1)S(1)} %pad_maximum_fusion.1), channel_id=1, source_target_pairs={{0,12},{4,8},{8,4},{12,0},{1,13},{5,9},{9,5},{13,1},{2,14},{6,10},... | collective-permute-start | bytes 1572872 | tf_op jit(solution)/shard_map/ppermute | solution.py:21
  61.4 24.2 %collective-permute-start.6 = (bf16[128,2048]{1,0:T(8,128)(2,1)S(1)}, bf16[128,2048]{1,0:T(8,128)(2,1)S(1)}, u32[]{:S(2)}, u32[]{:S(2)}) collective-permute-start(bf16[128,2048]{1,0:T(8,128)(2,1)S(1)} %pad_maximum_fusion.1), channel_id=1, source_target_pairs={{0,4},{4,0},{8,12},{12,8},{1,5},{5,1},{9,13},{13,9},{2,6},{6,2},{1... | collective-permute-start | bytes 1572872 | tf_op jit(solution)/shard_map/ppermute | solution.py:21
  86.9 15.3 %collective-permute-start.12 = (bf16[192,1024]{1,0:T(8,128)(2,1)S(1)}, bf16[192,1024]{1,0:T(8,128)(2,1)S(1)}, u32[]{:S(2)}, u32[]{:S(2)}) collective-permute-start(bf16[192,1024]{1,0:T(8,128)(2,1)S(1)} %pad_maximum_fusion.6), channel_id=1, source_target_pairs={{0,8},{4,12},{8,0},{12,4},{1,9},{5,13},{9,1},{13,5},{2,10},{6,14},... | collective-permute-start | bytes 1179656 | tf_op jit(solution)/shard_map/ppermute | solution.py:21
  116.3 11.4 %collective-permute-start.17 = (bf16[64,2048]{1,0:T(8,128)(2,1)S(1)}, bf16[64,2048]{1,0:T(8,128)(2,1)S(1)}, u32[]{:S(2)}, u32[]{:S(2)}) collective-permute-start(bf16[64,2048]{1,0:T(8,128)(2,1)S(1)} %get-tuple-element.102), channel_id=1, source_target_pairs={{0,3},{1,2},{2,1},{3,0},{4,7},{5,6},{6,5},{7,4},{8,11},{9,10},{10,... | collective-permute-start | bytes 786440 | tf_op jit(solution)/shard_map/ppermute | solution.py:21
  129.1 15.0 %collective-permute-start.20 = (bf16[32,2048]{1,0:T(8,128)(2,1)S(1)}, bf16[32,2048]{1,0:T(8,128)(2,1)S(1)}, u32[]{:S(2)}, u32[]{:S(2)}) collective-permute-start(bf16[32,2048]{1,0:T(8,128)(2,1)S(1)} %get-tuple-element.107), channel_id=1, source_target_pairs={{0,4},{4,0},{8,12},{12,8},{1,5},{5,1},{9,13},{13,9},{2,6},{6,2},{1... | collective-permute-start | bytes 393224 | tf_op jit(solution)/shard_map/ppermute | solution.py:21
  129.8 14.3 %collective-permute-start.22 = (bf16[32,2048]{1,0:T(8,128)(2,1)S(1)}, bf16[32,2048]{1,0:T(8,128)(2,1)S(1)}, u32[]{:S(2)}, u32[]{:S(2)}) collective-permute-start(bf16[32,2048]{1,0:T(8,128)(2,1)S(1)} %get-tuple-element.109), channel_id=1, source_target_pairs={{0,2},{1,3},{2,0},{3,1},{4,6},{5,7},{6,4},{7,5},{8,10},{9,11},{10,... | collective-permute-start | bytes 393224 | tf_op jit(solution)/shard_map/ppermute | solution.py:21
  130.6 13.6 %collective-permute-start.21 = (bf16[32,2048]{1,0:T(8,128)(2,1)S(1)}, bf16[32,2048]{1,0:T(8,128)(2,1)S(1)}, u32[]{:S(2)}, u32[]{:S(2)}) collective-permute-start(bf16[32,2048]{1,0:T(8,128)(2,1)S(1)} %get-tuple-element.109), channel_id=1, source_target_pairs={{0,3},{1,2},{2,1},{3,0},{4,7},{5,6},{6,5},{7,4},{8,11},{9,10},{10,... | collective-permute-start | bytes 393224 | tf_op jit(solution)/shard_map/ppermute | solution.py:21
  133.1 84.2 %all-to-all-start = ((bf16[16,2,384,128]{3,2,1,0:T(8,128)(2,1)}), bf16[16,2,384,128]{3,2,1,0:T(8,128)(2,1)}, u32[]{:S(2)}, u32[]{:S(2)}) async-start(bf16[16,2,384,128]{3,2,1,0:T(8,128)(2,1)} %get-tuple-element.85), calls=%async_computation | async-start | bytes 6291456 | tf_op jit(solution)/shard_map/all_to_all | solution.py:286
  146.5 13.2 %collective-permute-start.25 = (bf16[64,2048]{1,0:T(8,128)(2,1)S(1)}, bf16[64,2048]{1,0:T(8,128)(2,1)S(1)}, u32[]{:S(2)}, u32[]{:S(2)}) collective-permute-start(bf16[64,2048]{1,0:T(8,128)(2,1)S(1)} %pad_maximum_fusion.7), channel_id=1, source_target_pairs={{0,3},{1,2},{2,1},{3,0},{4,7},{5,6},{6,5},{7,4},{8,11},{9,10},{10,... | collective-permute-start | bytes 786440 | tf_op jit(solution)/shard_map/ppermute | solution.py:21
  148.5 13.2 %collective-permute-start.23 = (bf16[128,2048]{1,0:T(8,128)(2,1)S(1)}, bf16[128,2048]{1,0:T(8,128)(2,1)S(1)}, u32[]{:S(2)}, u32[]{:S(2)}) collective-permute-start(bf16[128,2048]{1,0:T(8,128)(2,1)S(1)} %pad_maximum_fusion.5), channel_id=1, source_target_pairs={{0,4},{4,0},{8,12},{12,8},{1,5},{5,1},{9,13},{13,9},{2,6},{6,2},{1... | collective-permute-start | bytes 1572872 | tf_op jit(solution)/shard_map/ppermute | solution.py:21
  183.4 16.5 %collective-permute-start.27 = (bf16[128,2048]{1,0:T(8,128)(2,1)S(1)}, bf16[128,2048]{1,0:T(8,128)(2,1)S(1)}, u32[]{:S(2)}, u32[]{:S(2)}) collective-permute-start(bf16[128,2048]{1,0:T(8,128)(2,1)S(1)} %slice.186), channel_id=1, source_target_pairs={{0,4},{4,0},{8,12},{12,8},{1,5},{5,1},{9,13},{13,9},{2,6},{6,2},{1... | collective-permute-start | bytes 1572872 | tf_op jit(solution)/shard_map/ppermute | solution.py:21
  186.4 13.4 %collective-permute-start.29 = (bf16[64,2048]{1,0:T(8,128)(2,1)S(1)}, bf16[64,2048]{1,0:T(8,128)(2,1)S(1)}, u32[]{:S(2)}, u32[]{:S(2)}) collective-permute-start(bf16[64,2048]{1,0:T(8,128)(2,1)S(1)} %get-tuple-element.97), channel_id=1, source_target_pairs={{0,3},{1,2},{2,1},{3,0},{4,7},{5,6},{6,5},{7,4},{8,11},{9,10},{10,... | collective-permute-start | bytes 786440 | tf_op jit(solution)/shard_map/ppermute | solution.py:21
  188.3 11.5 %collective-permute-start.28 = (bf16[64,2048]{1,0:T(8,128)(2,1)S(1)}, bf16[64,2048]{1,0:T(8,128)(2,1)S(1)}, u32[]{:S(2)}, u32[]{:S(2)}) collective-permute-start(bf16[64,2048]{1,0:T(8,128)(2,1)S(1)} %get-tuple-element.98), channel_id=1, source_target_pairs={{0,1},{1,0},{2,3},{3,2},{4,5},{5,4},{6,7},{7,6},{8,9},{9,8},{10,11... | collective-permute-start | bytes 786440 | tf_op jit(solution)/shard_map/ppermute | solution.py:21
  201.0 65.9 %collective-permute-start.32 = (bf16[32,2048]{1,0:T(8,128)(2,1)S(1)}, bf16[32,2048]{1,0:T(8,128)(2,1)S(1)}, u32[]{:S(2)}, u32[]{:S(2)}) collective-permute-start(bf16[32,2048]{1,0:T(8,128)(2,1)S(1)} %slice.193), channel_id=1, source_target_pairs={{0,4},{4,0},{8,12},{12,8},{1,5},{5,1},{9,13},{13,9},{2,6},{6,2},{1... | collective-permute-start | bytes 393224 | tf_op jit(solution)/shard_map/ppermute | solution.py:21
  204.4 62.5 %collective-permute-start.34 = (bf16[32,2048]{1,0:T(8,128)(2,1)}, bf16[32,2048]{1,0:T(8,128)(2,1)S(1)}, u32[]{:S(2)}, u32[]{:S(2)}) collective-permute-start(bf16[32,2048]{1,0:T(8,128)(2,1)} %get-tuple-element.104), channel_id=1, source_target_pairs={{0,2},{1,3},{2,0},{3,1},{4,6},{5,7},{6,4},{7,5},{8,10},{9,11},{10,... | collective-permute-start | bytes 393224 | tf_op jit(solution)/shard_map/ppermute | solution.py:21
  205.8 61.2 %collective-permute-start.33 = (bf16[32,2048]{1,0:T(8,128)(2,1)S(1)}, bf16[32,2048]{1,0:T(8,128)(2,1)S(1)}, u32[]{:S(2)}, u32[]{:S(2)}) collective-permute-start(bf16[32,2048]{1,0:T(8,128)(2,1)S(1)} %get-tuple-element.105), channel_id=1, source_target_pairs={{0,3},{1,2},{2,1},{3,0},{4,7},{5,6},{6,5},{7,4},{8,11},{9,10},{10,... | collective-permute-start | bytes 393224 | tf_op jit(solution)/shard_map/ppermute | solution.py:21
  205.8 61.2 %collective-permute-start.31 = (bf16[32,2048]{1,0:T(8,128)(2,1)S(1)}, bf16[32,2048]{1,0:T(8,128)(2,1)S(1)}, u32[]{:S(2)}, u32[]{:S(2)}) collective-permute-start(bf16[32,2048]{1,0:T(8,128)(2,1)S(1)} %get-tuple-element.106), channel_id=1, source_target_pairs={{0,1},{1,0},{2,3},{3,2},{4,5},{5,4},{6,7},{7,6},{8,9},{9,8},{10,11... | collective-permute-start | bytes 393224 | tf_op jit(solution)/shard_map/ppermute | solution.py:21
  (32 other events, 388.3 us)
Sparse Core Ops, SparseCore 0:
  36.7 44.6 all-gather.3
  103.1 57.4 all-gather.5
where the time goes:
time: 276 us; the launch traced here: 275 us
  waiting for transfers between devices  68.1 us (25%)
  Pallas kernels  59.1 us (21%)
  starting transfers between devices  53.8 us (19%)
  local copies, waits for them, and re-layouts  41.5 us (15%)
  other arithmetic  19.9 us (7%)
  matrix products  17.8 us (6%)
  between operations  14.5 us (5%)
    ppermute x35, waiting for transfers between devices, swap(): return lax.ppermute(array, axis, [(i, i ^ k) for i in range(size)])  59.1 us
    pallas_call x1, Pallas kernels, pick(): pl.pallas_call(pick_kernel, out_shape=jax.ShapeDtypeStruct(shape, moved.d...  49.6 us
    ppermute x35, starting transfers between devices, swap(): return lax.ppermute(array, axis, [(i, i ^ k) for i in range(size)])  42.7 us
    unnamed x57, local copies, waits for them, and re-layouts  22 us
    all_to_all x1, starting transfers between devices, body(): moved = lax.all_to_all(sent, 'rep', split_axis=0, concat_axis=0, tiled=True)  11.1 us
    pallas_call x1, Pallas kernels, attend(): pl.pallas_call(attend_kernel, out_shape=(jax.ShapeDtypeStruct((slots * sp...  9.44 us
    all_to_all x1, waiting for transfers between devices, body(): moved = lax.all_to_all(sent, 'rep', split_axis=0, concat_axis=0, tiled=True)  8.87 us
    dot_general x2, matrix products, body(): gate_up = jnp.dot(tokens, w_in, preferred_element_type=jnp.float32)  6.47 us
  transfers between devices with their start and end apart: 38, of which 15 were waited for; matrix products, arithmetic and copies ran while one was open for 24% of the time, Pallas kernels for 21%

commit v1 on v0

v1 whole, which is shorter than its diff:
```python
import math

import jax
import jax.numpy as jnp
import numpy as np
from jax import lax
from jax.experimental import pallas as pl
from jax.experimental.pallas import tpu as pltpu
from jax.sharding import PartitionSpec as P

EPSILON = 1e-05


def layer_norm(values):
    centred = values - jnp.mean(values, axis=-1, keepdims=True)
    spread = jnp.mean(centred * centred, axis=-1, keepdims=True)
    return centred * lax.rsqrt(spread + EPSILON)


def swap(axis, k, array):
    size = lax.axis_size(axis)
    return lax.ppermute(array, axis, [(i, i ^ k) for i in range(size)])


def together(sent):
    got = [swap(axis, k, array) for axis, k, array in sent]
    return lax.optimization_barrier(got)


def join(pieces):
    return lax.optimization_barrier(jnp.concatenate(pieces, axis=0))


def gather_plane(one, two, half):
    got = together([x for k in (1, 3, 2) for x in (("col", k, one), ("row", k, two))])
    extra = jnp.stack([two[half:], got[1][half:], got[5][half:], got[3][half:]], axis=0)
    one = join([one, got[0], got[4], got[2]])
    two = join([two[:half], got[1][:half], got[5][:half], got[3][:half]])
    got = together([x for k in (1, 3, 2) for x in (("row", k, one), ("col", k, two))])
    return [one, got[0], got[4], got[2], two, got[1], got[5], got[3]], extra


def gather_block(one, two):
    got = together([("col", 1, one), ("row", 1, two), ("col", 3, one), ("col", 2, one)])
    two = join([two, got[1]])
    one = join([one, got[0], got[3], got[2]])
    got = together([("col", 1, two), ("row", 1, one), ("col", 3, two), ("col", 2, two)])
    return [one, got[1], two, got[0], got[3], got[2]]


def wide_sum(arrays):
    total = arrays[0].astype(jnp.float32)
    for array in arrays[1:]:
        total = total + array.astype(jnp.float32)
    return total


def scatter_block(sums, half):
    one, two = sums[:2], sums[2:]
    got = together([("col", 1, two[1]), ("row", 1, one[1]), ("col", 3, two[3]), ("col", 2, two[2])])
    one = wide_sum([one[0], got[1]]).astype(jnp.bfloat16)
    two = wide_sum([two[0], got[0], got[3], got[2]]).astype(jnp.bfloat16)
    one = [one[half * n : half * (n + 1)] for n in range(4)]
    two = [two[half * n : half * (n + 1)] for n in range(2)]
    got = together([("col", 1, one[1]), ("row", 1, two[1]), ("col", 3, one[3]), ("col", 2, one[2])])
    return jnp.concatenate(
        [wide_sum([one[0], got[0], got[3], got[2]]), wide_sum([two[0], got[1]])], axis=0
    )


def norm_kernel(rows_ref, extra_ref, one_ref, two_ref):
    half = one_ref.shape[0]
    normed = layer_norm(rows_ref[...].astype(jnp.float32)).astype(jnp.bfloat16)
    one_ref[...] = normed[:half]
    two_ref[:half] = normed[half:]
    two_ref[half:] = extra_ref[...]


def norm(rows, extra):
    half, width = rows.shape[0] // 2, rows.shape[1]
    return pl.pallas_call(
        norm_kernel,
        out_shape=(
            jax.ShapeDtypeStruct((half, width), jnp.bfloat16),
            jax.ShapeDtypeStruct((half + extra.shape[0], width), jnp.bfloat16),
        ),
        cost_estimate=pl.CostEstimate(
            flops=8 * rows.size, transcendentals=0, bytes_accessed=4 * rows.size
        ),
        name="norm",
    )(rows, extra)


def mid_kernel(rows_ref, own_ref, a_ref, b_ref, c_ref, middle_ref, one_ref, two_ref):
    half = one_ref.shape[0]
    attention = wide_sum([own_ref[...], a_ref[...], b_ref[...], c_ref[...]])
    middle = (rows_ref[...].astype(jnp.float32) + attention).astype(jnp.bfloat16)
    middle_ref[...] = middle
    normed = layer_norm(middle.astype(jnp.float32)).astype(jnp.bfloat16)
    one_ref[...] = normed[:half]
    two_ref[...] = normed[half:]


def mid(rows, own, others):
    half, width = rows.shape[0] // 2, rows.shape[1]
    part = jax.ShapeDtypeStruct((half, width), jnp.bfloat16)
    return pl.pallas_call(
        mid_kernel,
        out_shape=(jax.ShapeDtypeStruct(rows.shape, jnp.bfloat16), part, part),
        cost_estimate=pl.CostEstimate(
            flops=12 * rows.size, transcendentals=0, bytes_accessed=14 * rows.size
        ),
        name="mid",
    )(rows, own, *others)


def joined_kernel(*refs):
    pieces, (heads_ref, out_ref, rows_ref, sems) = refs[:8], refs[8:]
    tall = pieces[0].shape[0]
    copies = [
        pltpu.make_async_copy(piece, rows_ref.at[pl.ds(tall * n, tall)], sems.at[n])
        for n, piece in enumerate(pieces)
    ]
    for copy in copies:
        copy.start()
    for n in range(4):
        copies[2 * n].wait()
        copies[2 * n + 1].wait()
        span = pl.ds(2 * tall * n, 2 * tall)
        out_ref[span, :] = jnp.dot(
            rows_ref[span, :], heads_ref[...], preferred_element_type=jnp.float32
        )


def join_heads(pieces, heads):
    tall, width = pieces[0].shape
    shape = (len(pieces) * tall, heads.shape[1])
    return pl.pallas_call(
        joined_kernel,
        out_shape=jax.ShapeDtypeStruct(shape, jnp.float32),
        in_specs=[pl.BlockSpec(memory_space=pl.ANY)] * len(pieces)
        + [pl.BlockSpec(memory_space=pltpu.VMEM)],
        out_specs=pl.BlockSpec(memory_space=pltpu.VMEM),
        scratch_shapes=[
            pltpu.VMEM((shape[0], width), jnp.bfloat16),
            pltpu.SemaphoreType.DMA((len(pieces),)),
        ],
        compiler_params=pltpu.CompilerParams(vmem_limit_bytes=24 << 20),
        cost_estimate=pl.CostEstimate(
            flops=2 * shape[0] * width * shape[1], transcendentals=0, bytes_accessed=7 << 20
        ),
        name="join_heads",
    )(*pieces, heads)


def feed_kernel(*refs):
    pieces, (w_in_ref, w_down_ref, fed_ref), outs = refs[:6], refs[6:9], refs[9:15]
    rows_ref, in_ref, down_ref, hidden_ref, sems = refs[15:]
    units, width = w_down_ref.shape
    shares, tall, _ = fed_ref.shape
    part_in, part_down = width // shares, units // shares
    jobs, at = [], 0
    for piece in pieces:
        jobs.append((piece, rows_ref.at[pl.ds(at, piece.shape[0])]))
        at += piece.shape[0]
    jobs.append((w_in_ref, in_ref.at[0]))
    jobs.append((w_down_ref, down_ref.at[0]))
    half = width // 2
    for r in range(shares):
        jobs.append(
            (fed_ref.at[r, pl.ds(0, part_in)], in_ref.at[1, pl.ds(part_in * r, part_in)])
        )
        for n in range(2):
            jobs.append(
                (
                    fed_ref.at[r, pl.ds(part_in + part_down * n, part_down)],
                    down_ref.at[1, pl.ds(part_down * r, part_down), pl.ds(half * n, half)],
                )
            )
    copies = [
        pltpu.make_async_copy(source, target, sems.at[n])
        for n, (source, target) in enumerate(jobs)
    ]
    for copy in copies:
        copy.start()
    for n, copy in enumerate(copies):
        if n < 7:
            copy.wait()
    step = 256
    for shard in range(2):
        if shard == 1:
            for copy in copies[7:]:
                copy.wait()

        @pl.loop(0, units // step)
        def _(j):
            at = pl.multiple_of(step * j, step)
            gate = jnp.dot(
                rows_ref[...],
                in_ref[shard, :, pl.ds(at, step)],
                preferred_element_type=jnp.float32,
            )
            up = jnp.dot(
                rows_ref[...],
                in_ref[shard, :, pl.ds(pl.multiple_of(units + at, step), step)],
                preferred_element_type=jnp.float32,
            )
            hidden = gate / (1.0 + jnp.exp(-gate)) * up
            hidden_ref[shard, :, pl.ds(at, step)] = hidden.astype(jnp.bfloat16)

    @pl.loop(0, width // step)
    def _(j):
        span = pl.ds(pl.multiple_of(step * j, step), step)
        total = jnp.dot(
            hidden_ref[0], down_ref[0, :, span], preferred_element_type=jnp.float32
        ) + jnp.dot(hidden_ref[1], down_ref[1, :, span], preferred_element_type=jnp.float32)
        total = total.astype(jnp.bfloat16)
        at = 0
        for out in outs:
            out[:, span] = total[at : at + out.shape[0]]
            at += out.shape[0]


def feed(pieces, w_in, w_down, fed):
    units, width = w_down.shape
    rows = sum(piece.shape[0] for piece in pieces)
    return pl.pallas_call(
        feed_kernel,
        out_shape=[jax.ShapeDtypeStruct(piece.shape, jnp.bfloat16) for piece in pieces],
        in_specs=[pl.BlockSpec(memory_space=pl.ANY)] * (len(pieces) + 3),
        out_specs=[pl.BlockSpec(memory_space=pltpu.VMEM)] * len(pieces),
        scratch_shapes=[
            pltpu.VMEM((rows, width), jnp.bfloat16),
            pltpu.VMEM((2, width, 2 * units), jnp.bfloat16),
            pltpu.VMEM((2, units, width), jnp.bfloat16),
            pltpu.VMEM((2, rows, units), jnp.bfloat16),
            pltpu.SemaphoreType.DMA((len(pieces) + 2 + 3 * fed.shape[0],)),
        ],
        compiler_params=pltpu.CompilerParams(vmem_limit_bytes=48 << 20),
        cost_estimate=pl.CostEstimate(
            flops=12 * rows * width * units, transcendentals=2 * rows * units,
            bytes_accessed=16 << 20,
        ),
        name="feed",
    )(*pieces, w_in, w_down, fed)


def attend_kernel(
    place_ref, length_ref, span_ref, target_ref,
    joined_ref, cache_ref, cos_ref, sin_ref, far_cos_ref, far_sin_ref, context_ref, new_ref,
):
    g = pl.program_id(0)
    row, column = place_ref[0], place_ref[1]
    request = request_of(g, row)
    length_old = length_ref[request]
    away = row ^ (request // 2)
    columns = [column ^ (2 * (request % 2) + n) for n in range(2)]

    def block(n):
        return joined_ref[pl.ds(pl.multiple_of(32 * n, 32), 32), :]

    joined = jnp.concatenate(
        [block(n) for c in columns for n in (4 * away + c, 16 + 4 * c + away)], axis=0
    )
    far_cos, far_sin = far_cos_ref[pl.ds(request, 1), :], far_sin_ref[pl.ds(request, 1), :]
    cosine = far_cos * cos_ref[...] - far_sin * sin_ref[...]
    sine = far_sin * cos_ref[...] + far_cos * sin_ref[...]

    def turned(part):
        return (part * cosine + pltpu.roll(part, 64, axis=1) * sine).astype(jnp.bfloat16)

    queries = turned(joined[:, :128])
    keys_new = turned(joined[:, 128:256])
    values_new = joined[:, 256:].astype(jnp.bfloat16)
    stored = cache_ref.shape[2]
    whole = new_ref.shape[2]
    live = lax.broadcasted_iota(jnp.int32, keys_new.shape, 0) < span_ref[request]
    rows = lax.broadcasted_iota(jnp.int32, (whole, keys_new.shape[1]), 0)
    for kind, fresh in enumerate((keys_new, values_new)):
        fresh = jnp.where(live, fresh.astype(jnp.float32), 0.0)
        fresh = jnp.concatenate(
            [fresh, jnp.zeros((whole - fresh.shape[0], fresh.shape[1]), jnp.float32)], axis=0
        )
        old = cache_ref[0, kind].astype(jnp.float32)
        old = jnp.concatenate(
            [old, jnp.zeros((whole - stored, old.shape[1]), jnp.float32)], axis=0
        )
        fresh = pltpu.roll(fresh, length_old, axis=0)
        new_ref[0, kind] = jnp.where(rows < length_old, old, fresh).astype(jnp.bfloat16)
    scale = 1.0 / math.sqrt(128)
    contract = (((1,), (1,)), ((), ()))
    old = (
        lax.dot_general(queries, cache_ref[0, 0], contract, preferred_element_type=jnp.float32)
        * scale
    )
    new = (
        lax.dot_general(queries, keys_new, contract, preferred_element_type=jnp.float32) * scale
    )
    old_ok = lax.broadcasted_iota(jnp.int32, old.shape, 1) < length_old
    new_ok = lax.broadcasted_iota(jnp.int32, new.shape, 1) <= lax.broadcasted_iota(
        jnp.int32, new.shape, 0
    )
    old = jnp.where(old_ok, old, -1e30)
    new = jnp.where(new_ok, new, -1e30)
    highest = jnp.maximum(
        jnp.max(old, axis=1, keepdims=True), jnp.max(new, axis=1, keepdims=True)
    )
    old = jnp.where(old_ok, jnp.exp(old - highest), 0.0)
    new = jnp.where(new_ok, jnp.exp(new - highest), 0.0)
    total = jnp.sum(old, axis=1, keepdims=True) + jnp.sum(new, axis=1, keepdims=True)
    old_weights = (old / total).astype(jnp.bfloat16)
    new_weights = (new / total).astype(jnp.bfloat16)
    stored_values = cache_ref[0, 1]
    context = jnp.dot(
        old_weights, stored_values, preferred_element_type=jnp.float32
    ) + jnp.dot(new_weights, values_new, preferred_element_type=jnp.float32)
    context = context.astype(jnp.bfloat16)
    for n in range(2):
        place = pl.multiple_of(64 * (4 * (g // 2) + columns[n]), 64)
        context_ref[pl.ds(place, 64), :] = context[64 * n : 64 * n + 64]


def request_of(g, row):
    return 2 * (row ^ (g // 2)) + g % 2


def attend(place, lengths, spans, targets, joined, cache, tables, replicas):
    slots, kinds, stored, size = cache.shape
    span = tables[0].shape[0]
    whole = lambda g, *refs: (0, 0)
    return pl.pallas_call(
        attend_kernel,
        out_shape=(
            jax.ShapeDtypeStruct((slots * span, size), jnp.bfloat16),
            jax.ShapeDtypeStruct((replicas, kinds, stored + span, size), jnp.bfloat16),
        ),
        grid_spec=pltpu.PrefetchScalarGridSpec(
            num_scalar_prefetch=4,
            grid=(slots,),
            in_specs=[
                pl.BlockSpec(joined.shape, whole),
                pl.BlockSpec(
                    (1, kinds, stored, size),
                    lambda g, place, *refs: (request_of(g, place[0]), 0, 0, 0),
                ),
            ]
            + [pl.BlockSpec(table.shape, whole) for table in tables],
            out_specs=[
                pl.BlockSpec((slots * span, size), whole),
                pl.BlockSpec(
                    (1, kinds, stored + span, size),
                    lambda g, place, lengths, spans, targets: (
                        targets[request_of(g, place[0])], 0, 0, 0,
                    ),
                ),
            ],
        ),
        cost_estimate=pl.CostEstimate(
            flops=4 * slots * span * (stored + span) * size,
            transcendentals=slots * span * (stored + span),
            bytes_accessed=6 << 20,
        ),
        name="attend",
    )(place, lengths, spans, targets, joined, cache, *tables)


def pick_kernel(source_ref, moved_ref, out_ref, held_ref, sems):
    slots = out_ref.shape[0]
    taken = [
        pltpu.make_async_copy(moved_ref.at[source_ref[t]], held_ref.at[t], sems.at[0, t])
        for t in range(slots)
    ]
    given = [
        pltpu.make_async_copy(held_ref.at[t], out_ref.at[t], sems.at[1, t]) for t in range(slots)
    ]
    for copy in taken:
        copy.start()
    for t in range(slots):
        taken[t].wait()
        given[t].start()
    for copy in given:
        copy.wait()


def pick(moved, source):
    shape = (source.shape[0],) + moved.shape[1:]
    return pl.pallas_call(
        pick_kernel,
        out_shape=jax.ShapeDtypeStruct(shape, moved.dtype),
        in_specs=[pl.BlockSpec(memory_space=pltpu.SMEM), pl.BlockSpec(memory_space=pl.ANY)],
        out_specs=pl.BlockSpec(memory_space=pl.ANY),
        scratch_shapes=[pltpu.VMEM(shape, moved.dtype), pltpu.SemaphoreType.DMA((2, shape[0]))],
        cost_estimate=pl.CostEstimate(
            flops=0, transcendentals=0, bytes_accessed=4 * math.prod(shape)
        ),
        name="pick",
    )(source, moved)


def body(hidden_in, w_qkv, w_out, w_gate_up, w_down, cache, span_len, cache_len, new_slot):
    slots, kinds, stored, _, size = cache.shape
    local_rows, width = hidden_in.shape
    units = w_down.shape[0]
    span = 16 * local_rows // slots
    replica = lax.axis_index("rep")
    replicas = lax.axis_size("rep")
    row, column = lax.axis_index("row"), lax.axis_index("col")
    cache = cache.reshape(slots, kinds, stored, size)
    lengths = lax.dynamic_slice_in_dim(cache_len, replica * slots, slots)
    spans = lax.dynamic_slice_in_dim(span_len, replica * slots, slots)
    targets = lax.dynamic_slice_in_dim(new_slot, replica * slots, slots) // slots
    my_slots = replica * slots + jnp.arange(slots, dtype=jnp.int32)
    arrivals = (new_slot[None, :] == my_slots[:, None]).astype(jnp.int32)
    requests = jnp.arange(new_slot.shape[0], dtype=jnp.int32)
    source = jnp.sum(arrivals * (requests // slots)[None, :], axis=1)

    share = size // replicas
    out_slice = lax.dynamic_slice_in_dim(w_out.reshape(size, width), replica * share, share)
    rows_in, rows_down = width // replicas, units // replicas
    in_slice = lax.dynamic_slice_in_dim(w_gate_up, replica * rows_in, rows_in)
    down_slice = lax.dynamic_slice_in_dim(w_down, replica * rows_down, rows_down)
    feed_slice = jnp.concatenate(
        [in_slice.reshape(rows_in, 2 * units), down_slice[:, : 2 * units], down_slice[:, 2 * units :]],
        axis=0,
    )

    one, two = norm(hidden_in, out_slice)
    pieces, out_slices = gather_plane(one, two, local_rows // 2)
    w_rows = lax.all_gather(out_slices, "rep", axis=1, tiled=True).reshape(4 * size, width)
    w_in = w_gate_up.reshape(width, 2 * units)
    pieces, w_in, feed_slice = lax.optimization_barrier((pieces, w_in, feed_slice))
    feed_far = swap("row", 2, feed_slice)
    joined = join_heads(pieces, w_qkv.reshape(width, 3 * size))
    joined, feed_far = lax.optimization_barrier((joined, feed_far))
    fed = lax.all_gather(feed_far, "rep", axis=0, tiled=False)

    frequency = 10000.0 ** (-(np.arange(size // 2) * 2.0 / size))
    frequency = np.concatenate([frequency, frequency])[None, :]
    sign = np.where(np.arange(size) < size // 2, -1.0, 1.0)[None, :]
    near = np.arange(span)[:, None] * frequency
    far = lengths.astype(jnp.float32)[:, None] * jnp.asarray(frequency, jnp.float32)
    tables = (
        jnp.asarray(np.cos(near), jnp.float32),
        jnp.asarray(np.sin(near) * sign, jnp.float32),
        jnp.cos(far),
        jnp.sin(far) * jnp.asarray(sign, jnp.float32),
    )
    place = jnp.stack([row, column]).astype(jnp.int32)
    context, sent = attend(place, lengths, spans, targets, joined, cache, tables, replicas)

    context = context.reshape(4, 4 * local_rows, size)
    got = together([("row", k, context[k]) for k in (1, 3, 2)])
    parts = jnp.concatenate([context[0], got[0], got[2], got[1]], axis=1)
    partial = jnp.dot(parts, w_rows, preferred_element_type=jnp.float32).astype(jnp.bfloat16)
    partial = partial.reshape(4, local_rows, width)
    got = together([("col", k, partial[k]) for k in (1, 3, 2)])
    middle, one, two = mid(hidden_in, partial[0], [got[0], got[2], got[1]])
    moved = lax.all_to_all(sent, "rep", split_axis=0, concat_axis=0, tiled=True)
    sums = feed(gather_block(one, two), w_in, w_down, fed)
    down_sum = scatter_block(sums, local_rows // 2)

    cache_out = pick(moved, source)
    first_row = (row * 4 + column) * local_rows
    within = first_row % span + jnp.arange(local_rows, dtype=jnp.int32)
    live = within < lax.dynamic_index_in_dim(spans, first_row // span, keepdims=False)
    hidden_out = jnp.where(live[:, None], middle.astype(jnp.float32) + down_sum, 0.0)
    return (
        hidden_out.astype(jnp.bfloat16),
        cache_out.reshape(slots, kinds, stored + span, 1, size),
    )


def solution(mesh):
    in_specs = (
        P(("rep", "row", "col"), None),
        P(None, ("row", "col"), None),
        P(("row", "col"), None, None),
        P(None, None, ("row", "col")),
        P(("row", "col"), None),
        P("rep", None, None, ("row", "col"), None),
        P(),
        P(),
        P(),
    )
    out_specs = (P(("rep", "row", "col"), None), P("rep", None, None, ("row", "col"), None))
    return jax.shard_map(body, mesh=mesh, in_specs=in_specs, out_specs=out_specs, check_vma=False)
```

time: 276 us -> 228 us (0.83)
  Pallas kernels: 59.1 us -> 33.3 us
  local copies, waits for them, and re-layouts: 41.5 us -> 23.2 us
  matrix products: 17.8 us -> 2.31 us
  waiting for transfers between devices: 68.1 us -> 80.2 us
  other arithmetic: 19.9 us -> 7.81 us
  starting transfers between devices: 53.8 us -> 64 us
    pallas_call x1, Pallas kernels: 49.6 us -> 3.09 us  [pick(): pl.pallas_call(pick_kernel, out_shape=jax.ShapeDtypeStruct(shape, moved.d...]
    all_gather x1, waiting for transfers between devices: 0.01 us -> 28.7 us  [body(): fed = lax.all_gather(feed_far, 'rep', axis=0, tiled=False)]
    pallas_call x0 -> x4, Pallas kernels: none -> 20.8 us  [the longest x1 12.4 us: feed(): pl.pallas_call(feed_kernel, out_shape=[jax.ShapeDtypeStruct(piece.shape,...]
    dot_general x6 -> x0, matrix products: 15.5 us -> none  [the longest x2 6.47 us: body(): gate_up = jnp.dot(tokens, w_in, preferred_element_type=jnp.float32)]
    all_to_all x1, waiting for transfers between devices: 8.87 us -> 0.01 us  [body(): moved = lax.all_to_all(sent, 'rep', split_axis=0, concat_axis=0, tiled=True)]
    ppermute x35, waiting for transfers between devices: 59.1 us -> 51.5 us  [swap(): return lax.ppermute(array, axis, [(i, i ^ k) for i in range(size)])]
    ppermute x35, starting transfers between devices: 42.7 us -> 49.6 us  [swap(): return lax.ppermute(array, axis, [(i, i ^ k) for i in range(size)])]
    unnamed x57 -> x48, local copies, waits for them, and re-layouts: 22 us -> 16 us
  transfers between devices with their start and end apart: 38 -> 38, of which waited for: 15 -> 23; matrix products, arithmetic and copies ran while one was open for 24% -> 9% of each run, Pallas kernels for 21% -> 14%
where the time goes in v1:
time: 228 us; the launch traced here: 225 us
  waiting for transfers between devices  80.2 us (35%)
  starting transfers between devices  64 us (28%)
  Pallas kernels  33.3 us (15%)
  local copies, waits for them, and re-layouts  23.2 us (10%)
  between operations  14.4 us (6%)
  other arithmetic  7.81 us (3%)
  matrix products  2.31 us (1%)
    ppermute x35, waiting for transfers between devices, swap(): return lax.ppermute(array, axis, [(i, i ^ k) for i in range(size)])  51.5 us
    ppermute x35, starting transfers between devices, swap(): return lax.ppermute(array, axis, [(i, i ^ k) for i in range(size)])  49.6 us
    all_gather x1, waiting for transfers between devices, body(): fed = lax.all_gather(feed_far, 'rep', axis=0, tiled=False)  28.7 us
    unnamed x48, local copies, waits for them, and re-layouts  16 us
    all_to_all x1, starting transfers between devices, body(): moved = lax.all_to_all(sent, 'rep', split_axis=0, concat_axis=0, tiled=True)  14.4 us
    pallas_call x1, Pallas kernels, feed(): pl.pallas_call(feed_kernel, out_shape=[jax.ShapeDtypeStruct(piece.shape,...  12.4 us
    pallas_call x1, Pallas kernels, attend(): pl.pallas_call(attend_kernel, out_shape=(jax.ShapeDtypeStruct((slots * sp...  9.39 us
  transfers between devices with their start and end apart: 38, of which 23 were waited for; matrix products, arithmetic and copies ran while one was open for 9% of the time, Pallas kernels for 14%

profile of v1, /device:TPU:1, one launch (start us, length us, event | category | flops | bytes accessed | tf_op | source)
XLA Modules:
  0.0 225.2 jit_solution(8298714805491096948)
XLA Ops:
  19.9 2.3 %collective-permute-done.2 = bf16[32,2048]{1,0:T(8,128)(2,1)S(1)} collective-permute-done((bf16[32,2048]{1,0:T(8,128)(2,1)}, bf16[32,2048]{1,0:T(8,128)(2,1)S(1)}, u32[]{:S(2)}, u32[]{:S(2)}) %collective-permute-start.2) | collective-permute-done | bytes 131104 | tf_op jit(solution)/shard_map/ppermute | solution.py:22
  22.2 2.2 collective-permute-done.4
  29.6 2.1 collective-permute-start.10
  32.1 6.2 %collective-permute-done.11.refs_6_ = bf16[128,2048]{1,0:T(8,128)(2,1)S(1)} collective-permute-done((bf16[128,2048]{1,0:T(8,128)(2,1)S(1)}, bf16[128,2048]{1,0:T(8,128)(2,1)S(1)}, u32[]{:S(2)}, u32[]{:S(2)}) %collective-permute-start.11) | collective-permute-done | bytes 524320 | tf_op jit(solution)/shard_map/ppermute | solution.py:22
  41.7 5.6 %copy.17 = bf16[256,8,2,512]{3,1,2,0:T(8,128)(2,1)} copy(bf16[256,8,2,512]{3,2,1,0:T(2,128)(2,1)} %bitcast.26) | data formatting | bytes 8388608
  48.5 4.5 %collective-permute-done.9.refs_7_ = bf16[128,2048]{1,0:T(8,128)(2,1)} collective-permute-done((bf16[128,2048]{1,0:T(8,128)(2,1)S(1)}, bf16[128,2048]{1,0:T(8,128)(2,1)}, u32[]{:S(2)}, u32[]{:S(2)}) %collective-permute-start.9) | collective-permute-done | bytes 524320 | tf_op jit(solution)/shard_map/ppermute | solution.py:22
  53.0 2.3 %collective-permute-start.12 = (bf16[192,1024]{1,0:T(8,128)(2,1)S(1)}, bf16[192,1024]{1,0:T(8,128)(2,1)S(1)}, u32[]{:S(2)}, u32[]{:S(2)}) collective-permute-start(bf16[192,1024]{1,0:T(8,128)(2,1)S(1)} %pad_maximum_fusion.3), channel_id=1, source_target_pairs={{0,8},{4,12},{8,0},{12,4},{1,9},{5,13},{9,1},{13,5},{2,10},{6,14},... | collective-permute-start | bytes 1179656 | tf_op jit(solution)/shard_map/ppermute | solution.py:22
  56.3 4.0 %join_heads.1.joined_ref = f32[1024,384]{1,0:T(8,128)S(1)} custom-call(bf16[128,2048]{1,0:T(8,128)(2,1)S(1)} %pad_maximum_fusion.refs_0_, bf16[128,2048]{1,0:T(8,128)(2,1)} %collective-permute-done.6.refs_1_, bf16[128,2048]{1,0:T(8,128)(2,1)} %collective-permute-done.10.refs_2_, bf16[128,2048]{1,0:T(8,128)(2,1)} %collective-permute-done.8.refs_3_, ...), custom_call_target="tpu_custom_call" | custom-call | flops 1610612736 | bytes 7340032 | tf_op jit(solution)/shard_map/join_heads/pallas_call | solution.py:138
  66.3 9.4 %attend.1 = (bf16[1024,128]{1,0:T(8,128)(2,1)}, bf16[16,2,384,128]{3,2,1,0:T(8,128)(2,1)}) custom-call(s32[2]{0:T(128)} %pad_add_fusion.place_ref, s32[8]{0:T(128)} %get-tuple-element.125.length_ref, s32[8]{0:T(128)} %dynamic_slice.29.span_ref, s32[8]{0:T(128)} %and_select_fusion.1.target_ref, f32[1024,384]{1,0:T(8,128)} %copy-done.1, ...), custom_call_target="tpu_custom_call" | custom-call | flops 201326592 | bytes 6291456 | tf_op jit(solution)/shard_map/attend/pallas_call | solution.py:331
  75.7 14.4 %all-to-all-start = ((bf16[16,2,384,128]{3,2,1,0:T(8,128)(2,1)}), bf16[16,2,384,128]{3,2,1,0:T(8,128)(2,1)}, u32[]{:S(2)}, u32[]{:S(2)}) async-start(bf16[16,2,384,128]{3,2,1,0:T(8,128)(2,1)} %get-tuple-element.119), calls=%async_computation | async-start | bytes 6291456 | tf_op jit(solution)/shard_map/all_to_all | solution.py:458
  97.2 2.3 %convolution_convert_fusion = bf16[256,2048]{1,0:T(8,128)(2,1)S(1)} fusion(bf16[512,2048]{1,0:T(8,128)(2,1)} %bitcast.33, bf16[256,128]{1,0:T(8,128)(2,1)S(1)} %collective-permute-done.14, bf16[256,128]{1,0:T(8,128)(2,1)S(1)} %collective-permute-done.15, bf16[256,128]{1,0:T(8,128)(2,1)S(1)} %collective-permute-done.13, bf16[256,128]{1,0:T(8,128)(2,1)S(1)} %get-tuple-element.135), kind=kOutput, calls=%fused_computation | convolution fusion | flops 538443776 | bytes 3407872 | tf_op jit(solution)/shard_map/dot_general | solution.py:454
  103.6 3.5 %collective-permute-done.16.a_ref = bf16[64,2048]{1,0:T(8,128)(2,1)S(1)} collective-permute-done((bf16[64,2048]{1,0:T(8,128)(2,1)S(1)}, bf16[64,2048]{1,0:T(8,128)(2,1)S(1)}, u32[]{:S(2)}, u32[]{:S(2)}) %collective-permute-start.16) | collective-permute-done | bytes 262176 | tf_op jit(solution)/shard_map/ppermute | solution.py:22
  108.9 4.8 %collective-permute-done.18.b_ref = bf16[64,2048]{1,0:T(8,128)(2,1)S(1)} collective-permute-done((bf16[64,2048]{1,0:T(8,128)(2,1)S(1)}, bf16[64,2048]{1,0:T(8,128)(2,1)S(1)}, u32[]{:S(2)}, u32[]{:S(2)}) %collective-permute-start.18) | collective-permute-done | bytes 262176 | tf_op jit(solution)/shard_map/ppermute | solution.py:22
  114.4 2.5 %mid.1 = (bf16[64,2048]{1,0:T(8,128)(2,1)}, bf16[32,2048]{1,0:T(8,128)(2,1)}, bf16[32,2048]{1,0:T(8,128)(2,1)}) custom-call(bf16[64,2048]{1,0:T(8,128)(2,1)} %rows_ref.3, bf16[64,2048]{1,0:T(8,128)(2,1)} %get-tuple-element.131.own_ref, bf16[64,2048]{1,0:T(8,128)(2,1)} %copy-done.12, bf16[64,2048]{1,0:T(8,128)(2,1)} %copy-done.14, bf16[64,2048]{1,0:T(8,128)(2,1)} %copy-done.13), custom_call_target="tpu_custom_call" | custom-call | flops 1572864 | bytes 1835008 | tf_op jit(solution)/shard_map/mid/pallas_call | solution.py:107
  131.2 2.2 collective-permute-done.23.refs_3_
  134.1 3.5 %collective-permute-done.25.refs_5_ = bf16[64,2048]{1,0:T(8,128)(2,1)S(1)} collective-permute-done((bf16[64,2048]{1,0:T(8,128)(2,1)S(1)}, bf16[64,2048]{1,0:T(8,128)(2,1)S(1)}, u32[]{:S(2)}, u32[]{:S(2)}) %collective-permute-start.25) | collective-permute-done | bytes 262176 | tf_op jit(solution)/shard_map/ppermute | solution.py:22
  140.4 28.7 %all-gather.6.cloned.1.call-done = bf16[3072,1024]{1,0:T(8,128)(2,1)} async-done(((bf16[192,1024]{1,0:T(8,128)(2,1)}), bf16[3072,1024]{1,0:T(8,128)(2,1)}) %all-gather.6.cloned.1.call-update) | async-done | bytes 6291472 | tf_op jit(solution)/shard_map/all_gather | solution.py:435
  171.9 12.4 %feed.1 = (bf16[128,2048]{1,0:T(8,128)(2,1)S(1)}, bf16[128,2048]{1,0:T(8,128)(2,1)S(1)}, bf16[64,2048]{1,0:T(8,128)(2,1)S(1)}, bf16[64,2048]{1,0:T(8,128)(2,1)},...) custom-call(bf16[128,2048]{1,0:T(8,128)(2,1)S(1)} %pad_maximum_fusion.2.refs_0_, ...), custom_call_target="tpu_custom_call" | custom-call | flops 6442450944 | bytes 16777216 | tf_op jit(solution)/shard_map/feed/pallas_call | solution.py:227
  184.3 3.7 %collective-permute-start.28 = (bf16[128,2048]{1,0:T(8,128)(2,1)S(1)}, bf16[128,2048]{1,0:T(8,128)(2,1)S(1)}, u32[]{:S(2)}, u32[]{:S(2)}) collective-permute-start(bf16[128,2048]{1,0:T(8,128)(2,1)S(1)} %get-tuple-element.107), channel_id=1, source_target_pairs={{0,4},{4,0},{8,12},{12,8},{1,5},{5,1},{9,13},{13,9},{2,6},{6,2},{1... | collective-permute-start | bytes 1572872 | tf_op jit(solution)/shard_map/ppermute | solution.py:22
  188.0 6.3 %collective-permute-start.27 = (bf16[64,2048]{1,0:T(8,128)(2,1)}, bf16[64,2048]{1,0:T(8,128)(2,1)S(1)}, u32[]{:S(2)}, u32[]{:S(2)}) collective-permute-start(bf16[64,2048]{1,0:T(8,128)(2,1)} %get-tuple-element.106), channel_id=1, source_target_pairs={{0,1},{1,0},{2,3},{3,2},{4,5},{5,4},{6,7},{7,6},{8,9},{9,8},{10,11... | collective-permute-start | bytes 786440 | tf_op jit(solution)/shard_map/ppermute | solution.py:22
  194.3 2.1 collective-permute-start.29
  197.8 2.7 %collective-permute-done.27 = bf16[64,2048]{1,0:T(8,128)(2,1)S(1)} collective-permute-done((bf16[64,2048]{1,0:T(8,128)(2,1)}, bf16[64,2048]{1,0:T(8,128)(2,1)S(1)}, u32[]{:S(2)}, u32[]{:S(2)}) %collective-permute-start.27) | collective-permute-done | bytes 262176 | tf_op jit(solution)/shard_map/ppermute | solution.py:22
  200.5 6.2 %collective-permute-done.29 = bf16[64,2048]{1,0:T(8,128)(2,1)S(1)} collective-permute-done((bf16[64,2048]{1,0:T(8,128)(2,1)}, bf16[64,2048]{1,0:T(8,128)(2,1)S(1)}, u32[]{:S(2)}, u32[]{:S(2)}) %collective-permute-start.29) | collective-permute-done | bytes 262176 | tf_op jit(solution)/shard_map/ppermute | solution.py:22
  214.2 3.1 %pick.1 = bf16[8,2,384,128]{3,2,1,0:T(8,128)(2,1)} custom-call(s32[8]{0:T(128)} %select_reduce_fusion.source_ref, bf16[16,2,384,128]{3,2,1,0:T(8,128)(2,1)} %all-to-all-done.moved_ref), custom_call_target="tpu_custom_call" | custom-call | bytes 3145728 | tf_op jit(solution)/shard_map/pick/pallas_call | solution.py:387
  (144 shorter events, 74.0 us)
Async XLA Ops:
  7.2 90.0 %all-gather.4.cloned.1.call-start = ((), (), s32[]{:S(2)}) async-start(), calls=%async_computation.1 | async-start | bytes 2228224 | tf_op jit(solution)/shard_map/all_gather | solution.py:429
  12.8 11.6 %collective-permute-start.1 = (bf16[40,2048]{1,0:T(8,128)(2,1)}, bf16[40,2048]{1,0:T(8,128)(2,1)S(1)}, u32[]{:S(2)}, u32[]{:S(2)}) collective-permute-start(bf16[40,2048]{1,0:T(8,128)(2,1)} %get-tuple-element.62), channel_id=1, source_target_pairs={{0,4},{4,0},{8,12},{12,8},{1,5},{5,1},{9,13},{13,9},{2,6},{6,2},{1... | collective-permute-start | bytes 491528 | tf_op jit(solution)/shard_map/ppermute | solution.py:22
  14.1 10.3 %collective-permute-start.3 = (bf16[40,2048]{1,0:T(8,128)(2,1)}, bf16[40,2048]{1,0:T(8,128)(2,1)S(1)}, u32[]{:S(2)}, u32[]{:S(2)}) collective-permute-start(bf16[40,2048]{1,0:T(8,128)(2,1)} %get-tuple-element.62), channel_id=1, source_target_pairs={{0,12},{4,8},{8,4},{12,0},{1,13},{5,9},{9,5},{13,1},{2,14},{6,10},... | collective-permute-start | bytes 491528 | tf_op jit(solution)/shard_map/ppermute | solution.py:22
  16.0 8.4 %collective-permute-start.5 = (bf16[40,2048]{1,0:T(8,128)(2,1)}, bf16[40,2048]{1,0:T(8,128)(2,1)S(1)}, u32[]{:S(2)}, u32[]{:S(2)}) collective-permute-start(bf16[40,2048]{1,0:T(8,128)(2,1)} %get-tuple-element.62), channel_id=1, source_target_pairs={{0,8},{4,12},{8,0},{12,4},{1,9},{5,13},{9,1},{13,5},{2,10},{6,14},... | collective-permute-start | bytes 491528 | tf_op jit(solution)/shard_map/ppermute | solution.py:22
  25.1 143.9 %all-gather.6.cloned.1.call-start = ((), (), s32[]{:S(2)}) async-start(), calls=%async_computation.2 | async-start | bytes 6684672 | tf_op jit(solution)/shard_map/all_gather | solution.py:435
  26.2 12.1 %collective-permute-start.11 = (bf16[128,2048]{1,0:T(8,128)(2,1)S(1)}, bf16[128,2048]{1,0:T(8,128)(2,1)S(1)}, u32[]{:S(2)}, u32[]{:S(2)}) collective-permute-start(bf16[128,2048]{1,0:T(8,128)(2,1)S(1)} %pad_maximum_fusion.1.refs_4_), channel_id=1, source_target_pairs={{0,2},{1,3},{2,0},{3,1},{4,6},{5,7},{6,4},{7,5},{8,10},{9,11},{10,... | collective-permute-start | bytes 1572872 | tf_op jit(solution)/shard_map/ppermute | solution.py:22
  28.2 20.3 %collective-permute-start.7 = (bf16[128,2048]{1,0:T(8,128)(2,1)S(1)}, bf16[128,2048]{1,0:T(8,128)(2,1)}, u32[]{:S(2)}, u32[]{:S(2)}) collective-permute-start(bf16[128,2048]{1,0:T(8,128)(2,1)S(1)} %pad_maximum_fusion.1.refs_4_), channel_id=1, source_target_pairs={{0,1},{1,0},{2,3},{3,2},{4,5},{5,4},{6,7},{7,6},{8,9},{9,8},{10,11... | collective-permute-start | bytes 1572872 | tf_op jit(solution)/shard_map/ppermute | solution.py:22
  28.2 24.8 %collective-permute-start.9 = (bf16[128,2048]{1,0:T(8,128)(2,1)S(1)}, bf16[128,2048]{1,0:T(8,128)(2,1)}, u32[]{:S(2)}, u32[]{:S(2)}) collective-permute-start(bf16[128,2048]{1,0:T(8,128)(2,1)S(1)} %pad_maximum_fusion.1.refs_4_), channel_id=1, source_target_pairs={{0,3},{1,2},{2,1},{3,0},{4,7},{5,6},{6,5},{7,4},{8,11},{9,10},{10,... | collective-permute-start | bytes 1572872 | tf_op jit(solution)/shard_map/ppermute | solution.py:22
  29.6 23.4 %collective-permute-start.10 = (bf16[128,2048]{1,0:T(8,128)(2,1)S(1)}, bf16[128,2048]{1,0:T(8,128)(2,1)}, u32[]{:S(2)}, u32[]{:S(2)}) collective-permute-start(bf16[128,2048]{1,0:T(8,128)(2,1)S(1)} %pad_maximum_fusion.refs_0_), channel_id=1, source_target_pairs={{0,8},{4,12},{8,0},{12,4},{1,9},{5,13},{9,1},{13,5},{2,10},{6,14},... | collective-permute-start | bytes 1572872 | tf_op jit(solution)/shard_map/ppermute | solution.py:22
  31.7 21.3 %collective-permute-start.6 = (bf16[128,2048]{1,0:T(8,128)(2,1)S(1)}, bf16[128,2048]{1,0:T(8,128)(2,1)}, u32[]{:S(2)}, u32[]{:S(2)}) collective-permute-start(bf16[128,2048]{1,0:T(8,128)(2,1)S(1)} %pad_maximum_fusion.refs_0_), channel_id=1, source_target_pairs={{0,4},{4,0},{8,12},{12,8},{1,5},{5,1},{9,13},{13,9},{2,6},{6,2},{1... | collective-permute-start | bytes 1572872 | tf_op jit(solution)/shard_map/ppermute | solution.py:22
  39.1 13.9 %collective-permute-start.8 = (bf16[128,2048]{1,0:T(8,128)(2,1)S(1)}, bf16[128,2048]{1,0:T(8,128)(2,1)}, u32[]{:S(2)}, u32[]{:S(2)}) collective-permute-start(bf16[128,2048]{1,0:T(8,128)(2,1)S(1)} %pad_maximum_fusion.refs_0_), channel_id=1, source_target_pairs={{0,12},{4,8},{8,4},{12,0},{1,13},{5,9},{9,5},{13,1},{2,14},{6,10},... | collective-permute-start | bytes 1572872 | tf_op jit(solution)/shard_map/ppermute | solution.py:22
  53.0 8.5 %collective-permute-start.12 = (bf16[192,1024]{1,0:T(8,128)(2,1)S(1)}, bf16[192,1024]{1,0:T(8,128)(2,1)S(1)}, u32[]{:S(2)}, u32[]{:S(2)}) collective-permute-start(bf16[192,1024]{1,0:T(8,128)(2,1)S(1)} %pad_maximum_fusion.3), channel_id=1, source_target_pairs={{0,8},{4,12},{8,0},{12,4},{1,9},{5,13},{9,1},{13,5},{2,10},{6,14},... | collective-permute-start | bytes 1179656 | tf_op jit(solution)/shard_map/ppermute | solution.py:22
  75.7 138.5 %all-to-all-start = ((bf16[16,2,384,128]{3,2,1,0:T(8,128)(2,1)}), bf16[16,2,384,128]{3,2,1,0:T(8,128)(2,1)}, u32[]{:S(2)}, u32[]{:S(2)}) async-start(bf16[16,2,384,128]{3,2,1,0:T(8,128)(2,1)} %get-tuple-element.119), calls=%async_computation | async-start | bytes 6291456 | tf_op jit(solution)/shard_map/all_to_all | solution.py:458
  100.8 8.0 %collective-permute-start.17 = (bf16[64,2048]{1,0:T(8,128)(2,1)S(1)}, bf16[64,2048]{1,0:T(8,128)(2,1)S(1)}, u32[]{:S(2)}, u32[]{:S(2)}) collective-permute-start(bf16[64,2048]{1,0:T(8,128)(2,1)S(1)} %get-tuple-element.129), channel_id=1, source_target_pairs={{0,3},{1,2},{2,1},{3,0},{4,7},{5,6},{6,5},{7,4},{8,11},{9,10},{10,... | collective-permute-start | bytes 786440 | tf_op jit(solution)/shard_map/ppermute | solution.py:22
  102.4 11.3 %collective-permute-start.18 = (bf16[64,2048]{1,0:T(8,128)(2,1)S(1)}, bf16[64,2048]{1,0:T(8,128)(2,1)S(1)}, u32[]{:S(2)}, u32[]{:S(2)}) collective-permute-start(bf16[64,2048]{1,0:T(8,128)(2,1)S(1)} %get-tuple-element.128), channel_id=1, source_target_pairs={{0,2},{1,3},{2,0},{3,1},{4,6},{5,7},{6,4},{7,5},{8,10},{9,11},{10,... | collective-permute-start | bytes 786440 | tf_op jit(solution)/shard_map/ppermute | solution.py:22
  125.9 14.5 %collective-permute-start.24 = (bf16[128,2048]{1,0:T(8,128)(2,1)S(1)}, bf16[128,2048]{1,0:T(8,128)(2,1)S(1)}, u32[]{:S(2)}, u32[]{:S(2)}) collective-permute-start(bf16[128,2048]{1,0:T(8,128)(2,1)S(1)} %pad_maximum_fusion.2.refs_0_), channel_id=1, source_target_pairs={{0,4},{4,0},{8,12},{12,8},{1,5},{5,1},{9,13},{13,9},{2,6},{6,2},{1... | collective-permute-start | bytes 1572872 | tf_op jit(solution)/shard_map/ppermute | solution.py:22
  129.2 8.4 %collective-permute-start.25 = (bf16[64,2048]{1,0:T(8,128)(2,1)S(1)}, bf16[64,2048]{1,0:T(8,128)(2,1)S(1)}, u32[]{:S(2)}, u32[]{:S(2)}) collective-permute-start(bf16[64,2048]{1,0:T(8,128)(2,1)S(1)} %pad_maximum_fusion.4.refs_2_), channel_id=1, source_target_pairs={{0,3},{1,2},{2,1},{3,0},{4,7},{5,6},{6,5},{7,4},{8,11},{9,10},{10,... | collective-permute-start | bytes 786440 | tf_op jit(solution)/shard_map/ppermute | solution.py:22
  130.3 9.4 %collective-permute-start.26 = (bf16[64,2048]{1,0:T(8,128)(2,1)S(1)}, bf16[64,2048]{1,0:T(8,128)(2,1)S(1)}, u32[]{:S(2)}, u32[]{:S(2)}) collective-permute-start(bf16[64,2048]{1,0:T(8,128)(2,1)S(1)} %pad_maximum_fusion.4.refs_2_), channel_id=1, source_target_pairs={{0,2},{1,3},{2,0},{3,1},{4,6},{5,7},{6,4},{7,5},{8,10},{9,11},{10,... | collective-permute-start | bytes 786440 | tf_op jit(solution)/shard_map/ppermute | solution.py:22
  184.3 24.3 %collective-permute-start.28 = (bf16[128,2048]{1,0:T(8,128)(2,1)S(1)}, bf16[128,2048]{1,0:T(8,128)(2,1)S(1)}, u32[]{:S(2)}, u32[]{:S(2)}) collective-permute-start(bf16[128,2048]{1,0:T(8,128)(2,1)S(1)} %get-tuple-element.107), channel_id=1, source_target_pairs={{0,4},{4,0},{8,12},{12,8},{1,5},{5,1},{9,13},{13,9},{2,6},{6,2},{1... | collective-permute-start | bytes 1572872 | tf_op jit(solution)/shard_map/ppermute | solution.py:22
  188.0 12.5 %collective-permute-start.27 = (bf16[64,2048]{1,0:T(8,128)(2,1)}, bf16[64,2048]{1,0:T(8,128)(2,1)S(1)}, u32[]{:S(2)}, u32[]{:S(2)}) collective-permute-start(bf16[64,2048]{1,0:T(8,128)(2,1)} %get-tuple-element.106), channel_id=1, source_target_pairs={{0,1},{1,0},{2,3},{3,2},{4,5},{5,4},{6,7},{7,6},{8,9},{9,8},{10,11... | collective-permute-start | bytes 786440 | tf_op jit(solution)/shard_map/ppermute | solution.py:22
  194.3 12.4 %collective-permute-start.29 = (bf16[64,2048]{1,0:T(8,128)(2,1)}, bf16[64,2048]{1,0:T(8,128)(2,1)S(1)}, u32[]{:S(2)}, u32[]{:S(2)}) collective-permute-start(bf16[64,2048]{1,0:T(8,128)(2,1)} %get-tuple-element.108), channel_id=1, source_target_pairs={{0,3},{1,2},{2,1},{3,0},{4,7},{5,6},{6,5},{7,4},{8,11},{9,10},{10,... | collective-permute-start | bytes 786440 | tf_op jit(solution)/shard_map/ppermute | solution.py:22
  196.4 12.2 %collective-permute-start.30 = (bf16[64,2048]{1,0:T(8,128)(2,1)S(1)}, bf16[64,2048]{1,0:T(8,128)(2,1)S(1)}, u32[]{:S(2)}, u32[]{:S(2)}) collective-permute-start(bf16[64,2048]{1,0:T(8,128)(2,1)S(1)} %get-tuple-element.109), channel_id=1, source_target_pairs={{0,2},{1,3},{2,0},{3,1},{4,6},{5,7},{6,4},{7,5},{8,10},{9,11},{10,... | collective-permute-start | bytes 786440 | tf_op jit(solution)/shard_map/ppermute | solution.py:22
  208.8 8.5 %collective-permute-start.32 = (bf16[32,2048]{1,0:T(8,128)(2,1)S(1)}, bf16[32,2048]{1,0:T(8,128)(2,1)S(1)}, u32[]{:S(2)}, u32[]{:S(2)}) collective-permute-start(bf16[32,2048]{1,0:T(8,128)(2,1)S(1)} %slice.110), channel_id=1, source_target_pairs={{0,4},{4,0},{8,12},{12,8},{1,5},{5,1},{9,13},{13,9},{2,6},{6,2},{1... | collective-permute-start | bytes 393224 | tf_op jit(solution)/shard_map/ppermute | solution.py:22
  209.5 7.8 %collective-permute-start.31 = (bf16[32,2048]{1,0:T(8,128)(2,1)S(1)}, bf16[32,2048]{1,0:T(8,128)(2,1)S(1)}, u32[]{:S(2)}, u32[]{:S(2)}) collective-permute-start(bf16[32,2048]{1,0:T(8,128)(2,1)S(1)} %get-tuple-element.134), channel_id=1, source_target_pairs={{0,1},{1,0},{2,3},{3,2},{4,5},{5,4},{6,7},{7,6},{8,9},{9,8},{10,11... | collective-permute-start | bytes 393224 | tf_op jit(solution)/shard_map/ppermute | solution.py:22
  (37 other events, 211.9 us)
Sparse Core Ops, SparseCore 0:
  25.3 43.3 all-gather.3
  70.5 98.5 all-gather.5

commit v2 on v1

--- a/solution.py
+++ b/solution.py
@@ -31,13 +31,14 @@
     return lax.optimization_barrier(jnp.concatenate(pieces, axis=0))
 
 
-def gather_plane(one, two, half):
-    got = together([x for k in (1, 3, 2) for x in (("col", k, one), ("row", k, two))])
-    extra = jnp.stack([two[half:], got[1][half:], got[5][half:], got[3][half:]], axis=0)
+def gather_plane(one, two, also):
+    sent = [x for k in (1, 3, 2) for x in (("col", k, one), ("row", k, two))]
+    got = lax.optimization_barrier([swap(*x) for x in sent] + also)
+    also = got[6:]
     one = join([one, got[0], got[4], got[2]])
-    two = join([two[:half], got[1][:half], got[5][:half], got[3][:half]])
+    two = join([two, got[1], got[5], got[3]])
     got = together([x for k in (1, 3, 2) for x in (("row", k, one), ("col", k, two))])
-    return [one, got[0], got[4], got[2], two, got[1], got[5], got[3]], extra
+    return [one, got[0], got[4], got[2], two, got[1], got[5], got[3]], also
 
 
 def gather_block(one, two):
@@ -68,27 +69,23 @@
     )
 
 
-def norm_kernel(rows_ref, extra_ref, one_ref, two_ref):
+def norm_kernel(rows_ref, one_ref, two_ref):
     half = one_ref.shape[0]
     normed = layer_norm(rows_ref[...].astype(jnp.float32)).astype(jnp.bfloat16)
     one_ref[...] = normed[:half]
-    two_ref[:half] = normed[half:]
-    two_ref[half:] = extra_ref[...]
-
-
-def norm(rows, extra):
-    half, width = rows.shape[0] // 2, rows.shape[1]
+    two_ref[...] = normed[half:]
+
+
+def norm(rows):
+    part = jax.ShapeDtypeStruct((rows.shape[0] // 2, rows.shape[1]), jnp.bfloat16)
     return pl.pallas_call(
         norm_kernel,
-        out_shape=(
-            jax.ShapeDtypeStruct((half, width), jnp.bfloat16),
-            jax.ShapeDtypeStruct((half + extra.shape[0], width), jnp.bfloat16),
-        ),
+        out_shape=(part, part),
         cost_estimate=pl.CostEstimate(
             flops=8 * rows.size, transcendentals=0, bytes_accessed=4 * rows.size
         ),
         name="norm",
-    )(rows, extra)
+    )(rows)
 
 
 def mid_kernel(rows_ref, own_ref, a_ref, b_ref, c_ref, middle_ref, one_ref, two_ref):
@@ -115,42 +112,83 @@
 
 
 def joined_kernel(*refs):
-    pieces, (heads_ref, out_ref, rows_ref, sems) = refs[:8], refs[8:]
+    pieces, (heads_ref, out_ref, rows_ref) = refs[:8], refs[8:]
     tall = pieces[0].shape[0]
+    for n in range(0, len(pieces), 4):
+        for m in range(4):
+            rows_ref[pl.ds(tall * m, tall), :] = pieces[n + m][...]
+        out_ref[pl.ds(tall * n, 4 * tall), :] = jnp.dot(
+            rows_ref[...], heads_ref[...], preferred_element_type=jnp.float32
+        )
+
+
+def join_heads(pieces, heads):
+    tall, width = pieces[0].shape
+    shape = (len(pieces) * tall, heads.shape[1])
+    in_vmem = pl.BlockSpec(memory_space=pltpu.VMEM)
+    return pl.pallas_call(
+        joined_kernel,
+        out_shape=jax.ShapeDtypeStruct(shape, jnp.float32),
+        in_specs=[in_vmem] * (len(pieces) + 1),
+        out_specs=in_vmem,
+        scratch_shapes=[pltpu.VMEM((4 * tall, width), jnp.bfloat16)],
+        compiler_params=pltpu.CompilerParams(vmem_limit_bytes=24 << 20),
+        cost_estimate=pl.CostEstimate(
+            flops=2 * shape[0] * width * shape[1], transcendentals=0, bytes_accessed=7 << 20
+        ),
+        name="join_heads",
+    )(*pieces, heads)
+
+
+def project_kernel(*refs):
+    parts, fed_ref, outs = refs[:4], refs[4], refs[5:9]
+    heads_ref, weight_ref, sems = refs[9:]
+    shares = fed_ref.shape[0]
+    tall = weight_ref.shape[0] // shares
     copies = [
-        pltpu.make_async_copy(piece, rows_ref.at[pl.ds(tall * n, tall)], sems.at[n])
-        for n, piece in enumerate(pieces)
+        pltpu.make_async_copy(
+            fed_ref.at[r, pl.ds(0, tall)], weight_ref.at[pl.ds(tall * r, tall)], sems.at[r]
+        )
+        for r in range(shares)
     ]
     for copy in copies:
         copy.start()
-    for n in range(4):
-        copies[2 * n].wait()
-        copies[2 * n + 1].wait()
-        span = pl.ds(2 * tall * n, 2 * tall)
-        out_ref[span, :] = jnp.dot(
-            rows_ref[span, :], heads_ref[...], preferred_element_type=jnp.float32
-        )
-
-
-def join_heads(pieces, heads):
-    tall, width = pieces[0].shape
-    shape = (len(pieces) * tall, heads.shape[1])
-    return pl.pallas_call(
-        joined_kernel,
-        out_shape=jax.ShapeDtypeStruct(shape, jnp.float32),
-        in_specs=[pl.BlockSpec(memory_space=pl.ANY)] * len(pieces)
-        + [pl.BlockSpec(memory_space=pltpu.VMEM)],
-        out_specs=pl.BlockSpec(memory_space=pltpu.VMEM),
+    size = parts[0].shape[1]
+    for n, part in enumerate(parts):
+        heads_ref[:, size * n : size * (n + 1)] = part[...]
+    for copy in copies:
+        copy.wait()
+    step = 512
+
+    @pl.loop(0, weight_ref.shape[1] // step)
+    def _(j):
+        span = pl.ds(pl.multiple_of(step * j, step), step)
+        total = jnp.dot(
+            heads_ref[...], weight_ref[:, span], preferred_element_type=jnp.float32
+        ).astype(jnp.bfloat16)
+        for n, out in enumerate(outs):
+            out[:, span] = total[out.shape[0] * n : out.shape[0] * (n + 1)]
+
+
+def project(parts, fed, local_rows):
+    rows, size = parts[0].shape
+    width = fed.shape[2]
+    in_vmem = pl.BlockSpec(memory_space=pltpu.VMEM)
+    return pl.pallas_call(
+        project_kernel,
+        out_shape=[jax.ShapeDtypeStruct((local_rows, width), jnp.bfloat16)] * 4,
+        in_specs=[in_vmem] * 4 + [pl.BlockSpec(memory_space=pl.ANY)],
+        out_specs=[in_vmem] * 4,
         scratch_shapes=[
-            pltpu.VMEM((shape[0], width), jnp.bfloat16),
-            pltpu.SemaphoreType.DMA((len(pieces),)),
+            pltpu.VMEM((rows, 4 * size), jnp.bfloat16),
+            pltpu.VMEM((4 * size, width), jnp.bfloat16),
+            pltpu.SemaphoreType.DMA((fed.shape[0],)),
         ],
-        compiler_params=pltpu.CompilerParams(vmem_limit_bytes=24 << 20),
-        cost_estimate=pl.CostEstimate(
-            flops=2 * shape[0] * width * shape[1], transcendentals=0, bytes_accessed=7 << 20
-        ),
-        name="join_heads",
-    )(*pieces, heads)
+        cost_estimate=pl.CostEstimate(
+            flops=8 * rows * size * width, transcendentals=0, bytes_accessed=4 << 20
+        ),
+        name="project",
+    )(*parts, fed)
 
 
 def feed_kernel(*refs):
@@ -159,37 +197,38 @@
     units, width = w_down_ref.shape
     shares, tall, _ = fed_ref.shape
     part_in, part_down = width // shares, units // shares
-    jobs, at = [], 0
-    for piece in pieces:
-        jobs.append((piece, rows_ref.at[pl.ds(at, piece.shape[0])]))
-        at += piece.shape[0]
-    jobs.append((w_in_ref, in_ref.at[0]))
-    jobs.append((w_down_ref, down_ref.at[0]))
+    first = tall - part_in // 2 - part_down
     half = width // 2
+    jobs = [(w_in_ref, in_ref.at[0]), (w_down_ref, down_ref.at[0])]
     for r in range(shares):
-        jobs.append(
-            (fed_ref.at[r, pl.ds(0, part_in)], in_ref.at[1, pl.ds(part_in * r, part_in)])
-        )
         for n in range(2):
             jobs.append(
                 (
-                    fed_ref.at[r, pl.ds(part_in + part_down * n, part_down)],
-                    down_ref.at[1, pl.ds(part_down * r, part_down), pl.ds(half * n, half)],
+                    fed_ref.at[r, pl.ds(first, part_in // 2), pl.ds(half * n, half)],
+                    in_ref.at[1, pl.ds(part_in * r + part_in // 2 * n, part_in // 2)],
                 )
             )
+        jobs.append(
+            (
+                fed_ref.at[r, pl.ds(tall - part_down, part_down)],
+                down_ref.at[1, pl.ds(part_down * r, part_down)],
+            )
+        )
     copies = [
         pltpu.make_async_copy(source, target, sems.at[n])
         for n, (source, target) in enumerate(jobs)
     ]
     for copy in copies:
         copy.start()
-    for n, copy in enumerate(copies):
-        if n < 7:
-            copy.wait()
+    at = 0
+    for piece in pieces:
+        rows_ref[pl.ds(at, piece.shape[0]), :] = piece[...]
+        at += piece.shape[0]
+    copies[0].wait()
     step = 256
     for shard in range(2):
         if shard == 1:
-            for copy in copies[7:]:
+            for copy in copies[1:]:
                 copy.wait()
 
         @pl.loop(0, units // step)
@@ -227,14 +266,15 @@
     return pl.pallas_call(
         feed_kernel,
         out_shape=[jax.ShapeDtypeStruct(piece.shape, jnp.bfloat16) for piece in pieces],
-        in_specs=[pl.BlockSpec(memory_space=pl.ANY)] * (len(pieces) + 3),
+        in_specs=[pl.BlockSpec(memory_space=pltpu.VMEM)] * len(pieces)
+        + [pl.BlockSpec(memory_space=pl.ANY)] * 3,
         out_specs=[pl.BlockSpec(memory_space=pltpu.VMEM)] * len(pieces),
         scratch_shapes=[
             pltpu.VMEM((rows, width), jnp.bfloat16),
             pltpu.VMEM((2, width, 2 * units), jnp.bfloat16),
             pltpu.VMEM((2, units, width), jnp.bfloat16),
             pltpu.VMEM((2, rows, units), jnp.bfloat16),
-            pltpu.SemaphoreType.DMA((len(pieces) + 2 + 3 * fed.shape[0],)),
+            pltpu.SemaphoreType.DMA((2 + 3 * fed.shape[0],)),
         ],
         compiler_params=pltpu.CompilerParams(vmem_limit_bytes=48 << 20),
         cost_estimate=pl.CostEstimate(
@@ -338,7 +378,7 @@
             num_scalar_prefetch=4,
             grid=(slots,),
             in_specs=[
-                pl.BlockSpec(joined.shape, whole),
+                pl.BlockSpec(memory_space=pltpu.VMEM),
                 pl.BlockSpec(
                     (1, kinds, stored, size),
                     lambda g, place, *refs: (request_of(g, place[0]), 0, 0, 0),
@@ -414,25 +454,34 @@
     requests = jnp.arange(new_slot.shape[0], dtype=jnp.int32)
     source = jnp.sum(arrivals * (requests // slots)[None, :], axis=1)
 
-    share = size // replicas
-    out_slice = lax.dynamic_slice_in_dim(w_out.reshape(size, width), replica * share, share)
+    one, two = norm(hidden_in)
+    one, two, w_gate_up = lax.optimization_barrier((one, two, w_gate_up))
+
+    out_rows = 4 * size // replicas
+    out_slice = lax.dynamic_slice_in_dim(
+        w_out.reshape(size, width), out_rows * (replica % (size // out_rows)), out_rows
+    )
+    per_head = size // out_rows
+    pairs = [
+        (4 * r + i, 4 * r + (i ^ (r // per_head))) for r in range(replicas) for i in range(4)
+    ]
+    out_far = lax.ppermute(out_slice, ("rep", "row"), pairs)
     rows_in, rows_down = width // replicas, units // replicas
     in_slice = lax.dynamic_slice_in_dim(w_gate_up, replica * rows_in, rows_in)
+    in_slice = in_slice.reshape(2, rows_in // 2, 2 * units)
     down_slice = lax.dynamic_slice_in_dim(w_down, replica * rows_down, rows_down)
     feed_slice = jnp.concatenate(
-        [in_slice.reshape(rows_in, 2 * units), down_slice[:, : 2 * units], down_slice[:, 2 * units :]],
-        axis=0,
-    )
-
-    one, two = norm(hidden_in, out_slice)
-    pieces, out_slices = gather_plane(one, two, local_rows // 2)
-    w_rows = lax.all_gather(out_slices, "rep", axis=1, tiled=True).reshape(4 * size, width)
+        [jnp.concatenate([in_slice[0], in_slice[1]], axis=1), down_slice], axis=0
+    )
+    feed_far = swap("row", 2, feed_slice)
+
+    pieces, (out_far, feed_far) = gather_plane(one, two, [out_far, feed_far])
+    fed = lax.all_gather(
+        jnp.concatenate([out_far, feed_far], axis=0), "rep", axis=0, tiled=False
+    )
     w_in = w_gate_up.reshape(width, 2 * units)
-    pieces, w_in, feed_slice = lax.optimization_barrier((pieces, w_in, feed_slice))
-    feed_far = swap("row", 2, feed_slice)
+    pieces, w_in = lax.optimization_barrier((pieces, w_in))
     joined = join_heads(pieces, w_qkv.reshape(width, 3 * size))
-    joined, feed_far = lax.optimization_barrier((joined, feed_far))
-    fed = lax.all_gather(feed_far, "rep", axis=0, tiled=False)
 
     frequency = 10000.0 ** (-(np.arange(size // 2) * 2.0 / size))
     frequency = np.concatenate([frequency, frequency])[None, :]
@@ -450,9 +499,8 @@
 
     context = context.reshape(4, 4 * local_rows, size)
     got = together([("row", k, context[k]) for k in (1, 3, 2)])
-    parts = jnp.concatenate([context[0], got[0], got[2], got[1]], axis=1)
-    partial = jnp.dot(parts, w_rows, preferred_element_type=jnp.float32).astype(jnp.bfloat16)
-    partial = partial.reshape(4, local_rows, width)
+    partial = project([context[0], got[0], got[2], got[1]], fed, local_rows)
+    partial, sent = lax.optimization_barrier((partial, sent))
     got = together([("col", k, partial[k]) for k in (1, 3, 2)])
     middle, one, two = mid(hidden_in, partial[0], [got[0], got[2], got[1]])
     moved = lax.all_to_all(sent, "rep", split_axis=0, concat_axis=0, tiled=True)

time: 228 us -> 204 us (0.89)
  starting transfers between devices: 64 us -> 49.9 us
  local copies, waits for them, and re-layouts: 23.2 us -> 14.9 us
  Pallas kernels: 33.3 us -> 37 us
  matrix products: 2.31 us -> 0 us
    all_gather x2 -> x1, waiting for transfers between devices: 28.7 us -> 10.3 us  [body(): lax.all_gather(jnp.concatenate([out_far, feed_far], axis=0), 'rep', axis=...]
    ppermute x35, waiting for transfers between devices: 51.5 us -> 67.7 us  [swap(): return lax.ppermute(array, axis, [(i, i ^ k) for i in range(size)])]
    ppermute x35, starting transfers between devices: 49.6 us -> 42.1 us  [swap(): return lax.ppermute(array, axis, [(i, i ^ k) for i in range(size)])]
    all_to_all x1, starting transfers between devices: 14.4 us -> 7.04 us  [body(): moved = lax.all_to_all(sent, 'rep', split_axis=0, concat_axis=0, tiled=True)]
    unnamed x48 -> x47, local copies, waits for them, and re-layouts: 16 us -> 10 us
    pallas_call x1 -> x2, Pallas kernels: 1.89 us -> 6.73 us  [the longest x1 4.8 us: project(): pl.pallas_call(project_kernel, out_shape=[jax.ShapeDtypeStruct((local_row...]
    dot_general x1 -> x0, matrix products: 2.31 us -> none  [body(): jnp.dot(parts, w_rows, preferred_element_type=jnp.float32)]
  transfers between devices with their start and end apart: 38 -> 38, of which waited for: 23 -> 23; matrix products, arithmetic and copies ran while one was open for 9% -> 8% of each run, Pallas kernels for 14% -> 13%
where the time goes in v2:
time: 204 us; the launch traced here: 202 us
  waiting for transfers between devices  78.1 us (38%)
  starting transfers between devices  49.9 us (24%)
  Pallas kernels  37 us (18%)
  local copies, waits for them, and re-layouts  14.9 us (7%)
  between operations  14.3 us (7%)
  other arithmetic  8.3 us (4%)
    ppermute x35, waiting for transfers between devices, swap(): return lax.ppermute(array, axis, [(i, i ^ k) for i in range(size)])  67.7 us
    ppermute x35, starting transfers between devices, swap(): return lax.ppermute(array, axis, [(i, i ^ k) for i in range(size)])  42.1 us
    pallas_call x1, Pallas kernels, feed(): pl.pallas_call(feed_kernel, out_shape=[jax.ShapeDtypeStruct(piece.shape,...  11.5 us
    all_gather x1, waiting for transfers between devices, body(): lax.all_gather(jnp.concatenate([out_far, feed_far], axis=0), 'rep', axis=...  10.3 us
    unnamed x47, local copies, waits for them, and re-layouts  10 us
    pallas_call x1, Pallas kernels, attend(): pl.pallas_call(attend_kernel, out_shape=(jax.ShapeDtypeStruct((slots * sp...  9.43 us
    all_to_all x1, starting transfers between devices, body(): moved = lax.all_to_all(sent, 'rep', split_axis=0, concat_axis=0, tiled=True)  7.04 us
    pallas_call x1, Pallas kernels, project(): pl.pallas_call(project_kernel, out_shape=[jax.ShapeDtypeStruct((local_row...  4.8 us
  transfers between devices with their start and end apart: 38, of which 23 were waited for; matrix products, arithmetic and copies ran while one was open for 8% of the time, Pallas kernels for 13%

profile of v2, /device:TPU:1, one launch (start us, length us, event | category | flops | bytes accessed | tf_op | source)
XLA Modules:
  0.0 202.5 jit_solution(4983568373000794437)
XLA Ops:
  11.4 3.8 %collective-permute-start.7 = (bf16[96,2048]{1,0:T(8,128)(2,1)S(1)}, bf16[96,2048]{1,0:T(8,128)(2,1)S(1)}, u32[]{:S(2)}, u32[]{:S(2)}) collective-permute-start(bf16[96,2048]{1,0:T(8,128)(2,1)S(1)} %pad_maximum_fusion.4), channel_id=1, source_target_pairs={{0,8},{4,12},{8,0},{12,4},{1,9},{5,13},{9,1},{13,5},{2,10},{6,14},... | collective-permute-start | bytes 1179656 | tf_op jit(solution)/shard_map/ppermute | solution.py:22
  15.9 2.8 %collective-permute-start.4 = (bf16[32,2048]{1,0:T(8,128)(2,1)}, bf16[32,2048]{1,0:T(8,128)(2,1)S(1)}, u32[]{:S(2)}, u32[]{:S(2)}) collective-permute-start(bf16[32,2048]{1,0:T(8,128)(2,1)} %get-tuple-element.74), channel_id=1, source_target_pairs={{0,2},{1,3},{2,0},{3,1},{4,6},{5,7},{6,4},{7,5},{8,10},{9,11},{10,... | collective-permute-start | bytes 393224 | tf_op jit(solution)/shard_map/ppermute | solution.py:22
  26.5 3.4 %collective-permute-done.3 = bf16[32,2048]{1,0:T(8,128)(2,1)S(1)} collective-permute-done((bf16[32,2048]{1,0:T(8,128)(2,1)}, bf16[32,2048]{1,0:T(8,128)(2,1)S(1)}, u32[]{:S(2)}, u32[]{:S(2)}) %collective-permute-start.3) | collective-permute-done | bytes 131104 | tf_op jit(solution)/shard_map/ppermute | solution.py:22
  35.3 2.9 %collective-permute-start.12 = (bf16[128,2048]{1,0:T(8,128)(2,1)S(1)}, bf16[128,2048]{1,0:T(8,128)(2,1)}, u32[]{:S(2)}, u32[]{:S(2)}) collective-permute-start(bf16[128,2048]{1,0:T(8,128)(2,1)S(1)} %pad_maximum_fusion.refs_0_), channel_id=1, source_target_pairs={{0,8},{4,12},{8,0},{12,4},{1,9},{5,13},{9,1},{13,5},{2,10},{6,14},... | collective-permute-start | bytes 1572872 | tf_op jit(solution)/shard_map/ppermute | solution.py:22
  38.9 5.3 %collective-permute-done.13.refs_6_ = bf16[128,2048]{1,0:T(8,128)(2,1)S(1)} collective-permute-done((bf16[128,2048]{1,0:T(8,128)(2,1)S(1)}, bf16[128,2048]{1,0:T(8,128)(2,1)S(1)}, u32[]{:S(2)}, u32[]{:S(2)}) %collective-permute-start.13) | collective-permute-done | bytes 524320 | tf_op jit(solution)/shard_map/ppermute | solution.py:22
  45.0 2.9 %collective-permute-start.8 = (bf16[128,2048]{1,0:T(8,128)(2,1)S(1)}, bf16[128,2048]{1,0:T(8,128)(2,1)}, u32[]{:S(2)}, u32[]{:S(2)}) collective-permute-start(bf16[128,2048]{1,0:T(8,128)(2,1)S(1)} %pad_maximum_fusion.refs_0_), channel_id=1, source_target_pairs={{0,4},{4,0},{8,12},{12,8},{1,5},{5,1},{9,13},{13,9},{2,6},{6,2},{1... | collective-permute-start | bytes 1572872 | tf_op jit(solution)/shard_map/ppermute | solution.py:22
  48.0 5.6 %copy.19 = bf16[256,8,2,512]{3,1,2,0:T(8,128)(2,1)} copy(bf16[256,8,2,512]{3,2,1,0:T(2,128)(2,1)} %bitcast.20) | data formatting | bytes 8388608
  57.6 4.5 %collective-permute-done.10.refs_3_ = bf16[128,2048]{1,0:T(8,128)(2,1)} collective-permute-done((bf16[128,2048]{1,0:T(8,128)(2,1)S(1)}, bf16[128,2048]{1,0:T(8,128)(2,1)}, u32[]{:S(2)}, u32[]{:S(2)}) %collective-permute-start.10) | collective-permute-done | bytes 524320 | tf_op jit(solution)/shard_map/ppermute | solution.py:22
  63.1 4.0 %join_heads.1.joined_ref = f32[1024,384]{1,0:T(8,128)S(1)} custom-call(bf16[128,2048]{1,0:T(8,128)(2,1)S(1)} %pad_maximum_fusion.refs_0_, bf16[128,2048]{1,0:T(8,128)(2,1)} %collective-permute-done.8.refs_1_, bf16[128,2048]{1,0:T(8,128)(2,1)} %collective-permute-done.12.refs_2_, bf16[128,2048]{1,0:T(8,128)(2,1)} %collective-permute-done.10.refs_3_, ...), custom_call_target="tpu_custom_call" | custom-call | flops 1610612736 | bytes 7340032 | tf_op jit(solution)/shard_map/join_heads/pallas_call | solution.py:129
  68.3 9.4 %attend.1 = (bf16[1024,128]{1,0:T(8,128)(2,1)}, bf16[16,2,384,128]{3,2,1,0:T(8,128)(2,1)}) custom-call(s32[2]{0:T(128)} %pad_add_fusion.place_ref, s32[8]{0:T(128)} %get-tuple-element.147.length_ref, s32[8]{0:T(128)} %dynamic_slice.29.span_ref, s32[8]{0:T(128)} %get-tuple-element.159.target_ref, f32[1024,384]{1,0:T(8,128)} %copy-done.1, ...), custom_call_target="tpu_custom_call" | custom-call | flops 201326592 | bytes 6291456 | tf_op jit(solution)/shard_map/attend/pallas_call | solution.py:371
  80.4 2.4 %collective-permute-start.15 = (bf16[256,128]{1,0:T(8,128)(2,1)S(1)}, bf16[256,128]{1,0:T(8,128)(2,1)S(1)}, u32[]{:S(2)}, u32[]{:S(2)}) collective-permute-start(bf16[256,128]{1,0:T(8,128)(2,1)S(1)} %get-tuple-element.154), channel_id=1, source_target_pairs={{0,12},{4,8},{8,4},{12,0},{1,13},{5,9},{9,5},{13,1},{2,14},{6,10},... | collective-permute-start | bytes 196616 | tf_op jit(solution)/shard_map/ppermute | solution.py:22
  86.3 10.3 %all-gather.3.cloned.1.call-done = bf16[2048,2048]{1,0:T(8,128)(2,1)} async-done(((bf16[128,2048]{1,0:T(8,128)(2,1)}), bf16[2048,2048]{1,0:T(8,128)(2,1)}) %all-gather.3.cloned.1.call-update) | async-done | bytes 8388624 | tf_op jit(solution)/shard_map/all_gather | solution.py:479
  96.7 4.8 %project.1 = (bf16[64,2048]{1,0:T(8,128)(2,1)}, bf16[64,2048]{1,0:T(8,128)(2,1)}, bf16[64,2048]{1,0:T(8,128)(2,1)}, bf16[64,2048]{1,0:T(8,128)(2,1)}) custom-call(bf16[256,128]{1,0:T(8,128)(2,1)} %get-tuple-element.156.refs_0_, bf16[256,128]{1,0:T(8,128)(2,1)} %copy-done.13, bf16[256,128]{1,0:T(8,128)(2,1)} %copy-done.11, bf16[256,128]{1,0:T(8,128)(2,1)} %copy-done.12, ...), custom_call_target="tpu_custom_call" | custom-call | flops 536870912 | bytes 4194304 | tf_op jit(solution)/shard_map/project/pallas_call | solution.py:177
  101.5 7.0 %all-to-all-start = ((bf16[16,2,384,128]{3,2,1,0:T(8,128)(2,1)}), bf16[16,2,384,128]{3,2,1,0:T(8,128)(2,1)}, u32[]{:S(2)}, u32[]{:S(2)}) async-start(bf16[16,2,384,128]{3,2,1,0:T(8,128)(2,1)} %get-tuple-element.141), calls=%async_computation | async-start | bytes 6291456 | tf_op jit(solution)/shard_map/all_to_all | solution.py:506
  111.9 4.6 %collective-permute-done.17.a_ref = bf16[64,2048]{1,0:T(8,128)(2,1)S(1)} collective-permute-done((bf16[64,2048]{1,0:T(8,128)(2,1)S(1)}, bf16[64,2048]{1,0:T(8,128)(2,1)S(1)}, u32[]{:S(2)}, u32[]{:S(2)}) %collective-permute-start.17) | collective-permute-done | bytes 262176 | tf_op jit(solution)/shard_map/ppermute | solution.py:22
  116.5 7.9 %collective-permute-done.18.c_ref = bf16[64,2048]{1,0:T(8,128)(2,1)S(1)} collective-permute-done((bf16[64,2048]{1,0:T(8,128)(2,1)S(1)}, bf16[64,2048]{1,0:T(8,128)(2,1)S(1)}, u32[]{:S(2)}, u32[]{:S(2)}) %collective-permute-start.18) | collective-permute-done | bytes 262176 | tf_op jit(solution)/shard_map/ppermute | solution.py:22
  125.8 2.4 %mid.1 = (bf16[64,2048]{1,0:T(8,128)(2,1)}, bf16[32,2048]{1,0:T(8,128)(2,1)}, bf16[32,2048]{1,0:T(8,128)(2,1)}) custom-call(bf16[64,2048]{1,0:T(8,128)(2,1)} %rows_ref.3, bf16[64,2048]{1,0:T(8,128)(2,1)} %get-tuple-element.108.own_ref, bf16[64,2048]{1,0:T(8,128)(2,1)} %copy-done.5, bf16[64,2048]{1,0:T(8,128)(2,1)} %copy-done.7, bf16[64,2048]{1,0:T(8,128)(2,1)} %copy-done.6), custom_call_target="tpu_custom_call" | custom-call | flops 1572864 | bytes 1835008 | tf_op jit(solution)/shard_map/mid/pallas_call | solution.py:104
  134.2 3.1 %collective-permute-done.22 = bf16[32,2048]{1,0:T(8,128)(2,1)S(1)} collective-permute-done((bf16[32,2048]{1,0:T(8,128)(2,1)}, bf16[32,2048]{1,0:T(8,128)(2,1)S(1)}, u32[]{:S(2)}, u32[]{:S(2)}) %collective-permute-start.22) | collective-permute-done | bytes 131104 | tf_op jit(solution)/shard_map/ppermute | solution.py:22
  143.4 3.7 %collective-permute-done.27.refs_4_ = bf16[64,2048]{1,0:T(8,128)(2,1)S(1)} collective-permute-done((bf16[64,2048]{1,0:T(8,128)(2,1)S(1)}, bf16[64,2048]{1,0:T(8,128)(2,1)S(1)}, u32[]{:S(2)}, u32[]{:S(2)}) %collective-permute-start.27) | collective-permute-done | bytes 262176 | tf_op jit(solution)/shard_map/ppermute | solution.py:22
  147.0 7.7 %collective-permute-done.26.refs_5_ = bf16[64,2048]{1,0:T(8,128)(2,1)S(1)} collective-permute-done((bf16[64,2048]{1,0:T(8,128)(2,1)S(1)}, bf16[64,2048]{1,0:T(8,128)(2,1)S(1)}, u32[]{:S(2)}, u32[]{:S(2)}) %collective-permute-start.26) | collective-permute-done | bytes 262176 | tf_op jit(solution)/shard_map/ppermute | solution.py:22
  154.7 11.5 %feed.1 = (bf16[128,2048]{1,0:T(8,128)(2,1)S(1)}, bf16[128,2048]{1,0:T(8,128)(2,1)S(1)}, bf16[64,2048]{1,0:T(8,128)(2,1)S(1)}, bf16[64,2048]{1,0:T(8,128)(2,1)S(...) custom-call(bf16[128,2048]{1,0:T(8,128)(2,1)S(1)} %pad_maximum_fusion.3.refs_0_, ...), custom_call_target="tpu_custom_call" | custom-call | flops 6442450944 | bytes 16777216 | tf_op jit(solution)/shard_map/feed/pallas_call | solution.py:266
  171.6 2.7 %collective-permute-done.28 = bf16[64,2048]{1,0:T(8,128)(2,1)S(1)} collective-permute-done((bf16[64,2048]{1,0:T(8,128)(2,1)S(1)}, bf16[64,2048]{1,0:T(8,128)(2,1)S(1)}, u32[]{:S(2)}, u32[]{:S(2)}) %collective-permute-start.28) | collective-permute-done | bytes 262176 | tf_op jit(solution)/shard_map/ppermute | solution.py:22
  176.0 6.2 %collective-permute-done.31 = bf16[64,2048]{1,0:T(8,128)(2,1)} collective-permute-done((bf16[64,2048]{1,0:T(8,128)(2,1)S(1)}, bf16[64,2048]{1,0:T(8,128)(2,1)}, u32[]{:S(2)}, u32[]{:S(2)}) %collective-permute-start.31) | collective-permute-done | bytes 262176 | tf_op jit(solution)/shard_map/ppermute | solution.py:22
  192.7 3.0 %pick.1 = bf16[8,2,384,128]{3,2,1,0:T(8,128)(2,1)} custom-call(s32[8]{0:T(128)} %select_reduce_fusion.source_ref, bf16[16,2,384,128]{3,2,1,0:T(8,128)(2,1)} %all-to-all-done.moved_ref), custom_call_target="tpu_custom_call" | custom-call | bytes 3145728 | tf_op jit(solution)/shard_map/pick/pallas_call | solution.py:427
  (133 shorter events, 66.2 us)
Async XLA Ops:
  7.2 89.5 %all-gather.3.cloned.1.call-start = ((), (), s32[]{:S(2)}) async-start(), calls=%async_computation.1 | async-start | bytes 8912896 | tf_op jit(solution)/shard_map/all_gather | solution.py:479
  11.4 18.5 %collective-permute-start.7 = (bf16[96,2048]{1,0:T(8,128)(2,1)S(1)}, bf16[96,2048]{1,0:T(8,128)(2,1)S(1)}, u32[]{:S(2)}, u32[]{:S(2)}) collective-permute-start(bf16[96,2048]{1,0:T(8,128)(2,1)S(1)} %pad_maximum_fusion.4), channel_id=1, source_target_pairs={{0,8},{4,12},{8,0},{12,4},{1,9},{5,13},{9,1},{13,5},{2,10},{6,14},... | collective-permute-start | bytes 1179656 | tf_op jit(solution)/shard_map/ppermute | solution.py:22
  19.6 6.9 %collective-permute-start.5 = (bf16[32,2048]{1,0:T(8,128)(2,1)}, bf16[32,2048]{1,0:T(8,128)(2,1)S(1)}, u32[]{:S(2)}, u32[]{:S(2)}) collective-permute-start(bf16[32,2048]{1,0:T(8,128)(2,1)} %get-tuple-element.75), channel_id=1, source_target_pairs={{0,8},{4,12},{8,0},{12,4},{1,9},{5,13},{9,1},{13,5},{2,10},{6,14},... | collective-permute-start | bytes 393224 | tf_op jit(solution)/shard_map/ppermute | solution.py:22
  21.8 8.1 %collective-permute-start.3 = (bf16[32,2048]{1,0:T(8,128)(2,1)}, bf16[32,2048]{1,0:T(8,128)(2,1)S(1)}, u32[]{:S(2)}, u32[]{:S(2)}) collective-permute-start(bf16[32,2048]{1,0:T(8,128)(2,1)} %get-tuple-element.75), channel_id=1, source_target_pairs={{0,12},{4,8},{8,4},{12,0},{1,13},{5,9},{9,5},{13,1},{2,14},{6,10},... | collective-permute-start | bytes 393224 | tf_op jit(solution)/shard_map/ppermute | solution.py:22
  30.8 13.4 %collective-permute-start.13 = (bf16[128,2048]{1,0:T(8,128)(2,1)S(1)}, bf16[128,2048]{1,0:T(8,128)(2,1)S(1)}, u32[]{:S(2)}, u32[]{:S(2)}) collective-permute-start(bf16[128,2048]{1,0:T(8,128)(2,1)S(1)} %pad_maximum_fusion.1.refs_4_), channel_id=1, source_target_pairs={{0,2},{1,3},{2,0},{3,1},{4,6},{5,7},{6,4},{7,5},{8,10},{9,11},{10,... | collective-permute-start | bytes 1572872 | tf_op jit(solution)/shard_map/ppermute | solution.py:22
  33.0 24.6 %collective-permute-start.11 = (bf16[128,2048]{1,0:T(8,128)(2,1)S(1)}, bf16[128,2048]{1,0:T(8,128)(2,1)}, u32[]{:S(2)}, u32[]{:S(2)}) collective-permute-start(bf16[128,2048]{1,0:T(8,128)(2,1)S(1)} %pad_maximum_fusion.1.refs_4_), channel_id=1, source_target_pairs={{0,3},{1,2},{2,1},{3,0},{4,7},{5,6},{6,5},{7,4},{8,11},{9,10},{10,... | collective-permute-start | bytes 1572872 | tf_op jit(solution)/shard_map/ppermute | solution.py:22
  35.2 22.4 %collective-permute-start.9 = (bf16[128,2048]{1,0:T(8,128)(2,1)S(1)}, bf16[128,2048]{1,0:T(8,128)(2,1)}, u32[]{:S(2)}, u32[]{:S(2)}) collective-permute-start(bf16[128,2048]{1,0:T(8,128)(2,1)S(1)} %pad_maximum_fusion.1.refs_4_), channel_id=1, source_target_pairs={{0,1},{1,0},{2,3},{3,2},{4,5},{5,4},{6,7},{7,6},{8,9},{9,8},{10,11... | collective-permute-start | bytes 1572872 | tf_op jit(solution)/shard_map/ppermute | solution.py:22
  35.3 22.3 %collective-permute-start.12 = (bf16[128,2048]{1,0:T(8,128)(2,1)S(1)}, bf16[128,2048]{1,0:T(8,128)(2,1)}, u32[]{:S(2)}, u32[]{:S(2)}) collective-permute-start(bf16[128,2048]{1,0:T(8,128)(2,1)S(1)} %pad_maximum_fusion.refs_0_), channel_id=1, source_target_pairs={{0,8},{4,12},{8,0},{12,4},{1,9},{5,13},{9,1},{13,5},{2,10},{6,14},... | collective-permute-start | bytes 1572872 | tf_op jit(solution)/shard_map/ppermute | solution.py:22
  38.1 23.9 %collective-permute-start.10 = (bf16[128,2048]{1,0:T(8,128)(2,1)S(1)}, bf16[128,2048]{1,0:T(8,128)(2,1)}, u32[]{:S(2)}, u32[]{:S(2)}) collective-permute-start(bf16[128,2048]{1,0:T(8,128)(2,1)S(1)} %pad_maximum_fusion.refs_0_), channel_id=1, source_target_pairs={{0,12},{4,8},{8,4},{12,0},{1,13},{5,9},{9,5},{13,1},{2,14},{6,10},... | collective-permute-start | bytes 1572872 | tf_op jit(solution)/shard_map/ppermute | solution.py:22
  45.0 17.0 %collective-permute-start.8 = (bf16[128,2048]{1,0:T(8,128)(2,1)S(1)}, bf16[128,2048]{1,0:T(8,128)(2,1)}, u32[]{:S(2)}, u32[]{:S(2)}) collective-permute-start(bf16[128,2048]{1,0:T(8,128)(2,1)S(1)} %pad_maximum_fusion.refs_0_), channel_id=1, source_target_pairs={{0,4},{4,0},{8,12},{12,8},{1,5},{5,1},{9,13},{13,9},{2,6},{6,2},{1... | collective-permute-start | bytes 1572872 | tf_op jit(solution)/shard_map/ppermute | solution.py:22
  101.5 91.2 %all-to-all-start = ((bf16[16,2,384,128]{3,2,1,0:T(8,128)(2,1)}), bf16[16,2,384,128]{3,2,1,0:T(8,128)(2,1)}, u32[]{:S(2)}, u32[]{:S(2)}) async-start(bf16[16,2,384,128]{3,2,1,0:T(8,128)(2,1)} %get-tuple-element.141), calls=%async_computation | async-start | bytes 6291456 | tf_op jit(solution)/shard_map/all_to_all | solution.py:506
  108.5 7.9 %collective-permute-start.17 = (bf16[64,2048]{1,0:T(8,128)(2,1)S(1)}, bf16[64,2048]{1,0:T(8,128)(2,1)S(1)}, u32[]{:S(2)}, u32[]{:S(2)}) collective-permute-start(bf16[64,2048]{1,0:T(8,128)(2,1)S(1)} %copy-done.20), channel_id=1, source_target_pairs={{0,1},{1,0},{2,3},{3,2},{4,5},{5,4},{6,7},{7,6},{8,9},{9,8},{10,11... | collective-permute-start | bytes 786440 | tf_op jit(solution)/shard_map/ppermute | solution.py:22
  110.0 14.4 %collective-permute-start.18 = (bf16[64,2048]{1,0:T(8,128)(2,1)S(1)}, bf16[64,2048]{1,0:T(8,128)(2,1)S(1)}, u32[]{:S(2)}, u32[]{:S(2)}) collective-permute-start(bf16[64,2048]{1,0:T(8,128)(2,1)S(1)} %copy-done.19), channel_id=1, source_target_pairs={{0,3},{1,2},{2,1},{3,0},{4,7},{5,6},{6,5},{7,4},{8,11},{9,10},{10,... | collective-permute-start | bytes 786440 | tf_op jit(solution)/shard_map/ppermute | solution.py:22
  111.8 12.6 %collective-permute-start.19 = (bf16[64,2048]{1,0:T(8,128)(2,1)S(1)}, bf16[64,2048]{1,0:T(8,128)(2,1)S(1)}, u32[]{:S(2)}, u32[]{:S(2)}) collective-permute-start(bf16[64,2048]{1,0:T(8,128)(2,1)S(1)} %copy-done.18), channel_id=1, source_target_pairs={{0,2},{1,3},{2,0},{3,1},{4,6},{5,7},{6,4},{7,5},{8,10},{9,11},{10,... | collective-permute-start | bytes 786440 | tf_op jit(solution)/shard_map/ppermute | solution.py:22
  128.2 9.1 %collective-permute-start.22 = (bf16[32,2048]{1,0:T(8,128)(2,1)}, bf16[32,2048]{1,0:T(8,128)(2,1)S(1)}, u32[]{:S(2)}, u32[]{:S(2)}) collective-permute-start(bf16[32,2048]{1,0:T(8,128)(2,1)} %get-tuple-element.116), channel_id=1, source_target_pairs={{0,3},{1,2},{2,1},{3,0},{4,7},{5,6},{6,5},{7,4},{8,11},{9,10},{10,... | collective-permute-start | bytes 393224 | tf_op jit(solution)/shard_map/ppermute | solution.py:22
  130.1 7.2 %collective-permute-start.20 = (bf16[32,2048]{1,0:T(8,128)(2,1)}, bf16[32,2048]{1,0:T(8,128)(2,1)S(1)}, u32[]{:S(2)}, u32[]{:S(2)}) collective-permute-start(bf16[32,2048]{1,0:T(8,128)(2,1)} %get-tuple-element.116), channel_id=1, source_target_pairs={{0,1},{1,0},{2,3},{3,2},{4,5},{5,4},{6,7},{7,6},{8,9},{9,8},{10,11... | collective-permute-start | bytes 393224 | tf_op jit(solution)/shard_map/ppermute | solution.py:22
  138.3 16.5 %collective-permute-start.25 = (bf16[128,2048]{1,0:T(8,128)(2,1)S(1)}, bf16[128,2048]{1,0:T(8,128)(2,1)S(1)}, u32[]{:S(2)}, u32[]{:S(2)}) collective-permute-start(bf16[128,2048]{1,0:T(8,128)(2,1)S(1)} %pad_maximum_fusion.3.refs_0_), channel_id=1, source_target_pairs={{0,4},{4,0},{8,12},{12,8},{1,5},{5,1},{9,13},{13,9},{2,6},{6,2},{1... | collective-permute-start | bytes 1572872 | tf_op jit(solution)/shard_map/ppermute | solution.py:22
  139.7 7.3 %collective-permute-start.27 = (bf16[64,2048]{1,0:T(8,128)(2,1)S(1)}, bf16[64,2048]{1,0:T(8,128)(2,1)S(1)}, u32[]{:S(2)}, u32[]{:S(2)}) collective-permute-start(bf16[64,2048]{1,0:T(8,128)(2,1)S(1)} %pad_maximum_fusion.5.refs_2_), channel_id=1, source_target_pairs={{0,2},{1,3},{2,0},{3,1},{4,6},{5,7},{6,4},{7,5},{8,10},{9,11},{10,... | collective-permute-start | bytes 786440 | tf_op jit(solution)/shard_map/ppermute | solution.py:22
  140.7 14.0 %collective-permute-start.26 = (bf16[64,2048]{1,0:T(8,128)(2,1)S(1)}, bf16[64,2048]{1,0:T(8,128)(2,1)S(1)}, u32[]{:S(2)}, u32[]{:S(2)}) collective-permute-start(bf16[64,2048]{1,0:T(8,128)(2,1)S(1)} %pad_maximum_fusion.5.refs_2_), channel_id=1, source_target_pairs={{0,3},{1,2},{2,1},{3,0},{4,7},{5,6},{6,5},{7,4},{8,11},{9,10},{10,... | collective-permute-start | bytes 786440 | tf_op jit(solution)/shard_map/ppermute | solution.py:22
  142.9 11.8 %collective-permute-start.24 = (bf16[64,2048]{1,0:T(8,128)(2,1)S(1)}, bf16[64,2048]{1,0:T(8,128)(2,1)S(1)}, u32[]{:S(2)}, u32[]{:S(2)}) collective-permute-start(bf16[64,2048]{1,0:T(8,128)(2,1)S(1)} %pad_maximum_fusion.5.refs_2_), channel_id=1, source_target_pairs={{0,1},{1,0},{2,3},{3,2},{4,5},{5,4},{6,7},{7,6},{8,9},{9,8},{10,11... | collective-permute-start | bytes 786440 | tf_op jit(solution)/shard_map/ppermute | solution.py:22
  166.2 16.0 %collective-permute-start.29 = (bf16[128,2048]{1,0:T(8,128)(2,1)S(1)}, bf16[128,2048]{1,0:T(8,128)(2,1)S(1)}, u32[]{:S(2)}, u32[]{:S(2)}) collective-permute-start(bf16[128,2048]{1,0:T(8,128)(2,1)S(1)} %get-tuple-element.129), channel_id=1, source_target_pairs={{0,4},{4,0},{8,12},{12,8},{1,5},{5,1},{9,13},{13,9},{2,6},{6,2},{1... | collective-permute-start | bytes 1572872 | tf_op jit(solution)/shard_map/ppermute | solution.py:22
  167.5 6.9 %collective-permute-start.28 = (bf16[64,2048]{1,0:T(8,128)(2,1)S(1)}, bf16[64,2048]{1,0:T(8,128)(2,1)S(1)}, u32[]{:S(2)}, u32[]{:S(2)}) collective-permute-start(bf16[64,2048]{1,0:T(8,128)(2,1)S(1)} %get-tuple-element.128), channel_id=1, source_target_pairs={{0,1},{1,0},{2,3},{3,2},{4,5},{5,4},{6,7},{7,6},{8,9},{9,8},{10,11... | collective-permute-start | bytes 786440 | tf_op jit(solution)/shard_map/ppermute | solution.py:22
  167.8 8.2 %collective-permute-start.30 = (bf16[64,2048]{1,0:T(8,128)(2,1)S(1)}, bf16[64,2048]{1,0:T(8,128)(2,1)}, u32[]{:S(2)}, u32[]{:S(2)}) collective-permute-start(bf16[64,2048]{1,0:T(8,128)(2,1)S(1)} %get-tuple-element.130), channel_id=1, source_target_pairs={{0,3},{1,2},{2,1},{3,0},{4,7},{5,6},{6,5},{7,4},{8,11},{9,10},{10,... | collective-permute-start | bytes 786440 | tf_op jit(solution)/shard_map/ppermute | solution.py:22
  169.8 12.4 %collective-permute-start.31 = (bf16[64,2048]{1,0:T(8,128)(2,1)S(1)}, bf16[64,2048]{1,0:T(8,128)(2,1)}, u32[]{:S(2)}, u32[]{:S(2)}) collective-permute-start(bf16[64,2048]{1,0:T(8,128)(2,1)S(1)} %get-tuple-element.131), channel_id=1, source_target_pairs={{0,2},{1,3},{2,0},{3,1},{4,6},{5,7},{6,4},{7,5},{8,10},{9,11},{10,... | collective-permute-start | bytes 786440 | tf_op jit(solution)/shard_map/ppermute | solution.py:22
  (36 other events, 269.9 us)
Sparse Core Ops, SparseCore 0:
  30.9 65.7 all-gather.2

commit v3 on v2

--- a/solution.py
+++ b/solution.py
@@ -31,14 +31,16 @@
     return lax.optimization_barrier(jnp.concatenate(pieces, axis=0))
 
 
-def gather_plane(one, two, also):
-    sent = [x for k in (1, 3, 2) for x in (("col", k, one), ("row", k, two))]
-    got = lax.optimization_barrier([swap(*x) for x in sent] + also)
-    also = got[6:]
+def gather_plane(one, two, two_more, also):
+    sent = [("col", 1, one), ("row", 1, two), ("col", 3, one), ("row", 3, two)]
+    sent += [("col", 2, one), ("row", 2, two_more)]
+    got = lax.optimization_barrier([swap(*x) for x in sent] + [also])
+    tall = two.shape[0]
+    more = [got[6], got[5][tall:]]
     one = join([one, got[0], got[4], got[2]])
-    two = join([two, got[1], got[5], got[3]])
+    two = join([two, got[1], got[5][:tall], got[3]])
     got = together([x for k in (1, 3, 2) for x in (("row", k, one), ("col", k, two))])
-    return [one, got[0], got[4], got[2], two, got[1], got[5], got[3]], also
+    return [one, got[0], got[4], got[2], two, got[1], got[5], got[3]], more
 
 
 def gather_block(one, two):
@@ -81,6 +83,7 @@
     return pl.pallas_call(
         norm_kernel,
         out_shape=(part, part),
+        compiler_params=pltpu.CompilerParams(vmem_limit_bytes=4 << 20),
         cost_estimate=pl.CostEstimate(
             flops=8 * rows.size, transcendentals=0, bytes_accessed=4 * rows.size
         ),
@@ -104,6 +107,7 @@
     return pl.pallas_call(
         mid_kernel,
         out_shape=(jax.ShapeDtypeStruct(rows.shape, jnp.bfloat16), part, part),
+        compiler_params=pltpu.CompilerParams(vmem_limit_bytes=6 << 20),
         cost_estimate=pl.CostEstimate(
             flops=12 * rows.size, transcendentals=0, bytes_accessed=14 * rows.size
         ),
@@ -132,7 +136,7 @@
         in_specs=[in_vmem] * (len(pieces) + 1),
         out_specs=in_vmem,
         scratch_shapes=[pltpu.VMEM((4 * tall, width), jnp.bfloat16)],
-        compiler_params=pltpu.CompilerParams(vmem_limit_bytes=24 << 20),
+        compiler_params=pltpu.CompilerParams(vmem_limit_bytes=10 << 20),
         cost_estimate=pl.CostEstimate(
             flops=2 * shape[0] * width * shape[1], transcendentals=0, bytes_accessed=7 << 20
         ),
@@ -177,13 +181,14 @@
     return pl.pallas_call(
         project_kernel,
         out_shape=[jax.ShapeDtypeStruct((local_rows, width), jnp.bfloat16)] * 4,
-        in_specs=[in_vmem] * 4 + [pl.BlockSpec(memory_space=pl.ANY)],
+        in_specs=[in_vmem] * 4 + [pl.BlockSpec(memory_space=pltpu.HBM)],
         out_specs=[in_vmem] * 4,
         scratch_shapes=[
             pltpu.VMEM((rows, 4 * size), jnp.bfloat16),
             pltpu.VMEM((4 * size, width), jnp.bfloat16),
             pltpu.SemaphoreType.DMA((fed.shape[0],)),
         ],
+        compiler_params=pltpu.CompilerParams(vmem_limit_bytes=10 << 20),
         cost_estimate=pl.CostEstimate(
             flops=8 * rows * size * width, transcendentals=0, bytes_accessed=4 << 20
         ),
@@ -199,19 +204,19 @@
     part_in, part_down = width // shares, units // shares
     first = tall - part_in // 2 - part_down
     half = width // 2
-    jobs = [(w_in_ref, in_ref.at[0]), (w_down_ref, down_ref.at[0])]
+    jobs = []
     for r in range(shares):
         for n in range(2):
             jobs.append(
                 (
                     fed_ref.at[r, pl.ds(first, part_in // 2), pl.ds(half * n, half)],
-                    in_ref.at[1, pl.ds(part_in * r + part_in // 2 * n, part_in // 2)],
+                    in_ref.at[pl.ds(part_in * r + part_in // 2 * n, part_in // 2)],
                 )
             )
         jobs.append(
             (
                 fed_ref.at[r, pl.ds(tall - part_down, part_down)],
-                down_ref.at[1, pl.ds(part_down * r, part_down)],
+                down_ref.at[pl.ds(part_down * r, part_down)],
             )
         )
     copies = [
@@ -224,11 +229,10 @@
     for piece in pieces:
         rows_ref[pl.ds(at, piece.shape[0]), :] = piece[...]
         at += piece.shape[0]
-    copies[0].wait()
     step = 256
-    for shard in range(2):
+    for shard, weight_ref in enumerate((w_in_ref, in_ref)):
         if shard == 1:
-            for copy in copies[1:]:
+            for copy in copies:
                 copy.wait()
 
         @pl.loop(0, units // step)
@@ -236,12 +240,12 @@
             at = pl.multiple_of(step * j, step)
             gate = jnp.dot(
                 rows_ref[...],
-                in_ref[shard, :, pl.ds(at, step)],
+                weight_ref[:, pl.ds(at, step)],
                 preferred_element_type=jnp.float32,
             )
             up = jnp.dot(
                 rows_ref[...],
-                in_ref[shard, :, pl.ds(pl.multiple_of(units + at, step), step)],
+                weight_ref[:, pl.ds(pl.multiple_of(units + at, step), step)],
                 preferred_element_type=jnp.float32,
             )
             hidden = gate / (1.0 + jnp.exp(-gate)) * up
@@ -251,8 +255,8 @@
     def _(j):
         span = pl.ds(pl.multiple_of(step * j, step), step)
         total = jnp.dot(
-            hidden_ref[0], down_ref[0, :, span], preferred_element_type=jnp.float32
-        ) + jnp.dot(hidden_ref[1], down_ref[1, :, span], preferred_element_type=jnp.float32)
+            hidden_ref[0], w_down_ref[:, span], preferred_element_type=jnp.float32
+        ) + jnp.dot(hidden_ref[1], down_ref[:, span], preferred_element_type=jnp.float32)
         total = total.astype(jnp.bfloat16)
         at = 0
         for out in outs:
@@ -266,17 +270,17 @@
     return pl.pallas_call(
         feed_kernel,
         out_shape=[jax.ShapeDtypeStruct(piece.shape, jnp.bfloat16) for piece in pieces],
-        in_specs=[pl.BlockSpec(memory_space=pltpu.VMEM)] * len(pieces)
-        + [pl.BlockSpec(memory_space=pl.ANY)] * 3,
+        in_specs=[pl.BlockSpec(memory_space=pltpu.VMEM)] * (len(pieces) + 2)
+        + [pl.BlockSpec(memory_space=pltpu.HBM)],
         out_specs=[pl.BlockSpec(memory_space=pltpu.VMEM)] * len(pieces),
         scratch_shapes=[
             pltpu.VMEM((rows, width), jnp.bfloat16),
-            pltpu.VMEM((2, width, 2 * units), jnp.bfloat16),
-            pltpu.VMEM((2, units, width), jnp.bfloat16),
+            pltpu.VMEM((width, 2 * units), jnp.bfloat16),
+            pltpu.VMEM((units, width), jnp.bfloat16),
             pltpu.VMEM((2, rows, units), jnp.bfloat16),
-            pltpu.SemaphoreType.DMA((2 + 3 * fed.shape[0],)),
+            pltpu.SemaphoreType.DMA((3 * fed.shape[0],)),
         ],
-        compiler_params=pltpu.CompilerParams(vmem_limit_bytes=48 << 20),
+        compiler_params=pltpu.CompilerParams(vmem_limit_bytes=18 << 20),
         cost_estimate=pl.CostEstimate(
             flops=12 * rows * width * units, transcendentals=2 * rows * units,
             bytes_accessed=16 << 20,
@@ -285,15 +289,10 @@
     )(*pieces, w_in, w_down, fed)
 
 
-def attend_kernel(
-    place_ref, length_ref, span_ref, target_ref,
-    joined_ref, cache_ref, cos_ref, sin_ref, far_cos_ref, far_sin_ref, context_ref, new_ref,
+def attend_one(
+    request, away, column, length_old, span_new,
+    joined_ref, cache_ref, cos_ref, sin_ref, far_cos_ref, far_sin_ref, new_ref,
 ):
-    g = pl.program_id(0)
-    row, column = place_ref[0], place_ref[1]
-    request = request_of(g, row)
-    length_old = length_ref[request]
-    away = row ^ (request // 2)
     columns = [column ^ (2 * (request % 2) + n) for n in range(2)]
 
     def block(n):
@@ -312,25 +311,24 @@
     queries = turned(joined[:, :128])
     keys_new = turned(joined[:, 128:256])
     values_new = joined[:, 256:].astype(jnp.bfloat16)
-    stored = cache_ref.shape[2]
-    whole = new_ref.shape[2]
-    live = lax.broadcasted_iota(jnp.int32, keys_new.shape, 0) < span_ref[request]
+    stored, whole = cache_ref.shape[1], new_ref.shape[1]
+    live = lax.broadcasted_iota(jnp.int32, keys_new.shape, 0) < span_new
     rows = lax.broadcasted_iota(jnp.int32, (whole, keys_new.shape[1]), 0)
     for kind, fresh in enumerate((keys_new, values_new)):
         fresh = jnp.where(live, fresh.astype(jnp.float32), 0.0)
         fresh = jnp.concatenate(
             [fresh, jnp.zeros((whole - fresh.shape[0], fresh.shape[1]), jnp.float32)], axis=0
         )
-        old = cache_ref[0, kind].astype(jnp.float32)
+        old = cache_ref[kind].astype(jnp.float32)
         old = jnp.concatenate(
             [old, jnp.zeros((whole - stored, old.shape[1]), jnp.float32)], axis=0
         )
         fresh = pltpu.roll(fresh, length_old, axis=0)
-        new_ref[0, kind] = jnp.where(rows < length_old, old, fresh).astype(jnp.bfloat16)
+        new_ref[kind] = jnp.where(rows < length_old, old, fresh).astype(jnp.bfloat16)
     scale = 1.0 / math.sqrt(128)
     contract = (((1,), (1,)), ((), ()))
     old = (
-        lax.dot_general(queries, cache_ref[0, 0], contract, preferred_element_type=jnp.float32)
+        lax.dot_general(queries, cache_ref[0], contract, preferred_element_type=jnp.float32)
         * scale
     )
     new = (
@@ -348,53 +346,76 @@
     old = jnp.where(old_ok, jnp.exp(old - highest), 0.0)
     new = jnp.where(new_ok, jnp.exp(new - highest), 0.0)
     total = jnp.sum(old, axis=1, keepdims=True) + jnp.sum(new, axis=1, keepdims=True)
-    old_weights = (old / total).astype(jnp.bfloat16)
-    new_weights = (new / total).astype(jnp.bfloat16)
-    stored_values = cache_ref[0, 1]
     context = jnp.dot(
-        old_weights, stored_values, preferred_element_type=jnp.float32
-    ) + jnp.dot(new_weights, values_new, preferred_element_type=jnp.float32)
-    context = context.astype(jnp.bfloat16)
-    for n in range(2):
-        place = pl.multiple_of(64 * (4 * (g // 2) + columns[n]), 64)
-        context_ref[pl.ds(place, 64), :] = context[64 * n : 64 * n + 64]
-
-
-def request_of(g, row):
-    return 2 * (row ^ (g // 2)) + g % 2
+        (old / total).astype(jnp.bfloat16), cache_ref[1], preferred_element_type=jnp.float32
+    ) + jnp.dot(
+        (new / total).astype(jnp.bfloat16), values_new, preferred_element_type=jnp.float32
+    )
+    return context.astype(jnp.bfloat16), columns
+
+
+def attend_kernel(
+    place_ref, length_ref, span_ref, target_ref,
+    joined_ref, cache_ref, cos_ref, sin_ref, far_cos_ref, far_sin_ref, *refs,
+):
+    contexts, (sent_ref, held_ref, sems) = refs[:4], refs[4:]
+    step = pl.program_id(0)
+    column = place_ref[1]
+    source_row = place_ref[0] ^ step
+
+    def copy_of(n, target):
+        return pltpu.make_async_copy(held_ref.at[n], sent_ref.at[target], sems.at[n])
+
+    for m in range(2):
+        request = 2 * source_row + m
+        context, columns = attend_one(
+            request, step, column, length_ref[request], span_ref[request],
+            joined_ref, cache_ref.at[m], cos_ref, sin_ref, far_cos_ref, far_sin_ref,
+            held_ref.at[2 * step + m],
+        )
+        for n in range(2):
+            for q in range(4):
+
+                @pl.when(step == q)
+                def _():
+                    at = pl.multiple_of(64 * columns[n], 64)
+                    contexts[q][pl.ds(at, 64), :] = context[64 * n : 64 * n + 64]
+
+        copy_of(2 * step + m, target_ref[request]).start()
+
+    @pl.when(step == 3)
+    def _():
+        for n in range(8):
+            copy_of(n, target_ref[2 * (place_ref[0] ^ (n // 2)) + n % 2]).wait()
 
 
 def attend(place, lengths, spans, targets, joined, cache, tables, replicas):
     slots, kinds, stored, size = cache.shape
     span = tables[0].shape[0]
-    whole = lambda g, *refs: (0, 0)
+    in_vmem = pl.BlockSpec(memory_space=pltpu.VMEM)
+    context = jax.ShapeDtypeStruct((slots // 4 * span, size), jnp.bfloat16)
     return pl.pallas_call(
         attend_kernel,
-        out_shape=(
-            jax.ShapeDtypeStruct((slots * span, size), jnp.bfloat16),
-            jax.ShapeDtypeStruct((replicas, kinds, stored + span, size), jnp.bfloat16),
-        ),
+        out_shape=[context] * 4
+        + [pltpu.HBM((replicas, kinds, stored + span, size), jnp.bfloat16)],
         grid_spec=pltpu.PrefetchScalarGridSpec(
             num_scalar_prefetch=4,
-            grid=(slots,),
+            grid=(4,),
             in_specs=[
-                pl.BlockSpec(memory_space=pltpu.VMEM),
+                in_vmem,
                 pl.BlockSpec(
-                    (1, kinds, stored, size),
-                    lambda g, place, *refs: (request_of(g, place[0]), 0, 0, 0),
+                    (slots // 4, kinds, stored, size),
+                    lambda step, place, *refs: (place[0] ^ step, 0, 0, 0),
                 ),
             ]
-            + [pl.BlockSpec(table.shape, whole) for table in tables],
-            out_specs=[
-                pl.BlockSpec((slots * span, size), whole),
-                pl.BlockSpec(
-                    (1, kinds, stored + span, size),
-                    lambda g, place, lengths, spans, targets: (
-                        targets[request_of(g, place[0])], 0, 0, 0,
-                    ),
-                ),
+            + [in_vmem] * len(tables),
+            out_specs=[in_vmem] * 4 + [pl.BlockSpec(memory_space=pltpu.HBM)],
+            scratch_shapes=[
+                pltpu.VMEM((slots, kinds, stored + span, size), jnp.bfloat16),
+                pltpu.SemaphoreType.DMA((slots,)),
             ],
         ),
+        compiler_params=pltpu.CompilerParams(vmem_limit_bytes=12 << 20),
         cost_estimate=pl.CostEstimate(
             flops=4 * slots * span * (stored + span) * size,
             transcendentals=slots * span * (stored + span),
@@ -427,8 +448,8 @@
     return pl.pallas_call(
         pick_kernel,
         out_shape=jax.ShapeDtypeStruct(shape, moved.dtype),
-        in_specs=[pl.BlockSpec(memory_space=pltpu.SMEM), pl.BlockSpec(memory_space=pl.ANY)],
-        out_specs=pl.BlockSpec(memory_space=pl.ANY),
+        in_specs=[pl.BlockSpec(memory_space=pltpu.SMEM), pl.BlockSpec(memory_space=pltpu.HBM)],
+        out_specs=pl.BlockSpec(memory_space=pltpu.HBM),
         scratch_shapes=[pltpu.VMEM(shape, moved.dtype), pltpu.SemaphoreType.DMA((2, shape[0]))],
         cost_estimate=pl.CostEstimate(
             flops=0, transcendentals=0, bytes_accessed=4 * math.prod(shape)
@@ -470,14 +491,13 @@
     in_slice = lax.dynamic_slice_in_dim(w_gate_up, replica * rows_in, rows_in)
     in_slice = in_slice.reshape(2, rows_in // 2, 2 * units)
     down_slice = lax.dynamic_slice_in_dim(w_down, replica * rows_down, rows_down)
-    feed_slice = jnp.concatenate(
-        [jnp.concatenate([in_slice[0], in_slice[1]], axis=1), down_slice], axis=0
-    )
-    feed_far = swap("row", 2, feed_slice)
-
-    pieces, (out_far, feed_far) = gather_plane(one, two, [out_far, feed_far])
+    two_more = jnp.concatenate(
+        [two, jnp.concatenate([in_slice[0], in_slice[1]], axis=1), down_slice], axis=0
+    )
+
+    pieces, more = gather_plane(one, two, two_more, out_far)
     fed = lax.all_gather(
-        jnp.concatenate([out_far, feed_far], axis=0), "rep", axis=0, tiled=False
+        jnp.concatenate(more, axis=0), "rep", axis=0, tiled=False
     )
     w_in = w_gate_up.reshape(width, 2 * units)
     pieces, w_in = lax.optimization_barrier((pieces, w_in))
@@ -495,12 +515,11 @@
         jnp.sin(far) * jnp.asarray(sign, jnp.float32),
     )
     place = jnp.stack([row, column]).astype(jnp.int32)
-    context, sent = attend(place, lengths, spans, targets, joined, cache, tables, replicas)
-
-    context = context.reshape(4, 4 * local_rows, size)
-    got = together([("row", k, context[k]) for k in (1, 3, 2)])
+    *context, sent = attend(place, lengths, spans, targets, joined, cache, tables, replicas)
+
+    got, sent = lax.optimization_barrier(([swap("row", k, context[k]) for k in (1, 3, 2)], sent))
+    fed = pltpu.with_memory_space_constraint(fed, pltpu.HBM)
     partial = project([context[0], got[0], got[2], got[1]], fed, local_rows)
-    partial, sent = lax.optimization_barrier((partial, sent))
     got = together([("col", k, partial[k]) for k in (1, 3, 2)])
     middle, one, two = mid(hidden_in, partial[0], [got[0], got[2], got[1]])
     moved = lax.all_to_all(sent, "rep", split_axis=0, concat_axis=0, tiled=True)

time: 204 us -> 186 us (0.912)
  Pallas kernels: 37 us -> 27.4 us
  waiting for transfers between devices: 78.1 us -> 69.8 us
  starting transfers between devices: 49.9 us -> 57.2 us
  local copies, waits for them, and re-layouts: 14.9 us -> 11.3 us
  other arithmetic: 8.3 us -> 4.89 us
    all_gather x1, waiting for transfers between devices: 10.3 us -> 0.01 us  [body(): lax.all_gather(jnp.concatenate(more, axis=0), 'rep', axis=0, tiled=False)]
    all_to_all x1, starting transfers between devices: 7.04 us -> 15.2 us  [body(): moved = lax.all_to_all(sent, 'rep', split_axis=0, concat_axis=0, tiled=True)]
    pallas_call x2, Pallas kernels: 11.4 us -> 7.36 us  [the longest x1 7.1 us: attend(): pl.pallas_call(attend_kernel, out_shape=[context] * 4 + [pltpu.HBM((repli...]
    ppermute x35 -> x34, waiting for transfers between devices: 67.7 us -> 69.8 us  [swap(): return lax.ppermute(array, axis, [(i, i ^ k) for i in range(size)])]
    unnamed x47 -> x35, local copies, waits for them, and re-layouts: 10 us -> 8.49 us
    ppermute x35 -> x34, starting transfers between devices: 42.1 us -> 41.3 us  [swap(): return lax.ppermute(array, axis, [(i, i ^ k) for i in range(size)])]
  transfers between devices with their start and end apart: 38 -> 37, of which waited for: 23 -> 21; matrix products, arithmetic and copies ran while one was open for 8% -> 5% of each run, Pallas kernels for 13% -> 15%
where the time goes in v3:
time: 186 us; the launch traced here: 185 us
  waiting for transfers between devices  69.8 us (38%)
  starting transfers between devices  57.2 us (31%)
  Pallas kernels  27.4 us (15%)
  between operations  14.4 us (8%)
  local copies, waits for them, and re-layouts  11.3 us (6%)
  other arithmetic  4.89 us (3%)
    ppermute x34, waiting for transfers between devices, swap(): return lax.ppermute(array, axis, [(i, i ^ k) for i in range(size)])  69.8 us
    ppermute x34, starting transfers between devices, swap(): return lax.ppermute(array, axis, [(i, i ^ k) for i in range(size)])  41.3 us
    all_to_all x1, starting transfers between devices, body(): moved = lax.all_to_all(sent, 'rep', split_axis=0, concat_axis=0, tiled=True)  15.2 us
    pallas_call x1, Pallas kernels, feed(): pl.pallas_call(feed_kernel, out_shape=[jax.ShapeDtypeStruct(piece.shape,...  9.45 us
    unnamed x35, local copies, waits for them, and re-layouts  8.49 us
    pallas_call x1, Pallas kernels, attend(): pl.pallas_call(attend_kernel, out_shape=[context] * 4 + [pltpu.HBM((repli...  7.1 us
    pallas_call x1, Pallas kernels, join_heads(): pl.pallas_call(joined_kernel, out_shape=jax.ShapeDtypeStruct(shape, jnp.f...  4.11 us
  transfers between devices with their start and end apart: 37, of which 21 were waited for; matrix products, arithmetic and copies ran while one was open for 5% of the time, Pallas kernels for 15%

profile of v3, /device:TPU:1, one launch (start us, length us, event | category | flops | bytes accessed | tf_op | source)
XLA Modules:
  0.0 185.0 jit_solution(5590033174250070773)
XLA Ops:
  10.7 3.8 %collective-permute-start.5 = (bf16[128,2048]{1,0:T(8,128)(2,1)S(1)}, bf16[128,2048]{1,0:T(8,128)(2,1)S(1)}, u32[]{:S(2)}, u32[]{:S(2)}) collective-permute-start(bf16[128,2048]{1,0:T(8,128)(2,1)S(1)} %fusion), channel_id=1, source_target_pairs={{0,8},{4,12},{8,0},{12,4},{1,9},{5,13},{9,1},{13,5},{2,10},{6,14},... | collective-permute-start | bytes 1572872 | tf_op jit(solution)/shard_map/ppermute | solution.py:22
  15.2 2.8 %collective-permute-start.4 = (bf16[32,2048]{1,0:T(8,128)(2,1)S(1)}, bf16[32,2048]{1,0:T(8,128)(2,1)S(1)}, u32[]{:S(2)}, u32[]{:S(2)}) collective-permute-start(bf16[32,2048]{1,0:T(8,128)(2,1)S(1)} %get-tuple-element.72), channel_id=1, source_target_pairs={{0,2},{1,3},{2,0},{3,1},{4,6},{5,7},{6,4},{7,5},{8,10},{9,11},{10,... | collective-permute-start | bytes 393224 | tf_op jit(solution)/shard_map/ppermute | solution.py:22
  21.0 2.9 %collective-permute-done.2 = bf16[32,2048]{1,0:T(8,128)(2,1)S(1)} collective-permute-done((bf16[32,2048]{1,0:T(8,128)(2,1)S(1)}, bf16[32,2048]{1,0:T(8,128)(2,1)S(1)}, u32[]{:S(2)}, u32[]{:S(2)}) %collective-permute-start.2) | collective-permute-done | bytes 131104 | tf_op jit(solution)/shard_map/ppermute | solution.py:22
  24.0 5.5 %collective-permute-done.3 = bf16[32,2048]{1,0:T(8,128)(2,1)S(1)} collective-permute-done((bf16[32,2048]{1,0:T(8,128)(2,1)S(1)}, bf16[32,2048]{1,0:T(8,128)(2,1)S(1)}, u32[]{:S(2)}, u32[]{:S(2)}) %collective-permute-start.3) | collective-permute-done | bytes 131104 | tf_op jit(solution)/shard_map/ppermute | solution.py:22
  30.5 3.1 %collective-permute-start.12 = (bf16[128,2048]{1,0:T(8,128)(2,1)S(1)}, bf16[128,2048]{1,0:T(8,128)(2,1)S(1)}, u32[]{:S(2)}, u32[]{:S(2)}) collective-permute-start(bf16[128,2048]{1,0:T(8,128)(2,1)S(1)} %fusion.2.refs_4_), channel_id=1, source_target_pairs={{0,2},{1,3},{2,0},{3,1},{4,6},{5,7},{6,4},{7,5},{8,10},{9,11},{10,... | collective-permute-start | bytes 1572872 | tf_op jit(solution)/shard_map/ppermute | solution.py:22
  34.5 3.0 %collective-permute-start.11 = (bf16[128,2048]{1,0:T(8,128)(2,1)S(1)}, bf16[128,2048]{1,0:T(8,128)(2,1)}, u32[]{:S(2)}, u32[]{:S(2)}) collective-permute-start(bf16[128,2048]{1,0:T(8,128)(2,1)S(1)} %pad_maximum_fusion.2.refs_0_), channel_id=1, source_target_pairs={{0,8},{4,12},{8,0},{12,4},{1,9},{5,13},{9,1},{13,5},{2,10},{6,14},... | collective-permute-start | bytes 1572872 | tf_op jit(solution)/shard_map/ppermute | solution.py:22
  38.2 6.3 %collective-permute-done.12.refs_6_ = bf16[128,2048]{1,0:T(8,128)(2,1)S(1)} collective-permute-done((bf16[128,2048]{1,0:T(8,128)(2,1)S(1)}, bf16[128,2048]{1,0:T(8,128)(2,1)S(1)}, u32[]{:S(2)}, u32[]{:S(2)}) %collective-permute-start.12) | collective-permute-done | bytes 524320 | tf_op jit(solution)/shard_map/ppermute | solution.py:22
  47.3 5.6 %copy.19 = bf16[256,8,2,512]{3,1,2,0:T(8,128)(2,1)} copy(bf16[256,8,2,512]{3,2,1,0:T(2,128)(2,1)} %bitcast.22) | data formatting | bytes 8388608
  53.2 4.0 %collective-permute-done.10.refs_7_ = bf16[128,2048]{1,0:T(8,128)(2,1)} collective-permute-done((bf16[128,2048]{1,0:T(8,128)(2,1)S(1)}, bf16[128,2048]{1,0:T(8,128)(2,1)}, u32[]{:S(2)}, u32[]{:S(2)}) %collective-permute-start.10) | collective-permute-done | bytes 524320 | tf_op jit(solution)/shard_map/ppermute | solution.py:22
  57.3 4.0 %collective-permute-done.9.refs_3_ = bf16[128,2048]{1,0:T(8,128)(2,1)} collective-permute-done((bf16[128,2048]{1,0:T(8,128)(2,1)S(1)}, bf16[128,2048]{1,0:T(8,128)(2,1)}, u32[]{:S(2)}, u32[]{:S(2)}) %collective-permute-start.9) | collective-permute-done | bytes 524320 | tf_op jit(solution)/shard_map/ppermute | solution.py:22
  62.3 4.1 %join_heads.1.joined_ref = f32[1024,384]{1,0:T(8,128)S(1)} custom-call(bf16[128,2048]{1,0:T(8,128)(2,1)S(1)} %pad_maximum_fusion.2.refs_0_, bf16[128,2048]{1,0:T(8,128)(2,1)} %collective-permute-done.7.refs_1_, bf16[128,2048]{1,0:T(8,128)(2,1)} %collective-permute-done.11.refs_2_, bf16[128,2048]{1,0:T(8,128)(2,1)} %collective-permute-done.9.refs_3_, ...), custom_call_target="tpu_custom_call" | custom-call | flops 1610612736 | bytes 7340032 | tf_op jit(solution)/shard_map/join_heads/pallas_call | solution.py:133
  66.4 7.1 %attend.1 = (bf16[256,128]{1,0:T(8,128)(2,1)S(1)}, bf16[256,128]{1,0:T(8,128)(2,1)S(1)}, bf16[256,128]{1,0:T(8,128)(2,1)S(1)}, bf16[256,128]{1,0:T(8,128)(2,1)S(1)}, bf16[16,2,384,128]{3,2,1,0:T(8,128)(2,1)}) custom-call(s32[2]{0:T(128)S(1)} %pad_add_fusion.place_ref, s32[8]{0:T(128)S(1)} %get-tuple-element.143.length_ref, s32[8]{0:T(128)S(1)} %dynamic_slice.29.span_ref, ...), custom_call_target="tpu_custom_call" | custom-call | flops 201326592 | bytes 6291456 | tf_op jit(solution)/shard_map/attend/pallas_call | solution.py:397
  81.4 15.2 %all-to-all-start = ((bf16[16,2,384,128]{3,2,1,0:T(8,128)(2,1)}), bf16[16,2,384,128]{3,2,1,0:T(8,128)(2,1)}, u32[]{:S(2)}, u32[]{:S(2)}) async-start(bf16[16,2,384,128]{3,2,1,0:T(8,128)(2,1)} %get-tuple-element.137), calls=%async_computation | async-start | bytes 6291456 | tf_op jit(solution)/shard_map/all_to_all | solution.py:525
  96.6 3.1 %project.1 = (bf16[64,2048]{1,0:T(8,128)(2,1)S(1)}, bf16[64,2048]{1,0:T(8,128)(2,1)S(1)}, bf16[64,2048]{1,0:T(8,128)(2,1)S(1)}, bf16[64,2048]{1,0:T(8,128)(2,1)S(1)}) custom-call(bf16[256,128]{1,0:T(8,128)(2,1)S(1)} %get-tuple-element.95.refs_0_, bf16[256,128]{1,0:T(8,128)(2,1)S(1)} %collective-permute-done.13.refs_1_, ...), custom_call_target="tpu_custom_call" | custom-call | flops 536870912 | bytes 4194304 | tf_op jit(solution)/shard_map/project/pallas_call | solution.py:181
  103.2 4.5 %collective-permute-done.16.a_ref = bf16[64,2048]{1,0:T(8,128)(2,1)S(1)} collective-permute-done((bf16[64,2048]{1,0:T(8,128)(2,1)S(1)}, bf16[64,2048]{1,0:T(8,128)(2,1)S(1)}, u32[]{:S(2)}, u32[]{:S(2)}) %collective-permute-start.16) | collective-permute-done | bytes 262176 | tf_op jit(solution)/shard_map/ppermute | solution.py:22
  107.7 7.9 %collective-permute-done.17.c_ref = bf16[64,2048]{1,0:T(8,128)(2,1)S(1)} collective-permute-done((bf16[64,2048]{1,0:T(8,128)(2,1)S(1)}, bf16[64,2048]{1,0:T(8,128)(2,1)S(1)}, u32[]{:S(2)}, u32[]{:S(2)}) %collective-permute-start.17) | collective-permute-done | bytes 262176 | tf_op jit(solution)/shard_map/ppermute | solution.py:22
  122.1 2.4 %collective-permute-done.21 = bf16[32,2048]{1,0:T(8,128)(2,1)S(1)} collective-permute-done((bf16[32,2048]{1,0:T(8,128)(2,1)S(1)}, bf16[32,2048]{1,0:T(8,128)(2,1)S(1)}, u32[]{:S(2)}, u32[]{:S(2)}) %collective-permute-start.21) | collective-permute-done | bytes 131104 | tf_op jit(solution)/shard_map/ppermute | solution.py:22
  124.8 2.2 %collective-permute-start.24 = (bf16[128,2048]{1,0:T(8,128)(2,1)S(1)}, bf16[128,2048]{1,0:T(8,128)(2,1)S(1)}, u32[]{:S(2)}, u32[]{:S(2)}) collective-permute-start(bf16[128,2048]{1,0:T(8,128)(2,1)S(1)} %pad_maximum_fusion.4.refs_0_), channel_id=1, source_target_pairs={{0,4},{4,0},{8,12},{12,8},{1,5},{5,1},{9,13},{13,9},{2,6},{6,2},{1... | collective-permute-start | bytes 1572872 | tf_op jit(solution)/shard_map/ppermute | solution.py:22
  129.7 5.5 %collective-permute-done.26.refs_4_ = bf16[64,2048]{1,0:T(8,128)(2,1)S(1)} collective-permute-done((bf16[64,2048]{1,0:T(8,128)(2,1)S(1)}, bf16[64,2048]{1,0:T(8,128)(2,1)S(1)}, u32[]{:S(2)}, u32[]{:S(2)}) %collective-permute-start.26) | collective-permute-done | bytes 262176 | tf_op jit(solution)/shard_map/ppermute | solution.py:22
  135.2 7.3 %collective-permute-done.25.refs_5_ = bf16[64,2048]{1,0:T(8,128)(2,1)S(1)} collective-permute-done((bf16[64,2048]{1,0:T(8,128)(2,1)S(1)}, bf16[64,2048]{1,0:T(8,128)(2,1)S(1)}, u32[]{:S(2)}, u32[]{:S(2)}) %collective-permute-start.25) | collective-permute-done | bytes 262176 | tf_op jit(solution)/shard_map/ppermute | solution.py:22
  142.5 9.5 %feed.1 = (bf16[128,2048]{1,0:T(8,128)(2,1)S(1)}, bf16[128,2048]{1,0:T(8,128)(2,1)S(1)}, bf16[64,2048]{1,0:T(8,128)(2,1)S(1)}, bf16[64,2048]{1,0:T(8,128)(2,1)S(...) custom-call(bf16[128,2048]{1,0:T(8,128)(2,1)S(1)} %pad_maximum_fusion.4.refs_0_, ...), custom_call_target="tpu_custom_call" | custom-call | flops 6442450944 | bytes 16777216 | tf_op jit(solution)/shard_map/feed/pallas_call | solution.py:270
  156.6 2.5 %collective-permute-done.27 = bf16[64,2048]{1,0:T(8,128)(2,1)} collective-permute-done((bf16[64,2048]{1,0:T(8,128)(2,1)S(1)}, bf16[64,2048]{1,0:T(8,128)(2,1)}, u32[]{:S(2)}, u32[]{:S(2)}) %collective-permute-start.27) | collective-permute-done | bytes 262176 | tf_op jit(solution)/shard_map/ppermute | solution.py:22
  161.2 6.3 %collective-permute-done.30 = bf16[64,2048]{1,0:T(8,128)(2,1)} collective-permute-done((bf16[64,2048]{1,0:T(8,128)(2,1)S(1)}, bf16[64,2048]{1,0:T(8,128)(2,1)}, u32[]{:S(2)}, u32[]{:S(2)}) %collective-permute-start.30) | collective-permute-done | bytes 262176 | tf_op jit(solution)/shard_map/ppermute | solution.py:22
  173.7 3.0 %pick.1 = bf16[8,2,384,128]{3,2,1,0:T(8,128)(2,1)} custom-call(s32[8]{0:T(128)} %select_reduce_fusion.source_ref, bf16[16,2,384,128]{3,2,1,0:T(8,128)(2,1)} %all-to-all-done.moved_ref), custom_call_target="tpu_custom_call" | custom-call | bytes 3145728 | tf_op jit(solution)/shard_map/pick/pallas_call | solution.py:448
  (120 shorter events, 49.0 us)
Async XLA Ops:
  7.2 89.4 %all-gather.3.cloned.1.call-start = ((), (), s32[]{:S(2)}) async-start(), calls=%async_computation.1 | async-start | bytes 8912896 | tf_op jit(solution)/shard_map/all_gather | solution.py:499
  10.7 18.8 %collective-permute-start.5 = (bf16[128,2048]{1,0:T(8,128)(2,1)S(1)}, bf16[128,2048]{1,0:T(8,128)(2,1)S(1)}, u32[]{:S(2)}, u32[]{:S(2)}) collective-permute-start(bf16[128,2048]{1,0:T(8,128)(2,1)S(1)} %fusion), channel_id=1, source_target_pairs={{0,8},{4,12},{8,0},{12,4},{1,9},{5,13},{9,1},{13,5},{2,10},{6,14},... | collective-permute-start | bytes 1572872 | tf_op jit(solution)/shard_map/ppermute | solution.py:22
  18.9 10.6 %collective-permute-start.3 = (bf16[32,2048]{1,0:T(8,128)(2,1)S(1)}, bf16[32,2048]{1,0:T(8,128)(2,1)S(1)}, u32[]{:S(2)}, u32[]{:S(2)}) collective-permute-start(bf16[32,2048]{1,0:T(8,128)(2,1)S(1)} %get-tuple-element.73), channel_id=1, source_target_pairs={{0,12},{4,8},{8,4},{12,0},{1,13},{5,9},{9,5},{13,1},{2,14},{6,10},... | collective-permute-start | bytes 393224 | tf_op jit(solution)/shard_map/ppermute | solution.py:22
  20.9 8.6 %collective-permute-start.1 = (bf16[32,2048]{1,0:T(8,128)(2,1)S(1)}, bf16[32,2048]{1,0:T(8,128)(2,1)S(1)}, u32[]{:S(2)}, u32[]{:S(2)}) collective-permute-start(bf16[32,2048]{1,0:T(8,128)(2,1)S(1)} %get-tuple-element.73), channel_id=1, source_target_pairs={{0,4},{4,0},{8,12},{12,8},{1,5},{5,1},{9,13},{13,9},{2,6},{6,2},{1... | collective-permute-start | bytes 393224 | tf_op jit(solution)/shard_map/ppermute | solution.py:22
  30.5 14.1 %collective-permute-start.12 = (bf16[128,2048]{1,0:T(8,128)(2,1)S(1)}, bf16[128,2048]{1,0:T(8,128)(2,1)S(1)}, u32[]{:S(2)}, u32[]{:S(2)}) collective-permute-start(bf16[128,2048]{1,0:T(8,128)(2,1)S(1)} %fusion.2.refs_4_), channel_id=1, source_target_pairs={{0,2},{1,3},{2,0},{3,1},{4,6},{5,7},{6,4},{7,5},{8,10},{9,11},{10,... | collective-permute-start | bytes 1572872 | tf_op jit(solution)/shard_map/ppermute | solution.py:22
  33.5 23.7 %collective-permute-start.10 = (bf16[128,2048]{1,0:T(8,128)(2,1)S(1)}, bf16[128,2048]{1,0:T(8,128)(2,1)}, u32[]{:S(2)}, u32[]{:S(2)}) collective-permute-start(bf16[128,2048]{1,0:T(8,128)(2,1)S(1)} %fusion.2.refs_4_), channel_id=1, source_target_pairs={{0,3},{1,2},{2,1},{3,0},{4,7},{5,6},{6,5},{7,4},{8,11},{9,10},{10,... | collective-permute-start | bytes 1572872 | tf_op jit(solution)/shard_map/ppermute | solution.py:22
  34.4 22.9 %collective-permute-start.8 = (bf16[128,2048]{1,0:T(8,128)(2,1)S(1)}, bf16[128,2048]{1,0:T(8,128)(2,1)}, u32[]{:S(2)}, u32[]{:S(2)}) collective-permute-start(bf16[128,2048]{1,0:T(8,128)(2,1)S(1)} %fusion.2.refs_4_), channel_id=1, source_target_pairs={{0,1},{1,0},{2,3},{3,2},{4,5},{5,4},{6,7},{7,6},{8,9},{9,8},{10,11... | collective-permute-start | bytes 1572872 | tf_op jit(solution)/shard_map/ppermute | solution.py:22
  34.5 22.8 %collective-permute-start.11 = (bf16[128,2048]{1,0:T(8,128)(2,1)S(1)}, bf16[128,2048]{1,0:T(8,128)(2,1)}, u32[]{:S(2)}, u32[]{:S(2)}) collective-permute-start(bf16[128,2048]{1,0:T(8,128)(2,1)S(1)} %pad_maximum_fusion.2.refs_0_), channel_id=1, source_target_pairs={{0,8},{4,12},{8,0},{12,4},{1,9},{5,13},{9,1},{13,5},{2,10},{6,14},... | collective-permute-start | bytes 1572872 | tf_op jit(solution)/shard_map/ppermute | solution.py:22
  37.5 23.8 %collective-permute-start.9 = (bf16[128,2048]{1,0:T(8,128)(2,1)S(1)}, bf16[128,2048]{1,0:T(8,128)(2,1)}, u32[]{:S(2)}, u32[]{:S(2)}) collective-permute-start(bf16[128,2048]{1,0:T(8,128)(2,1)S(1)} %pad_maximum_fusion.2.refs_0_), channel_id=1, source_target_pairs={{0,12},{4,8},{8,4},{12,0},{1,13},{5,9},{9,5},{13,1},{2,14},{6,10},... | collective-permute-start | bytes 1572872 | tf_op jit(solution)/shard_map/ppermute | solution.py:22
  45.4 15.9 %collective-permute-start.7 = (bf16[128,2048]{1,0:T(8,128)(2,1)S(1)}, bf16[128,2048]{1,0:T(8,128)(2,1)}, u32[]{:S(2)}, u32[]{:S(2)}) collective-permute-start(bf16[128,2048]{1,0:T(8,128)(2,1)S(1)} %pad_maximum_fusion.2.refs_0_), channel_id=1, source_target_pairs={{0,4},{4,0},{8,12},{12,8},{1,5},{5,1},{9,13},{13,9},{2,6},{6,2},{1... | collective-permute-start | bytes 1572872 | tf_op jit(solution)/shard_map/ppermute | solution.py:22
  81.4 92.3 %all-to-all-start = ((bf16[16,2,384,128]{3,2,1,0:T(8,128)(2,1)}), bf16[16,2,384,128]{3,2,1,0:T(8,128)(2,1)}, u32[]{:S(2)}, u32[]{:S(2)}) async-start(bf16[16,2,384,128]{3,2,1,0:T(8,128)(2,1)} %get-tuple-element.137), calls=%async_computation | async-start | bytes 6291456 | tf_op jit(solution)/shard_map/all_to_all | solution.py:525
  99.7 8.0 %collective-permute-start.16 = (bf16[64,2048]{1,0:T(8,128)(2,1)S(1)}, bf16[64,2048]{1,0:T(8,128)(2,1)S(1)}, u32[]{:S(2)}, u32[]{:S(2)}) collective-permute-start(bf16[64,2048]{1,0:T(8,128)(2,1)S(1)} %get-tuple-element.105), channel_id=1, source_target_pairs={{0,1},{1,0},{2,3},{3,2},{4,5},{5,4},{6,7},{7,6},{8,9},{9,8},{10,11... | collective-permute-start | bytes 786440 | tf_op jit(solution)/shard_map/ppermute | solution.py:22
  101.3 14.4 %collective-permute-start.17 = (bf16[64,2048]{1,0:T(8,128)(2,1)S(1)}, bf16[64,2048]{1,0:T(8,128)(2,1)S(1)}, u32[]{:S(2)}, u32[]{:S(2)}) collective-permute-start(bf16[64,2048]{1,0:T(8,128)(2,1)S(1)} %get-tuple-element.106), channel_id=1, source_target_pairs={{0,3},{1,2},{2,1},{3,0},{4,7},{5,6},{6,5},{7,4},{8,11},{9,10},{10,... | collective-permute-start | bytes 786440 | tf_op jit(solution)/shard_map/ppermute | solution.py:22
  103.1 12.5 %collective-permute-start.18 = (bf16[64,2048]{1,0:T(8,128)(2,1)S(1)}, bf16[64,2048]{1,0:T(8,128)(2,1)S(1)}, u32[]{:S(2)}, u32[]{:S(2)}) collective-permute-start(bf16[64,2048]{1,0:T(8,128)(2,1)S(1)} %get-tuple-element.107), channel_id=1, source_target_pairs={{0,2},{1,3},{2,0},{3,1},{4,6},{5,7},{6,4},{7,5},{8,10},{9,11},{10,... | collective-permute-start | bytes 786440 | tf_op jit(solution)/shard_map/ppermute | solution.py:22
  124.8 17.7 %collective-permute-start.24 = (bf16[128,2048]{1,0:T(8,128)(2,1)S(1)}, bf16[128,2048]{1,0:T(8,128)(2,1)S(1)}, u32[]{:S(2)}, u32[]{:S(2)}) collective-permute-start(bf16[128,2048]{1,0:T(8,128)(2,1)S(1)} %pad_maximum_fusion.4.refs_0_), channel_id=1, source_target_pairs={{0,4},{4,0},{8,12},{12,8},{1,5},{5,1},{9,13},{13,9},{2,6},{6,2},{1... | collective-permute-start | bytes 1572872 | tf_op jit(solution)/shard_map/ppermute | solution.py:22
  127.0 8.2 %collective-permute-start.26 = (bf16[64,2048]{1,0:T(8,128)(2,1)S(1)}, bf16[64,2048]{1,0:T(8,128)(2,1)S(1)}, u32[]{:S(2)}, u32[]{:S(2)}) collective-permute-start(bf16[64,2048]{1,0:T(8,128)(2,1)S(1)} %pad_maximum_fusion.5.refs_2_), channel_id=1, source_target_pairs={{0,2},{1,3},{2,0},{3,1},{4,6},{5,7},{6,4},{7,5},{8,10},{9,11},{10,... | collective-permute-start | bytes 786440 | tf_op jit(solution)/shard_map/ppermute | solution.py:22
  127.6 14.9 %collective-permute-start.25 = (bf16[64,2048]{1,0:T(8,128)(2,1)S(1)}, bf16[64,2048]{1,0:T(8,128)(2,1)S(1)}, u32[]{:S(2)}, u32[]{:S(2)}) collective-permute-start(bf16[64,2048]{1,0:T(8,128)(2,1)S(1)} %pad_maximum_fusion.5.refs_2_), channel_id=1, source_target_pairs={{0,3},{1,2},{2,1},{3,0},{4,7},{5,6},{6,5},{7,4},{8,11},{9,10},{10,... | collective-permute-start | bytes 786440 | tf_op jit(solution)/shard_map/ppermute | solution.py:22
  129.4 13.1 %collective-permute-start.23 = (bf16[64,2048]{1,0:T(8,128)(2,1)S(1)}, bf16[64,2048]{1,0:T(8,128)(2,1)S(1)}, u32[]{:S(2)}, u32[]{:S(2)}) collective-permute-start(bf16[64,2048]{1,0:T(8,128)(2,1)S(1)} %pad_maximum_fusion.5.refs_2_), channel_id=1, source_target_pairs={{0,1},{1,0},{2,3},{3,2},{4,5},{5,4},{6,7},{7,6},{8,9},{9,8},{10,11... | collective-permute-start | bytes 786440 | tf_op jit(solution)/shard_map/ppermute | solution.py:22
  152.0 15.5 %collective-permute-start.28 = (bf16[128,2048]{1,0:T(8,128)(2,1)S(1)}, bf16[128,2048]{1,0:T(8,128)(2,1)S(1)}, u32[]{:S(2)}, u32[]{:S(2)}) collective-permute-start(bf16[128,2048]{1,0:T(8,128)(2,1)S(1)} %get-tuple-element.125), channel_id=1, source_target_pairs={{0,4},{4,0},{8,12},{12,8},{1,5},{5,1},{9,13},{13,9},{2,6},{6,2},{1... | collective-permute-start | bytes 1572872 | tf_op jit(solution)/shard_map/ppermute | solution.py:22
  152.1 7.0 %collective-permute-start.27 = (bf16[64,2048]{1,0:T(8,128)(2,1)S(1)}, bf16[64,2048]{1,0:T(8,128)(2,1)}, u32[]{:S(2)}, u32[]{:S(2)}) collective-permute-start(bf16[64,2048]{1,0:T(8,128)(2,1)S(1)} %get-tuple-element.124), channel_id=1, source_target_pairs={{0,1},{1,0},{2,3},{3,2},{4,5},{5,4},{6,7},{7,6},{8,9},{9,8},{10,11... | collective-permute-start | bytes 786440 | tf_op jit(solution)/shard_map/ppermute | solution.py:22
  152.9 8.2 %collective-permute-start.29 = (bf16[64,2048]{1,0:T(8,128)(2,1)S(1)}, bf16[64,2048]{1,0:T(8,128)(2,1)}, u32[]{:S(2)}, u32[]{:S(2)}) collective-permute-start(bf16[64,2048]{1,0:T(8,128)(2,1)S(1)} %get-tuple-element.126), channel_id=1, source_target_pairs={{0,3},{1,2},{2,1},{3,0},{4,7},{5,6},{6,5},{7,4},{8,11},{9,10},{10,... | collective-permute-start | bytes 786440 | tf_op jit(solution)/shard_map/ppermute | solution.py:22
  154.9 12.6 %collective-permute-start.30 = (bf16[64,2048]{1,0:T(8,128)(2,1)S(1)}, bf16[64,2048]{1,0:T(8,128)(2,1)}, u32[]{:S(2)}, u32[]{:S(2)}) collective-permute-start(bf16[64,2048]{1,0:T(8,128)(2,1)S(1)} %get-tuple-element.127), channel_id=1, source_target_pairs={{0,2},{1,3},{2,0},{3,1},{4,6},{5,7},{6,4},{7,5},{8,10},{9,11},{10,... | collective-permute-start | bytes 786440 | tf_op jit(solution)/shard_map/ppermute | solution.py:22
  168.7 7.9 %collective-permute-start.32 = (bf16[32,2048]{1,0:T(8,128)(2,1)S(1)}, bf16[32,2048]{1,0:T(8,128)(2,1)S(1)}, u32[]{:S(2)}, u32[]{:S(2)}) collective-permute-start(bf16[32,2048]{1,0:T(8,128)(2,1)S(1)} %slice.44), channel_id=1, source_target_pairs={{0,4},{4,0},{8,12},{12,8},{1,5},{5,1},{9,13},{13,9},{2,6},{6,2},{1... | collective-permute-start | bytes 393224 | tf_op jit(solution)/shard_map/ppermute | solution.py:22
  169.6 7.1 %collective-permute-start.34 = (bf16[32,2048]{1,0:T(8,128)(2,1)S(1)}, bf16[32,2048]{1,0:T(8,128)(2,1)S(1)}, u32[]{:S(2)}, u32[]{:S(2)}) collective-permute-start(bf16[32,2048]{1,0:T(8,128)(2,1)S(1)} %get-tuple-element.146), channel_id=1, source_target_pairs={{0,2},{1,3},{2,0},{3,1},{4,6},{5,7},{6,4},{7,5},{8,10},{9,11},{10,... | collective-permute-start | bytes 393224 | tf_op jit(solution)/shard_map/ppermute | solution.py:22
  (29 other events, 245.1 us)
Sparse Core Ops, SparseCore 0:
  30.5 65.3 all-gather.2

commit v4 on v3

--- a/solution.py
+++ b/solution.py
@@ -31,16 +31,15 @@
     return lax.optimization_barrier(jnp.concatenate(pieces, axis=0))
 
 
-def gather_plane(one, two, two_more, also):
+def gather_plane(one, two, two_more):
     sent = [("col", 1, one), ("row", 1, two), ("col", 3, one), ("row", 3, two)]
-    sent += [("col", 2, one), ("row", 2, two_more)]
-    got = lax.optimization_barrier([swap(*x) for x in sent] + [also])
+    got = together(sent + [("col", 2, one), ("row", 2, two_more)])
     tall = two.shape[0]
-    more = [got[6], got[5][tall:]]
+    more = got[5][tall:]
     one = join([one, got[0], got[4], got[2]])
     two = join([two, got[1], got[5][:tall], got[3]])
-    got = together([x for k in (1, 3, 2) for x in (("row", k, one), ("col", k, two))])
-    return [one, got[0], got[4], got[2], two, got[1], got[5], got[3]], more
+    got = together([x for k in (2, 3, 1) for x in (("row", k, one), ("col", k, two))])
+    return [one, got[4], got[0], got[2], two, got[5], got[1], got[3]], more
 
 
 def gather_block(one, two):
@@ -495,9 +494,10 @@
         [two, jnp.concatenate([in_slice[0], in_slice[1]], axis=1), down_slice], axis=0
     )
 
-    pieces, more = gather_plane(one, two, two_more, out_far)
+    one, two, two_more, out_far = lax.optimization_barrier((one, two, two_more, out_far))
+    pieces, feed_far = gather_plane(one, two, two_more)
     fed = lax.all_gather(
-        jnp.concatenate(more, axis=0), "rep", axis=0, tiled=False
+        jnp.concatenate([out_far, feed_far], axis=0), "rep", axis=0, tiled=False
     )
     w_in = w_gate_up.reshape(width, 2 * units)
     pieces, w_in = lax.optimization_barrier((pieces, w_in))

time: 186 us -> 190 us (1.022)
  waiting for transfers between devices: 69.8 us -> 74.7 us
    ppermute x34, waiting for transfers between devices: 69.8 us -> 74.7 us  [swap(): return lax.ppermute(array, axis, [(i, i ^ k) for i in range(size)])]
    ppermute x34, starting transfers between devices: 41.3 us -> 37.6 us  [swap(): return lax.ppermute(array, axis, [(i, i ^ k) for i in range(size)])]
    all_to_all x1, starting transfers between devices: 15.2 us -> 17.3 us  [body(): moved = lax.all_to_all(sent, 'rep', split_axis=0, concat_axis=0, tiled=True)]
  transfers between devices with their start and end apart: 37 -> 37, of which waited for: 21 -> 19; matrix products, arithmetic and copies ran while one was open for 5% -> 6% of each run, Pallas kernels for 15% -> 15%
where the time goes in v4:
time: 190 us; the launch traced here: 189 us
  waiting for transfers between devices  74.7 us (39%)
  starting transfers between devices  55.5 us (29%)
  Pallas kernels  27.4 us (14%)
  between operations  14.4 us (8%)
  local copies, waits for them, and re-layouts  12.2 us (6%)
  other arithmetic  4.89 us (3%)
    ppermute x34, waiting for transfers between devices, swap(): return lax.ppermute(array, axis, [(i, i ^ k) for i in range(size)])  74.7 us
    ppermute x34, starting transfers between devices, swap(): return lax.ppermute(array, axis, [(i, i ^ k) for i in range(size)])  37.6 us
    all_to_all x1, starting transfers between devices, body(): moved = lax.all_to_all(sent, 'rep', split_axis=0, concat_axis=0, tiled=True)  17.3 us
    pallas_call x1, Pallas kernels, feed(): pl.pallas_call(feed_kernel, out_shape=[jax.ShapeDtypeStruct(piece.shape,...  9.45 us
    unnamed x35, local copies, waits for them, and re-layouts  9.42 us
    pallas_call x1, Pallas kernels, attend(): pl.pallas_call(attend_kernel, out_shape=[context] * 4 + [pltpu.HBM((repli...  7.11 us
    pallas_call x1, Pallas kernels, join_heads(): pl.pallas_call(joined_kernel, out_shape=jax.ShapeDtypeStruct(shape, jnp.f...  4.15 us
  transfers between devices with their start and end apart: 37, of which 19 were waited for; matrix products, arithmetic and copies ran while one was open for 6% of the time, Pallas kernels for 15%

profile of v4, /device:TPU:1, one launch (start us, length us, event | category | flops | bytes accessed | tf_op | source)
XLA Modules:
  0.0 189.2 jit_solution(3609897943821251744)
XLA Ops:
  12.3 3.8 %collective-permute-start.6 = (bf16[128,2048]{1,0:T(8,128)(2,1)S(1)}, bf16[128,2048]{1,0:T(8,128)(2,1)S(1)}, u32[]{:S(2)}, u32[]{:S(2)}) collective-permute-start(bf16[128,2048]{1,0:T(8,128)(2,1)S(1)} %pad_maximum_fusion), channel_id=1, source_target_pairs={{0,8},{4,12},{8,0},{12,4},{1,9},{5,13},{9,1},{13,5},{2,10},{6,14},... | collective-permute-start | bytes 1572872 | tf_op jit(solution)/shard_map/ppermute | solution.py:22
  16.9 2.7 %collective-permute-start.5 = (bf16[32,2048]{1,0:T(8,128)(2,1)S(1)}, bf16[32,2048]{1,0:T(8,128)(2,1)S(1)}, u32[]{:S(2)}, u32[]{:S(2)}) collective-permute-start(bf16[32,2048]{1,0:T(8,128)(2,1)S(1)} %get-tuple-element.78), channel_id=1, source_target_pairs={{0,2},{1,3},{2,0},{3,1},{4,6},{5,7},{6,4},{7,5},{8,10},{9,11},{10,... | collective-permute-start | bytes 393224 | tf_op jit(solution)/shard_map/ppermute | solution.py:22
  20.5 10.8 %collective-permute-done.4 = bf16[32,2048]{1,0:T(8,128)(2,1)S(1)} collective-permute-done((bf16[32,2048]{1,0:T(8,128)(2,1)S(1)}, bf16[32,2048]{1,0:T(8,128)(2,1)S(1)}, u32[]{:S(2)}, u32[]{:S(2)}) %collective-permute-start.4) | collective-permute-done | bytes 131104 | tf_op jit(solution)/shard_map/ppermute | solution.py:22
  32.6 3.3 %collective-permute-done.1 = bf16[32,2048]{1,0:T(8,128)(2,1)S(1)} collective-permute-done((bf16[32,2048]{1,0:T(8,128)(2,1)S(1)}, bf16[32,2048]{1,0:T(8,128)(2,1)S(1)}, u32[]{:S(2)}, u32[]{:S(2)}) %collective-permute-start.1) | collective-permute-done | bytes 131104 | tf_op jit(solution)/shard_map/ppermute | solution.py:22
  43.6 5.5 %collective-permute-done.12.refs_5_ = bf16[128,2048]{1,0:T(8,128)(2,1)S(1)} collective-permute-done((bf16[128,2048]{1,0:T(8,128)(2,1)S(1)}, bf16[128,2048]{1,0:T(8,128)(2,1)S(1)}, u32[]{:S(2)}, u32[]{:S(2)}) %collective-permute-start.12) | collective-permute-done | bytes 524320 | tf_op jit(solution)/shard_map/ppermute | solution.py:22
  50.0 5.6 %copy.19 = bf16[256,8,2,512]{3,1,2,0:T(8,128)(2,1)} copy(bf16[256,8,2,512]{3,2,1,0:T(2,128)(2,1)} %bitcast.22) | data formatting | bytes 8388608
  55.9 6.7 %collective-permute-done.8.refs_6_ = bf16[128,2048]{1,0:T(8,128)(2,1)} collective-permute-done((bf16[128,2048]{1,0:T(8,128)(2,1)S(1)}, bf16[128,2048]{1,0:T(8,128)(2,1)}, u32[]{:S(2)}, u32[]{:S(2)}) %collective-permute-start.8) | collective-permute-done | bytes 524320 | tf_op jit(solution)/shard_map/ppermute | solution.py:22
  62.7 3.4 %collective-permute-done.7.refs_2_ = bf16[128,2048]{1,0:T(8,128)(2,1)} collective-permute-done((bf16[128,2048]{1,0:T(8,128)(2,1)S(1)}, bf16[128,2048]{1,0:T(8,128)(2,1)}, u32[]{:S(2)}, u32[]{:S(2)}) %collective-permute-start.7) | collective-permute-done | bytes 524320 | tf_op jit(solution)/shard_map/ppermute | solution.py:22
  67.2 4.2 %join_heads.1.joined_ref = f32[1024,384]{1,0:T(8,128)S(1)} custom-call(bf16[128,2048]{1,0:T(8,128)(2,1)S(1)} %pad_maximum_fusion.1.refs_0_, bf16[128,2048]{1,0:T(8,128)(2,1)} %collective-permute-done.11.refs_1_, bf16[128,2048]{1,0:T(8,128)(2,1)} %collective-permute-done.7.refs_2_, bf16[128,2048]{1,0:T(8,128)(2,1)} %collective-permute-done.9.refs_3_, ...), custom_call_target="tpu_custom_call" | custom-call | flops 1610612736 | bytes 7340032 | tf_op jit(solution)/shard_map/join_heads/pallas_call | solution.py:132
  71.4 7.1 %attend.1 = (bf16[256,128]{1,0:T(8,128)(2,1)S(1)}, bf16[256,128]{1,0:T(8,128)(2,1)S(1)}, bf16[256,128]{1,0:T(8,128)(2,1)S(1)}, bf16[256,128]{1,0:T(8,128)(2,1)S(1)}, bf16[16,2,384,128]{3,2,1,0:T(8,128)(2,1)}) custom-call(s32[2]{0:T(128)S(1)} %pad_add_fusion.place_ref, s32[8]{0:T(128)S(1)} %get-tuple-element.149.length_ref, s32[8]{0:T(128)S(1)} %dynamic_slice.29.span_ref, ...), custom_call_target="tpu_custom_call" | custom-call | flops 201326592 | bytes 6291456 | tf_op jit(solution)/shard_map/attend/pallas_call | solution.py:396
  78.9 3.0 %collective-permute-start.15 = (bf16[256,128]{1,0:T(8,128)(2,1)S(1)}, bf16[256,128]{1,0:T(8,128)(2,1)S(1)}, u32[]{:S(2)}, u32[]{:S(2)}) collective-permute-start(bf16[256,128]{1,0:T(8,128)(2,1)S(1)} %get-tuple-element.104), channel_id=1, source_target_pairs={{0,8},{4,12},{8,0},{12,4},{1,9},{5,13},{9,1},{13,5},{2,10},{6,14},... | collective-permute-start | bytes 196616 | tf_op jit(solution)/shard_map/ppermute | solution.py:22
  82.1 2.2 %collective-permute-done.14.refs_3_ = bf16[256,128]{1,0:T(8,128)(2,1)S(1)} collective-permute-done((bf16[256,128]{1,0:T(8,128)(2,1)S(1)}, bf16[256,128]{1,0:T(8,128)(2,1)S(1)}, u32[]{:S(2)}, u32[]{:S(2)}) %collective-permute-start.14) | collective-permute-done | bytes 65568 | tf_op jit(solution)/shard_map/ppermute | solution.py:22
  84.3 17.3 %all-to-all-start = ((bf16[16,2,384,128]{3,2,1,0:T(8,128)(2,1)}), bf16[16,2,384,128]{3,2,1,0:T(8,128)(2,1)}, u32[]{:S(2)}, u32[]{:S(2)}) async-start(bf16[16,2,384,128]{3,2,1,0:T(8,128)(2,1)} %get-tuple-element.143), calls=%async_computation | async-start | bytes 6291456 | tf_op jit(solution)/shard_map/all_to_all | solution.py:525
  101.6 3.1 %project.1 = (bf16[64,2048]{1,0:T(8,128)(2,1)S(1)}, bf16[64,2048]{1,0:T(8,128)(2,1)S(1)}, bf16[64,2048]{1,0:T(8,128)(2,1)S(1)}, bf16[64,2048]{1,0:T(8,128)(2,1)S(1)}) custom-call(bf16[256,128]{1,0:T(8,128)(2,1)S(1)} %get-tuple-element.101.refs_0_, bf16[256,128]{1,0:T(8,128)(2,1)S(1)} %collective-permute-done.13.refs_1_, ...), custom_call_target="tpu_custom_call" | custom-call | flops 536870912 | bytes 4194304 | tf_op jit(solution)/shard_map/project/pallas_call | solution.py:180
  108.0 4.6 %collective-permute-done.16.a_ref = bf16[64,2048]{1,0:T(8,128)(2,1)S(1)} collective-permute-done((bf16[64,2048]{1,0:T(8,128)(2,1)S(1)}, bf16[64,2048]{1,0:T(8,128)(2,1)S(1)}, u32[]{:S(2)}, u32[]{:S(2)}) %collective-permute-start.16) | collective-permute-done | bytes 262176 | tf_op jit(solution)/shard_map/ppermute | solution.py:22
  112.7 5.4 %collective-permute-done.17.c_ref = bf16[64,2048]{1,0:T(8,128)(2,1)S(1)} collective-permute-done((bf16[64,2048]{1,0:T(8,128)(2,1)S(1)}, bf16[64,2048]{1,0:T(8,128)(2,1)S(1)}, u32[]{:S(2)}, u32[]{:S(2)}) %collective-permute-start.17) | collective-permute-done | bytes 262176 | tf_op jit(solution)/shard_map/ppermute | solution.py:22
  124.8 2.3 %collective-permute-done.22 = bf16[32,2048]{1,0:T(8,128)(2,1)S(1)} collective-permute-done((bf16[32,2048]{1,0:T(8,128)(2,1)S(1)}, bf16[32,2048]{1,0:T(8,128)(2,1)S(1)}, u32[]{:S(2)}, u32[]{:S(2)}) %collective-permute-start.22) | collective-permute-done | bytes 131104 | tf_op jit(solution)/shard_map/ppermute | solution.py:22
  127.0 3.1 %collective-permute-done.21 = bf16[32,2048]{1,0:T(8,128)(2,1)S(1)} collective-permute-done((bf16[32,2048]{1,0:T(8,128)(2,1)S(1)}, bf16[32,2048]{1,0:T(8,128)(2,1)S(1)}, u32[]{:S(2)}, u32[]{:S(2)}) %collective-permute-start.21) | collective-permute-done | bytes 131104 | tf_op jit(solution)/shard_map/ppermute | solution.py:22
  133.8 5.0 %collective-permute-done.26.refs_4_ = bf16[64,2048]{1,0:T(8,128)(2,1)S(1)} collective-permute-done((bf16[64,2048]{1,0:T(8,128)(2,1)S(1)}, bf16[64,2048]{1,0:T(8,128)(2,1)S(1)}, u32[]{:S(2)}, u32[]{:S(2)}) %collective-permute-start.26) | collective-permute-done | bytes 262176 | tf_op jit(solution)/shard_map/ppermute | solution.py:22
  138.8 7.7 %collective-permute-done.25.refs_5_ = bf16[64,2048]{1,0:T(8,128)(2,1)S(1)} collective-permute-done((bf16[64,2048]{1,0:T(8,128)(2,1)S(1)}, bf16[64,2048]{1,0:T(8,128)(2,1)S(1)}, u32[]{:S(2)}, u32[]{:S(2)}) %collective-permute-start.25) | collective-permute-done | bytes 262176 | tf_op jit(solution)/shard_map/ppermute | solution.py:22
  146.6 9.5 %feed.1 = (bf16[128,2048]{1,0:T(8,128)(2,1)S(1)}, bf16[128,2048]{1,0:T(8,128)(2,1)S(1)}, bf16[64,2048]{1,0:T(8,128)(2,1)S(1)}, bf16[64,2048]{1,0:T(8,128)(2,1)S(...) custom-call(bf16[128,2048]{1,0:T(8,128)(2,1)S(1)} %pad_maximum_fusion.4.refs_0_, ...), custom_call_target="tpu_custom_call" | custom-call | flops 6442450944 | bytes 16777216 | tf_op jit(solution)/shard_map/feed/pallas_call | solution.py:269
  160.8 3.4 %collective-permute-done.27 = bf16[64,2048]{1,0:T(8,128)(2,1)} collective-permute-done((bf16[64,2048]{1,0:T(8,128)(2,1)S(1)}, bf16[64,2048]{1,0:T(8,128)(2,1)}, u32[]{:S(2)}, u32[]{:S(2)}) %collective-permute-start.27) | collective-permute-done | bytes 262176 | tf_op jit(solution)/shard_map/ppermute | solution.py:22
  165.2 6.4 %collective-permute-done.30 = bf16[64,2048]{1,0:T(8,128)(2,1)} collective-permute-done((bf16[64,2048]{1,0:T(8,128)(2,1)S(1)}, bf16[64,2048]{1,0:T(8,128)(2,1)}, u32[]{:S(2)}, u32[]{:S(2)}) %collective-permute-start.30) | collective-permute-done | bytes 262176 | tf_op jit(solution)/shard_map/ppermute | solution.py:22
  177.9 3.0 %pick.1 = bf16[8,2,384,128]{3,2,1,0:T(8,128)(2,1)} custom-call(s32[8]{0:T(128)} %select_reduce_fusion.source_ref, bf16[16,2,384,128]{3,2,1,0:T(8,128)(2,1)} %all-to-all-done.moved_ref), custom_call_target="tpu_custom_call" | custom-call | bytes 3145728 | tf_op jit(solution)/shard_map/pick/pallas_call | solution.py:447
  (120 shorter events, 45.7 us)
Async XLA Ops:
  7.2 94.4 %all-gather.3.cloned.1.call-start = ((), (), s32[]{:S(2)}) async-start(), calls=%async_computation.1 | async-start | bytes 8912896 | tf_op jit(solution)/shard_map/all_gather | solution.py:499
  12.3 23.6 %collective-permute-start.6 = (bf16[128,2048]{1,0:T(8,128)(2,1)S(1)}, bf16[128,2048]{1,0:T(8,128)(2,1)S(1)}, u32[]{:S(2)}, u32[]{:S(2)}) collective-permute-start(bf16[128,2048]{1,0:T(8,128)(2,1)S(1)} %pad_maximum_fusion), channel_id=1, source_target_pairs={{0,8},{4,12},{8,0},{12,4},{1,9},{5,13},{9,1},{13,5},{2,10},{6,14},... | collective-permute-start | bytes 1572872 | tf_op jit(solution)/shard_map/ppermute | solution.py:22
  16.1 15.2 %collective-permute-start.4 = (bf16[32,2048]{1,0:T(8,128)(2,1)S(1)}, bf16[32,2048]{1,0:T(8,128)(2,1)S(1)}, u32[]{:S(2)}, u32[]{:S(2)}) collective-permute-start(bf16[32,2048]{1,0:T(8,128)(2,1)S(1)} %get-tuple-element.79), channel_id=1, source_target_pairs={{0,12},{4,8},{8,4},{12,0},{1,13},{5,9},{9,5},{13,1},{2,14},{6,10},... | collective-permute-start | bytes 393224 | tf_op jit(solution)/shard_map/ppermute | solution.py:22
  16.9 15.7 %collective-permute-start.2 = (bf16[32,2048]{1,0:T(8,128)(2,1)S(1)}, bf16[32,2048]{1,0:T(8,128)(2,1)S(1)}, u32[]{:S(2)}, u32[]{:S(2)}) collective-permute-start(bf16[32,2048]{1,0:T(8,128)(2,1)S(1)} %get-tuple-element.79), channel_id=1, source_target_pairs={{0,4},{4,0},{8,12},{12,8},{1,5},{5,1},{9,13},{13,9},{2,6},{6,2},{1... | collective-permute-start | bytes 393224 | tf_op jit(solution)/shard_map/ppermute | solution.py:22
  16.9 15.7 %collective-permute-start.5 = (bf16[32,2048]{1,0:T(8,128)(2,1)S(1)}, bf16[32,2048]{1,0:T(8,128)(2,1)S(1)}, u32[]{:S(2)}, u32[]{:S(2)}) collective-permute-start(bf16[32,2048]{1,0:T(8,128)(2,1)S(1)} %get-tuple-element.78), channel_id=1, source_target_pairs={{0,2},{1,3},{2,0},{3,1},{4,6},{5,7},{6,4},{7,5},{8,10},{9,11},{10,... | collective-permute-start | bytes 393224 | tf_op jit(solution)/shard_map/ppermute | solution.py:22
  19.7 12.9 %collective-permute-start.3 = (bf16[32,2048]{1,0:T(8,128)(2,1)S(1)}, bf16[32,2048]{1,0:T(8,128)(2,1)S(1)}, u32[]{:S(2)}, u32[]{:S(2)}) collective-permute-start(bf16[32,2048]{1,0:T(8,128)(2,1)S(1)} %get-tuple-element.78), channel_id=1, source_target_pairs={{0,3},{1,2},{2,1},{3,0},{4,7},{5,6},{6,5},{7,4},{8,11},{9,10},{10,... | collective-permute-start | bytes 393224 | tf_op jit(solution)/shard_map/ppermute | solution.py:22
  36.9 12.3 %collective-permute-start.12 = (bf16[128,2048]{1,0:T(8,128)(2,1)S(1)}, bf16[128,2048]{1,0:T(8,128)(2,1)S(1)}, u32[]{:S(2)}, u32[]{:S(2)}) collective-permute-start(bf16[128,2048]{1,0:T(8,128)(2,1)S(1)} %pad_maximum_fusion.2.refs_4_), channel_id=1, source_target_pairs={{0,1},{1,0},{2,3},{3,2},{4,5},{5,4},{6,7},{7,6},{8,9},{9,8},{10,11... | collective-permute-start | bytes 1572872 | tf_op jit(solution)/shard_map/ppermute | solution.py:22
  38.2 17.7 %collective-permute-start.10 = (bf16[128,2048]{1,0:T(8,128)(2,1)S(1)}, bf16[128,2048]{1,0:T(8,128)(2,1)}, u32[]{:S(2)}, u32[]{:S(2)}) collective-permute-start(bf16[128,2048]{1,0:T(8,128)(2,1)S(1)} %pad_maximum_fusion.2.refs_4_), channel_id=1, source_target_pairs={{0,3},{1,2},{2,1},{3,0},{4,7},{5,6},{6,5},{7,4},{8,11},{9,10},{10,... | collective-permute-start | bytes 1572872 | tf_op jit(solution)/shard_map/ppermute | solution.py:22
  40.0 22.6 %collective-permute-start.8 = (bf16[128,2048]{1,0:T(8,128)(2,1)S(1)}, bf16[128,2048]{1,0:T(8,128)(2,1)}, u32[]{:S(2)}, u32[]{:S(2)}) collective-permute-start(bf16[128,2048]{1,0:T(8,128)(2,1)S(1)} %pad_maximum_fusion.2.refs_4_), channel_id=1, source_target_pairs={{0,2},{1,3},{2,0},{3,1},{4,6},{5,7},{6,4},{7,5},{8,10},{9,11},{10,... | collective-permute-start | bytes 1572872 | tf_op jit(solution)/shard_map/ppermute | solution.py:22
  40.7 21.9 %collective-permute-start.11 = (bf16[128,2048]{1,0:T(8,128)(2,1)S(1)}, bf16[128,2048]{1,0:T(8,128)(2,1)}, u32[]{:S(2)}, u32[]{:S(2)}) collective-permute-start(bf16[128,2048]{1,0:T(8,128)(2,1)S(1)} %pad_maximum_fusion.1.refs_0_), channel_id=1, source_target_pairs={{0,4},{4,0},{8,12},{12,8},{1,5},{5,1},{9,13},{13,9},{2,6},{6,2},{1... | collective-permute-start | bytes 1572872 | tf_op jit(solution)/shard_map/ppermute | solution.py:22
  42.1 20.6 %collective-permute-start.9 = (bf16[128,2048]{1,0:T(8,128)(2,1)S(1)}, bf16[128,2048]{1,0:T(8,128)(2,1)}, u32[]{:S(2)}, u32[]{:S(2)}) collective-permute-start(bf16[128,2048]{1,0:T(8,128)(2,1)S(1)} %pad_maximum_fusion.1.refs_0_), channel_id=1, source_target_pairs={{0,12},{4,8},{8,4},{12,0},{1,13},{5,9},{9,5},{13,1},{2,14},{6,10},... | collective-permute-start | bytes 1572872 | tf_op jit(solution)/shard_map/ppermute | solution.py:22
  49.9 16.2 %collective-permute-start.7 = (bf16[128,2048]{1,0:T(8,128)(2,1)S(1)}, bf16[128,2048]{1,0:T(8,128)(2,1)}, u32[]{:S(2)}, u32[]{:S(2)}) collective-permute-start(bf16[128,2048]{1,0:T(8,128)(2,1)S(1)} %pad_maximum_fusion.1.refs_0_), channel_id=1, source_target_pairs={{0,8},{4,12},{8,0},{12,4},{1,9},{5,13},{9,1},{13,5},{2,10},{6,14},... | collective-permute-start | bytes 1572872 | tf_op jit(solution)/shard_map/ppermute | solution.py:22
  84.3 93.6 %all-to-all-start = ((bf16[16,2,384,128]{3,2,1,0:T(8,128)(2,1)}), bf16[16,2,384,128]{3,2,1,0:T(8,128)(2,1)}, u32[]{:S(2)}, u32[]{:S(2)}) async-start(bf16[16,2,384,128]{3,2,1,0:T(8,128)(2,1)} %get-tuple-element.143), calls=%async_computation | async-start | bytes 6291456 | tf_op jit(solution)/shard_map/all_to_all | solution.py:525
  104.7 7.9 %collective-permute-start.16 = (bf16[64,2048]{1,0:T(8,128)(2,1)S(1)}, bf16[64,2048]{1,0:T(8,128)(2,1)S(1)}, u32[]{:S(2)}, u32[]{:S(2)}) collective-permute-start(bf16[64,2048]{1,0:T(8,128)(2,1)S(1)} %get-tuple-element.111), channel_id=1, source_target_pairs={{0,1},{1,0},{2,3},{3,2},{4,5},{5,4},{6,7},{7,6},{8,9},{9,8},{10,11... | collective-permute-start | bytes 786440 | tf_op jit(solution)/shard_map/ppermute | solution.py:22
  105.5 12.5 %collective-permute-start.17 = (bf16[64,2048]{1,0:T(8,128)(2,1)S(1)}, bf16[64,2048]{1,0:T(8,128)(2,1)S(1)}, u32[]{:S(2)}, u32[]{:S(2)}) collective-permute-start(bf16[64,2048]{1,0:T(8,128)(2,1)S(1)} %get-tuple-element.112), channel_id=1, source_target_pairs={{0,3},{1,2},{2,1},{3,0},{4,7},{5,6},{6,5},{7,4},{8,11},{9,10},{10,... | collective-permute-start | bytes 786440 | tf_op jit(solution)/shard_map/ppermute | solution.py:22
  107.4 12.7 %collective-permute-start.18 = (bf16[64,2048]{1,0:T(8,128)(2,1)S(1)}, bf16[64,2048]{1,0:T(8,128)(2,1)S(1)}, u32[]{:S(2)}, u32[]{:S(2)}) collective-permute-start(bf16[64,2048]{1,0:T(8,128)(2,1)S(1)} %get-tuple-element.113), channel_id=1, source_target_pairs={{0,2},{1,3},{2,0},{3,1},{4,6},{5,7},{6,4},{7,5},{8,10},{9,11},{10,... | collective-permute-start | bytes 786440 | tf_op jit(solution)/shard_map/ppermute | solution.py:22
  121.8 8.4 %collective-permute-start.21 = (bf16[32,2048]{1,0:T(8,128)(2,1)S(1)}, bf16[32,2048]{1,0:T(8,128)(2,1)S(1)}, u32[]{:S(2)}, u32[]{:S(2)}) collective-permute-start(bf16[32,2048]{1,0:T(8,128)(2,1)S(1)} %get-tuple-element.118), channel_id=1, source_target_pairs={{0,3},{1,2},{2,1},{3,0},{4,7},{5,6},{6,5},{7,4},{8,11},{9,10},{10,... | collective-permute-start | bytes 393224 | tf_op jit(solution)/shard_map/ppermute | solution.py:22
  130.2 16.3 %collective-permute-start.24 = (bf16[128,2048]{1,0:T(8,128)(2,1)S(1)}, bf16[128,2048]{1,0:T(8,128)(2,1)S(1)}, u32[]{:S(2)}, u32[]{:S(2)}) collective-permute-start(bf16[128,2048]{1,0:T(8,128)(2,1)S(1)} %pad_maximum_fusion.4.refs_0_), channel_id=1, source_target_pairs={{0,4},{4,0},{8,12},{12,8},{1,5},{5,1},{9,13},{13,9},{2,6},{6,2},{1... | collective-permute-start | bytes 1572872 | tf_op jit(solution)/shard_map/ppermute | solution.py:22
  131.5 15.1 %collective-permute-start.25 = (bf16[64,2048]{1,0:T(8,128)(2,1)S(1)}, bf16[64,2048]{1,0:T(8,128)(2,1)S(1)}, u32[]{:S(2)}, u32[]{:S(2)}) collective-permute-start(bf16[64,2048]{1,0:T(8,128)(2,1)S(1)} %pad_maximum_fusion.5.refs_2_), channel_id=1, source_target_pairs={{0,3},{1,2},{2,1},{3,0},{4,7},{5,6},{6,5},{7,4},{8,11},{9,10},{10,... | collective-permute-start | bytes 786440 | tf_op jit(solution)/shard_map/ppermute | solution.py:22
  133.7 12.9 %collective-permute-start.23 = (bf16[64,2048]{1,0:T(8,128)(2,1)S(1)}, bf16[64,2048]{1,0:T(8,128)(2,1)S(1)}, u32[]{:S(2)}, u32[]{:S(2)}) collective-permute-start(bf16[64,2048]{1,0:T(8,128)(2,1)S(1)} %pad_maximum_fusion.5.refs_2_), channel_id=1, source_target_pairs={{0,1},{1,0},{2,3},{3,2},{4,5},{5,4},{6,7},{7,6},{8,9},{9,8},{10,11... | collective-permute-start | bytes 786440 | tf_op jit(solution)/shard_map/ppermute | solution.py:22
  156.0 15.6 %collective-permute-start.28 = (bf16[128,2048]{1,0:T(8,128)(2,1)S(1)}, bf16[128,2048]{1,0:T(8,128)(2,1)S(1)}, u32[]{:S(2)}, u32[]{:S(2)}) collective-permute-start(bf16[128,2048]{1,0:T(8,128)(2,1)S(1)} %get-tuple-element.131), channel_id=1, source_target_pairs={{0,4},{4,0},{8,12},{12,8},{1,5},{5,1},{9,13},{13,9},{2,6},{6,2},{1... | collective-permute-start | bytes 1572872 | tf_op jit(solution)/shard_map/ppermute | solution.py:22
  157.1 8.2 %collective-permute-start.29 = (bf16[64,2048]{1,0:T(8,128)(2,1)S(1)}, bf16[64,2048]{1,0:T(8,128)(2,1)}, u32[]{:S(2)}, u32[]{:S(2)}) collective-permute-start(bf16[64,2048]{1,0:T(8,128)(2,1)S(1)} %get-tuple-element.132), channel_id=1, source_target_pairs={{0,3},{1,2},{2,1},{3,0},{4,7},{5,6},{6,5},{7,4},{8,11},{9,10},{10,... | collective-permute-start | bytes 786440 | tf_op jit(solution)/shard_map/ppermute | solution.py:22
  159.0 12.6 %collective-permute-start.30 = (bf16[64,2048]{1,0:T(8,128)(2,1)S(1)}, bf16[64,2048]{1,0:T(8,128)(2,1)}, u32[]{:S(2)}, u32[]{:S(2)}) collective-permute-start(bf16[64,2048]{1,0:T(8,128)(2,1)S(1)} %get-tuple-element.133), channel_id=1, source_target_pairs={{0,2},{1,3},{2,0},{3,1},{4,6},{5,7},{6,4},{7,5},{8,10},{9,11},{10,... | collective-permute-start | bytes 786440 | tf_op jit(solution)/shard_map/ppermute | solution.py:22
  172.9 8.0 %collective-permute-start.32 = (bf16[32,2048]{1,0:T(8,128)(2,1)S(1)}, bf16[32,2048]{1,0:T(8,128)(2,1)S(1)}, u32[]{:S(2)}, u32[]{:S(2)}) collective-permute-start(bf16[32,2048]{1,0:T(8,128)(2,1)S(1)} %slice.44), channel_id=1, source_target_pairs={{0,4},{4,0},{8,12},{12,8},{1,5},{5,1},{9,13},{13,9},{2,6},{6,2},{1... | collective-permute-start | bytes 393224 | tf_op jit(solution)/shard_map/ppermute | solution.py:22
  (29 other events, 243.7 us)
Sparse Core Ops, SparseCore 0:
  36.9 63.4 all-gather.2
